TPU v7x, 128 devices: a whole 4x4x4 slice. The times are simulated.
128 devices in a mesh: grid: 16 (over z_lo, y, core), sta: 8 (over z_hi, x).
Axes of the slice: x: 4, y: 4, z: 4 (z_hi: 2, z_lo: 2; z = z_hi * 2 + z_lo), core: 2. Of those that a mesh axis runs over, the one named last changes fastest.
Arguments:
- spectra: bfloat16 [64, 2, 6144], P(None, None, 'sta'), may hold values from -6 to 6
- lag_samples: int32 [16, 6144], P('grid', 'sta'), may hold values from 0 to 5999
- slowness: bfloat16 [16, 3, 6144], P('grid', None, 'sta'), may hold values from -3 to 3
- spread_taps: float32 [3, 17], replicated, may hold values from 0.02 to 0.2
Outputs:
- stacked: float32 [16, 32, 8, 128], P('grid')
- deblurred: float32 [16, 32, 8, 128], P('grid')
All inputs are finite; a program needn't handle non-finite values.
Results may differ from a plain program's by a relative error of at most 0.0015.
Values may be sent and summed in bfloat16 or wider, within the bound.
A program may use at most 64 MiB of HBM per device.

v0:
```python
import math

import jax
import jax.numpy as jnp
from jax import lax
from jax.sharding import PartitionSpec as P

STATIONS = 6144
FREQS = 64
F0 = 600
NT = 6000
TAPS = 17
HALF = 8
ITERS = 4
CX = 32
CY = 8
CZ = 128


TWO_PI = 2.0 * math.pi
BACKGROUND = 0.05


def with_halo(array, sides, width):
    for axis, dim in sides:
        size, length = (lax.axis_size(axis), array.shape[dim])
        up = [(i, (i + 1) % size) for i in range(size - 1)]
        down = [(j, i) for i, j in up]
        last = lax.slice_in_dim(array, length - width, length, axis=dim)
        leading = lax.slice_in_dim(array, 0, width, axis=dim)
        before = lax.ppermute(last, axis, up)
        after = lax.ppermute(leading, axis, down)
        array = jnp.concatenate([before, array, after], axis=dim)
    return array


def align_rows(spectra, lag_row):
    bins = F0 + jnp.arange(FREQS, dtype=jnp.int32)
    cycles = bins[:, None] * lag_row[None, :] % NT
    turned = cycles.astype(jnp.float32) * (TWO_PI / NT)
    cosine = jnp.cos(turned)
    sine = jnp.sin(turned)
    real_in = spectra[:, 0, :].astype(jnp.float32)
    imag_in = spectra[:, 1, :].astype(jnp.float32)
    real_out = real_in * cosine + imag_in * sine
    imag_out = imag_in * cosine - real_in * sine
    return jnp.stack([real_out, imag_out], axis=1).astype(jnp.bfloat16)


def beam_freq(freq, aligned_row, slow_rows):
    omega = (F0 + freq).astype(jnp.float32) * (TWO_PI / NT)
    slow = slow_rows.astype(jnp.float32)
    x_coord = jnp.arange(CX, dtype=jnp.float32) - (CX - 1) / 2.0
    y_coord = jnp.arange(CY, dtype=jnp.float32) - (CY - 1) / 2.0
    z_coord = jnp.arange(CZ, dtype=jnp.float32) - (CZ - 1) / 2.0
    phase_x = (omega * slow[0])[None, :] * x_coord[:, None]
    phase_y = (omega * slow[1])[None, :] * y_coord[:, None]
    phase = phase_x[:, None, :] + phase_y[None, :, :]
    cosine = jnp.cos(phase)
    sine = jnp.sin(phase)
    real_in = aligned_row[0].astype(jnp.float32)[None, None, :]
    imag_in = aligned_row[1].astype(jnp.float32)[None, None, :]
    front_real = (real_in * cosine + imag_in * sine).astype(jnp.bfloat16).reshape(CX * CY, -1)
    front_imag = (imag_in * cosine - real_in * sine).astype(jnp.bfloat16).reshape(CX * CY, -1)
    left_side = jnp.concatenate([front_real, front_imag], axis=1)
    phase_z = (omega * slow[2])[:, None] * z_coord[None, :]
    depth_real = jnp.cos(phase_z).astype(jnp.bfloat16)
    depth_imag = jnp.sin(phase_z).astype(jnp.bfloat16)
    upper_rows = jnp.concatenate([depth_real, -depth_imag], axis=1)
    lower_rows = jnp.concatenate([depth_imag, depth_real], axis=1)
    right_side = jnp.concatenate([upper_rows, lower_rows], axis=0)
    return jnp.dot(left_side, right_side, preferred_element_type=jnp.float32)


def freq_beams(freq_ids, aligned_rows, slow_rows):
    return lax.map(lambda pair: beam_freq(pair[0], pair[1], slow_rows), (freq_ids, aligned_rows))


def band_matrix(taps, length):
    rows = jnp.arange(length, dtype=jnp.int32)[:, None]
    columns = jnp.arange(length + 2 * HALF, dtype=jnp.int32)[None, :]
    offset = columns - rows
    picks = jnp.arange(TAPS, dtype=jnp.int32)[:, None, None]
    return jnp.sum(jnp.where(offset[None] == picks, taps[:, None, None], 0.0), axis=0)


def blur(volume, bands):
    band_x, square_y, square_z = bands
    padded = with_halo(volume.astype(jnp.bfloat16), (("grid", 0),), HALF).astype(volume.dtype)
    along_x = jnp.einsum("ip,pyz->iyz", band_x, padded, precision=lax.Precision.HIGHEST)
    along_y = jnp.einsum("jq,xqz->xjz", square_y, along_x, precision=lax.Precision.HIGHEST)
    return jnp.einsum("xyw,kw->xyk", along_y, square_z, precision=lax.Precision.HIGHEST)


def per_device(spectra, lag_samples, slowness, spread_taps):
    groups = lax.axis_size("sta")
    own_count = FREQS // groups
    first_bin = lax.axis_index("sta") * own_count
    aligned = align_rows(spectra, lag_samples[0])
    own_ids = first_bin + jnp.arange(own_count, dtype=jnp.int32)
    rows = lax.dynamic_slice_in_dim(
        lax.all_gather(aligned, "sta", axis=2, tiled=True), first_bin, own_count, 0
    )
    beams = freq_beams(own_ids, rows, lax.all_gather(slowness, "sta", axis=2, tiled=True)[0])
    squares = jnp.sum(beams * beams, axis=0)
    local_power = squares[:, :CZ] + squares[:, CZ:]
    summed = lax.psum(local_power, "sta")
    stacked = (summed / (FREQS * STATIONS) + BACKGROUND).reshape(CX, CY, CZ)
    square_y = band_matrix(spread_taps[1], CY)[:, HALF : HALF + CY]
    square_z = band_matrix(spread_taps[2], CZ)[:, HALF : HALF + CZ]
    bands = (band_matrix(spread_taps[0], CX), square_y, square_z)
    estimate = stacked
    for sweep in range(ITERS):
        blurred = blur(estimate, bands)
        estimate = estimate * blur(stacked / blurred, bands)
    return (stacked[None], estimate[None])


def solution(mesh):
    placed = (P(None, None, "sta"), P("grid", "sta"), P("grid", None, "sta"), P())
    return jax.shard_map(
        per_device,
        mesh=mesh,
        in_specs=placed,
        out_specs=(P("grid", None, None, None), P("grid", None, None, None)),
        check_vma=False,
    )
```

profile of v0, /device:TPU:1, one launch (start us, length us, event | category | flops | bytes accessed | tf_op | source)
XLA Modules:
  0.0 642.4 jit_solution(14156776172203744260)
XLA Ops:
  7.2 1.4 fusion.106
  11.0 30.3 %all_gather.7 = bf16[1,3,6144]{2,1,0:T(4,128)(2,1)S(1)} all-gather(bf16[1,3,768]{2,1,0:T(4,128)(2,1)} %param.8), channel_id=1, replica_groups=mesh['grid'=16,'sta'=8] {'sta'}, dimensions={2}, use_global_device_ids=true | all-gather | bytes 41472 | tf_op jit(solution)/shard_map/all_gather | solution.py:104
  42.3 22.0 %all-gather.2.cloned.1.call-done = bf16[64,2,6144]{2,0,1:T(8,128)(2,1)} async-done(((bf16[64,2,768]{2,0,1:T(8,128)(2,1)}), bf16[64,2,6144]{2,0,1:T(8,128)(2,1)}) %all-gather.2.cloned.1.call-update) | async-done | bytes 1572880 | tf_op jit(solution)/shard_map/all_gather | solution.py:102
  65.5 408.7 %while.12 = (s32[]{:T(128)}, f32[8,256,256]{2,1,0:T(8,128)S(1)}, bf16[8,2,6144]{2,1,0:T(2,128)(2,1)S(1)}, s32[8]{0:T(128)S(1)}, bf16[3,6144]{1,0:T(4,128)(2,1)S(...) while((s32[]{:T(128)}, f32[8,256,256]{2,1,0:T(8,128)S(1)}, ...), condition=%wide.region_1.2_spmd, body=%wide.region_0.1_spmd.sunk | while | flops 1669103744 | bytes 24729580 | solution.py:76
  67.1 23.7 %fusion.136 = (bf16[256,6144]{1,0:T(8,128)(2,1)S(1)}, bf16[256,6144]{1,0:T(8,128)(2,1)S(1)}) fusion(f32[6144]{0:T(1024)S(1)} %bitcast.160, f32[8,6144]{1,0:T(8,128)S(1)} %broadcast_multiply_fusion.4, f32[32,6144]{1,0:T(8,128)S(1)} %broadcast_multiply_fusion.5, f32[6144]{0:T(1024)S(1)} %bitcast.159), kind=kLoop, calls=%fused_computation.6.clone.1 | loop fusion | flops 14155776 | bytes 7323648 | tf_op jit(solution)/shard_map/while/body/eval_jaxpr/convert_element_type | solution.py:63
  90.9 12.3 %fusion.134 = (bf16[6144,128]{1,0:T(8,128)(2,1)S(1)}, bf16[6144,128]{1,0:T(8,128)(2,1)S(1)}) fusion(f32[128]{0:T(128)S(1)} %iota_add_fusion.8, f32[6144]{0:T(1024)S(1)} %bitcast.157), kind=kLoop, calls=%fused_computation.26.clone.2 | loop fusion | flops 2359296 | bytes 3170816 | tf_op jit(solution)/shard_map/while/body/eval_jaxpr/convert_element_type | solution.py:68
  103.2 11.5 %fusion.135 = bf16[6144,128]{1,0:T(8,128)(2,1)S(1)} fusion(f32[128]{0:T(128)S(1)} %iota_add_fusion.8, f32[6144]{0:T(1024)S(1)} %bitcast.158), kind=kLoop, calls=%fused_computation.30.clone.1 | loop fusion | flops 3932160 | bytes 1597952 | tf_op jit(solution)/shard_map/while/body/eval_jaxpr/neg | solution.py:69
  114.8 1.8 fusion.137
  118.2 23.7 %fusion.136 = (bf16[256,6144]{1,0:T(8,128)(2,1)S(1)}, bf16[256,6144]{1,0:T(8,128)(2,1)S(1)}) fusion(f32[6144]{0:T(1024)S(1)} %bitcast.160, f32[8,6144]{1,0:T(8,128)S(1)} %broadcast_multiply_fusion.4, f32[32,6144]{1,0:T(8,128)S(1)} %broadcast_multiply_fusion.5, f32[6144]{0:T(1024)S(1)} %bitcast.159), kind=kLoop, calls=%fused_computation.6.clone.1 | loop fusion | flops 14155776 | bytes 7323648 | tf_op jit(solution)/shard_map/while/body/eval_jaxpr/convert_element_type | solution.py:63
  142.0 12.3 %fusion.134 = (bf16[6144,128]{1,0:T(8,128)(2,1)S(1)}, bf16[6144,128]{1,0:T(8,128)(2,1)S(1)}) fusion(f32[128]{0:T(128)S(1)} %iota_add_fusion.8, f32[6144]{0:T(1024)S(1)} %bitcast.157), kind=kLoop, calls=%fused_computation.26.clone.2 | loop fusion | flops 2359296 | bytes 3170816 | tf_op jit(solution)/shard_map/while/body/eval_jaxpr/convert_element_type | solution.py:68
  154.3 11.5 %fusion.135 = bf16[6144,128]{1,0:T(8,128)(2,1)S(1)} fusion(f32[128]{0:T(128)S(1)} %iota_add_fusion.8, f32[6144]{0:T(1024)S(1)} %bitcast.158), kind=kLoop, calls=%fused_computation.30.clone.1 | loop fusion | flops 3932160 | bytes 1597952 | tf_op jit(solution)/shard_map/while/body/eval_jaxpr/neg | solution.py:69
  165.8 1.8 fusion.137
  169.3 23.7 %fusion.136 = (bf16[256,6144]{1,0:T(8,128)(2,1)S(1)}, bf16[256,6144]{1,0:T(8,128)(2,1)S(1)}) fusion(f32[6144]{0:T(1024)S(1)} %bitcast.160, f32[8,6144]{1,0:T(8,128)S(1)} %broadcast_multiply_fusion.4, f32[32,6144]{1,0:T(8,128)S(1)} %broadcast_multiply_fusion.5, f32[6144]{0:T(1024)S(1)} %bitcast.159), kind=kLoop, calls=%fused_computation.6.clone.1 | loop fusion | flops 14155776 | bytes 7323648 | tf_op jit(solution)/shard_map/while/body/eval_jaxpr/convert_element_type | solution.py:63
  193.1 12.3 %fusion.134 = (bf16[6144,128]{1,0:T(8,128)(2,1)S(1)}, bf16[6144,128]{1,0:T(8,128)(2,1)S(1)}) fusion(f32[128]{0:T(128)S(1)} %iota_add_fusion.8, f32[6144]{0:T(1024)S(1)} %bitcast.157), kind=kLoop, calls=%fused_computation.26.clone.2 | loop fusion | flops 2359296 | bytes 3170816 | tf_op jit(solution)/shard_map/while/body/eval_jaxpr/convert_element_type | solution.py:68
  205.4 11.5 %fusion.135 = bf16[6144,128]{1,0:T(8,128)(2,1)S(1)} fusion(f32[128]{0:T(128)S(1)} %iota_add_fusion.8, f32[6144]{0:T(1024)S(1)} %bitcast.158), kind=kLoop, calls=%fused_computation.30.clone.1 | loop fusion | flops 3932160 | bytes 1597952 | tf_op jit(solution)/shard_map/while/body/eval_jaxpr/neg | solution.py:69
  216.9 1.8 fusion.137
  220.4 23.7 %fusion.136 = (bf16[256,6144]{1,0:T(8,128)(2,1)S(1)}, bf16[256,6144]{1,0:T(8,128)(2,1)S(1)}) fusion(f32[6144]{0:T(1024)S(1)} %bitcast.160, f32[8,6144]{1,0:T(8,128)S(1)} %broadcast_multiply_fusion.4, f32[32,6144]{1,0:T(8,128)S(1)} %broadcast_multiply_fusion.5, f32[6144]{0:T(1024)S(1)} %bitcast.159), kind=kLoop, calls=%fused_computation.6.clone.1 | loop fusion | flops 14155776 | bytes 7323648 | tf_op jit(solution)/shard_map/while/body/eval_jaxpr/convert_element_type | solution.py:63
  244.1 12.3 %fusion.134 = (bf16[6144,128]{1,0:T(8,128)(2,1)S(1)}, bf16[6144,128]{1,0:T(8,128)(2,1)S(1)}) fusion(f32[128]{0:T(128)S(1)} %iota_add_fusion.8, f32[6144]{0:T(1024)S(1)} %bitcast.157), kind=kLoop, calls=%fused_computation.26.clone.2 | loop fusion | flops 2359296 | bytes 3170816 | tf_op jit(solution)/shard_map/while/body/eval_jaxpr/convert_element_type | solution.py:68
  256.5 11.5 %fusion.135 = bf16[6144,128]{1,0:T(8,128)(2,1)S(1)} fusion(f32[128]{0:T(128)S(1)} %iota_add_fusion.8, f32[6144]{0:T(1024)S(1)} %bitcast.158), kind=kLoop, calls=%fused_computation.30.clone.1 | loop fusion | flops 3932160 | bytes 1597952 | tf_op jit(solution)/shard_map/while/body/eval_jaxpr/neg | solution.py:69
  268.0 1.8 fusion.137
  271.5 23.7 %fusion.136 = (bf16[256,6144]{1,0:T(8,128)(2,1)S(1)}, bf16[256,6144]{1,0:T(8,128)(2,1)S(1)}) fusion(f32[6144]{0:T(1024)S(1)} %bitcast.160, f32[8,6144]{1,0:T(8,128)S(1)} %broadcast_multiply_fusion.4, f32[32,6144]{1,0:T(8,128)S(1)} %broadcast_multiply_fusion.5, f32[6144]{0:T(1024)S(1)} %bitcast.159), kind=kLoop, calls=%fused_computation.6.clone.1 | loop fusion | flops 14155776 | bytes 7323648 | tf_op jit(solution)/shard_map/while/body/eval_jaxpr/convert_element_type | solution.py:63
  295.2 12.3 %fusion.134 = (bf16[6144,128]{1,0:T(8,128)(2,1)S(1)}, bf16[6144,128]{1,0:T(8,128)(2,1)S(1)}) fusion(f32[128]{0:T(128)S(1)} %iota_add_fusion.8, f32[6144]{0:T(1024)S(1)} %bitcast.157), kind=kLoop, calls=%fused_computation.26.clone.2 | loop fusion | flops 2359296 | bytes 3170816 | tf_op jit(solution)/shard_map/while/body/eval_jaxpr/convert_element_type | solution.py:68
  307.6 11.5 %fusion.135 = bf16[6144,128]{1,0:T(8,128)(2,1)S(1)} fusion(f32[128]{0:T(128)S(1)} %iota_add_fusion.8, f32[6144]{0:T(1024)S(1)} %bitcast.158), kind=kLoop, calls=%fused_computation.30.clone.1 | loop fusion | flops 3932160 | bytes 1597952 | tf_op jit(solution)/shard_map/while/body/eval_jaxpr/neg | solution.py:69
  319.1 1.8 fusion.137
  322.6 23.7 %fusion.136 = (bf16[256,6144]{1,0:T(8,128)(2,1)S(1)}, bf16[256,6144]{1,0:T(8,128)(2,1)S(1)}) fusion(f32[6144]{0:T(1024)S(1)} %bitcast.160, f32[8,6144]{1,0:T(8,128)S(1)} %broadcast_multiply_fusion.4, f32[32,6144]{1,0:T(8,128)S(1)} %broadcast_multiply_fusion.5, f32[6144]{0:T(1024)S(1)} %bitcast.159), kind=kLoop, calls=%fused_computation.6.clone.1 | loop fusion | flops 14155776 | bytes 7323648 | tf_op jit(solution)/shard_map/while/body/eval_jaxpr/convert_element_type | solution.py:63
  346.3 12.3 %fusion.134 = (bf16[6144,128]{1,0:T(8,128)(2,1)S(1)}, bf16[6144,128]{1,0:T(8,128)(2,1)S(1)}) fusion(f32[128]{0:T(128)S(1)} %iota_add_fusion.8, f32[6144]{0:T(1024)S(1)} %bitcast.157), kind=kLoop, calls=%fused_computation.26.clone.2 | loop fusion | flops 2359296 | bytes 3170816 | tf_op jit(solution)/shard_map/while/body/eval_jaxpr/convert_element_type | solution.py:68
  358.7 11.5 %fusion.135 = bf16[6144,128]{1,0:T(8,128)(2,1)S(1)} fusion(f32[128]{0:T(128)S(1)} %iota_add_fusion.8, f32[6144]{0:T(1024)S(1)} %bitcast.158), kind=kLoop, calls=%fused_computation.30.clone.1 | loop fusion | flops 3932160 | bytes 1597952 | tf_op jit(solution)/shard_map/while/body/eval_jaxpr/neg | solution.py:69
  370.2 1.8 fusion.137
  373.6 23.7 %fusion.136 = (bf16[256,6144]{1,0:T(8,128)(2,1)S(1)}, bf16[256,6144]{1,0:T(8,128)(2,1)S(1)}) fusion(f32[6144]{0:T(1024)S(1)} %bitcast.160, f32[8,6144]{1,0:T(8,128)S(1)} %broadcast_multiply_fusion.4, f32[32,6144]{1,0:T(8,128)S(1)} %broadcast_multiply_fusion.5, f32[6144]{0:T(1024)S(1)} %bitcast.159), kind=kLoop, calls=%fused_computation.6.clone.1 | loop fusion | flops 14155776 | bytes 7323648 | tf_op jit(solution)/shard_map/while/body/eval_jaxpr/convert_element_type | solution.py:63
  397.4 12.3 %fusion.134 = (bf16[6144,128]{1,0:T(8,128)(2,1)S(1)}, bf16[6144,128]{1,0:T(8,128)(2,1)S(1)}) fusion(f32[128]{0:T(128)S(1)} %iota_add_fusion.8, f32[6144]{0:T(1024)S(1)} %bitcast.157), kind=kLoop, calls=%fused_computation.26.clone.2 | loop fusion | flops 2359296 | bytes 3170816 | tf_op jit(solution)/shard_map/while/body/eval_jaxpr/convert_element_type | solution.py:68
  409.7 11.5 %fusion.135 = bf16[6144,128]{1,0:T(8,128)(2,1)S(1)} fusion(f32[128]{0:T(128)S(1)} %iota_add_fusion.8, f32[6144]{0:T(1024)S(1)} %bitcast.158), kind=kLoop, calls=%fused_computation.30.clone.1 | loop fusion | flops 3932160 | bytes 1597952 | tf_op jit(solution)/shard_map/while/body/eval_jaxpr/neg | solution.py:69
  421.3 1.8 fusion.137
  424.7 23.7 %fusion.136 = (bf16[256,6144]{1,0:T(8,128)(2,1)S(1)}, bf16[256,6144]{1,0:T(8,128)(2,1)S(1)}) fusion(f32[6144]{0:T(1024)S(1)} %bitcast.160, f32[8,6144]{1,0:T(8,128)S(1)} %broadcast_multiply_fusion.4, f32[32,6144]{1,0:T(8,128)S(1)} %broadcast_multiply_fusion.5, f32[6144]{0:T(1024)S(1)} %bitcast.159), kind=kLoop, calls=%fused_computation.6.clone.1 | loop fusion | flops 14155776 | bytes 7323648 | tf_op jit(solution)/shard_map/while/body/eval_jaxpr/convert_element_type | solution.py:63
  448.5 12.3 %fusion.134 = (bf16[6144,128]{1,0:T(8,128)(2,1)S(1)}, bf16[6144,128]{1,0:T(8,128)(2,1)S(1)}) fusion(f32[128]{0:T(128)S(1)} %iota_add_fusion.8, f32[6144]{0:T(1024)S(1)} %bitcast.157), kind=kLoop, calls=%fused_computation.26.clone.2 | loop fusion | flops 2359296 | bytes 3170816 | tf_op jit(solution)/shard_map/while/body/eval_jaxpr/convert_element_type | solution.py:68
  460.8 11.5 %fusion.135 = bf16[6144,128]{1,0:T(8,128)(2,1)S(1)} fusion(f32[128]{0:T(128)S(1)} %iota_add_fusion.8, f32[6144]{0:T(1024)S(1)} %bitcast.158), kind=kLoop, calls=%fused_computation.30.clone.1 | loop fusion | flops 3932160 | bytes 1597952 | tf_op jit(solution)/shard_map/while/body/eval_jaxpr/neg | solution.py:69
  472.3 1.8 fusion.137
  475.2 78.1 %all-reduce.2.cloned.1.call-done = f32[256,128]{1,0:T(8,128)} async-done(((f32[256,128]{1,0:T(8,128)}), f32[256,128]{1,0:T(8,128)}) %all-reduce.2.cloned.1.call-update) | async-done | bytes 131088 | tf_op jit(solution)/shard_map/psum | solution.py:107
  553.3 1.0 fusion.59
  554.3 9.1 %collective-permute-start = (bf16[8,8,128]{2,0,1:T(8,128)(2,1)S(1)}, bf16[8,8,128]{2,0,1:T(8,128)(2,1)S(1)}, u32[]{:S(2)}, u32[]{:S(2)}) collective-permute-start(bf16[8,8,128]{2,0,1:T(8,128)(2,1)S(1)} %get-tuple-element.119), channel_id=1, source_target_pairs={{0,8},{8,16},{16,24},{24,32},{32,40},{40,48},{48,56},{56,64},{64,7... | collective-permute-start | bytes 49160 | tf_op jit(solution)/shard_map/ppermute | solution.py:31
  563.5 1.9 collective-permute-start.1
  565.5 3.0 collective-permute-done.1
  569.1 1.2 fusion.36
  570.3 1.9 collective-permute-start.2
  572.2 2.4 collective-permute-start.3
  574.6 2.6 collective-permute-done.3
  577.8 1.2 fusion.115
  579.0 1.9 collective-permute-start.4
  580.9 2.4 collective-permute-start.5
  583.3 2.7 collective-permute-done.5
  586.8 1.9 collective-permute-start.6
  588.8 2.4 collective-permute-start.7
  591.2 3.1 collective-permute-done.7
  595.1 1.9 collective-permute-start.8
  597.1 2.6 collective-permute-start.9
  599.7 4.6 collective-permute-done.9
  605.1 1.9 collective-permute-start.10
  607.0 2.4 collective-permute-start.11
  609.4 4.8 collective-permute-done.11
  615.0 1.9 collective-permute-start.12
  617.0 2.4 collective-permute-start.13
  619.4 4.8 collective-permute-done.13
  625.0 1.9 collective-permute-start.14
  626.9 2.4 collective-permute-start.15
  630.0 4.1 collective-permute-done.15
  (142 shorter events, 20.4 us)
Async XLA Ops:
  7.2 57.2 %all-gather.2.cloned.1.call-start = ((), (), s32[]{:S(2)}) async-start(), calls=%async_computation | async-start | bytes 1769472 | tf_op jit(solution)/shard_map/all_gather | solution.py:102
  11.0 542.3 %all-reduce.2.cloned.1.call-start = ((), (), s32[]{:S(2)}) async-start(), calls=%async_computation.1 | async-start | bytes 262144 | tf_op jit(solution)/shard_map/psum | solution.py:107
  553.3 33.3 %copy-start = (f32[256,128]{1,0:T(8,128)S(1)}, f32[256,128]{1,0:T(8,128)}, u32[]{:S(2)}) copy-start(f32[256,128]{1,0:T(8,128)} %all-reduce.2.cloned.1.call-done) | copy-start | bytes 393220
  554.3 11.2 %collective-permute-start = (bf16[8,8,128]{2,0,1:T(8,128)(2,1)S(1)}, bf16[8,8,128]{2,0,1:T(8,128)(2,1)S(1)}, u32[]{:S(2)}, u32[]{:S(2)}) collective-permute-start(bf16[8,8,128]{2,0,1:T(8,128)(2,1)S(1)} %get-tuple-element.119), channel_id=1, source_target_pairs={{0,8},{8,16},{16,24},{24,32},{32,40},{40,48},{48,56},{56,64},{64,7... | collective-permute-start | bytes 49160 | tf_op jit(solution)/shard_map/ppermute | solution.py:31
  563.5 5.1 collective-permute-start.1
  570.3 4.3 collective-permute-start.2
  572.2 5.1 collective-permute-start.3
  579.0 4.3 collective-permute-start.4
  580.9 5.1 collective-permute-start.5
  586.8 4.3 collective-permute-start.6
  588.8 5.5 collective-permute-start.7
  595.1 4.5 collective-permute-start.8
  597.1 7.2 %collective-permute-start.9 = (bf16[8,8,128]{2,1,0:T(8,128)(2,1)S(1)}, bf16[8,8,128]{2,1,0:T(8,128)(2,1)S(1)}, u32[]{:S(2)}, u32[]{:S(2)}) collective-permute-start(bf16[8,8,128]{2,1,0:T(8,128)(2,1)S(1)} %get-tuple-element.112), channel_id=1, source_target_pairs={{8,0},{16,8},{24,16},{32,24},{40,32},{48,40},{56,48},{64,56},{72,6... | collective-permute-start | bytes 49160 | tf_op jit(solution)/shard_map/ppermute | solution.py:32
  605.1 4.3 collective-permute-start.10
  607.0 7.2 %collective-permute-start.11 = (bf16[8,8,128]{2,1,0:T(8,128)(2,1)S(1)}, bf16[8,8,128]{2,1,0:T(8,128)(2,1)S(1)}, u32[]{:S(2)}, u32[]{:S(2)}) collective-permute-start(bf16[8,8,128]{2,1,0:T(8,128)(2,1)S(1)} %get-tuple-element.110), channel_id=1, source_target_pairs={{8,0},{16,8},{24,16},{32,24},{40,32},{48,40},{56,48},{64,56},{72,6... | collective-permute-start | bytes 49160 | tf_op jit(solution)/shard_map/ppermute | solution.py:32
  615.0 4.3 collective-permute-start.12
  617.0 7.2 %collective-permute-start.13 = (bf16[8,8,128]{2,1,0:T(8,128)(2,1)S(1)}, bf16[8,8,128]{2,1,0:T(8,128)(2,1)S(1)}, u32[]{:S(2)}, u32[]{:S(2)}) collective-permute-start(bf16[8,8,128]{2,1,0:T(8,128)(2,1)S(1)} %get-tuple-element.108), channel_id=1, source_target_pairs={{8,0},{16,8},{24,16},{32,24},{40,32},{48,40},{56,48},{64,56},{72,6... | collective-permute-start | bytes 49160 | tf_op jit(solution)/shard_map/ppermute | solution.py:32
  625.0 5.0 collective-permute-start.14
  626.9 7.2 %collective-permute-start.15 = (bf16[8,8,128]{2,1,0:T(8,128)(2,1)S(1)}, bf16[8,8,128]{2,1,0:T(8,128)(2,1)S(1)}, u32[]{:S(2)}, u32[]{:S(2)}) collective-permute-start(bf16[8,8,128]{2,1,0:T(8,128)(2,1)S(1)} %get-tuple-element.106), channel_id=1, source_target_pairs={{8,0},{16,8},{24,16},{32,24},{40,32},{48,40},{56,48},{64,56},{72,6... | collective-permute-start | bytes 49160 | tf_op jit(solution)/shard_map/ppermute | solution.py:32
Sparse Core Ops, SparseCore 0:
  11.1 53.2 all-gather.1
  475.2 78.0 all-reduce.1
where the time goes:
time: 649 us; the launch traced here: 642 us
  other arithmetic  389 us (60%)
  waiting for transfers between devices  130 us (20%)
  starting transfers between devices  41.6 us (6%)
  blocking collectives  30.3 us (5%)
  matrix products  23.3 us (4%)
  between operations  14.6 us (2%)
  local copies, waits for them, and re-layouts  8.06 us (1%)
    convert_element_type x8, other arithmetic, beam_freq(): (real_in * cosine + imag_in * sine).astype(jnp.bfloat16)  190 us
    convert_element_type x8, other arithmetic, beam_freq(): depth_imag = jnp.sin(phase_z).astype(jnp.bfloat16)  98.6 us
    neg x8, other arithmetic, beam_freq(): upper_rows = jnp.concatenate([depth_real, -depth_imag], axis=1)  92.1 us
    psum x1, waiting for transfers between devices, per_device(): summed = lax.psum(local_power, 'sta')  78.1 us
    all_gather x1, blocking collectives, per_device(): lax.all_gather(slowness, 'sta', axis=2, tiled=True)[0]  30.3 us
    ppermute x8, waiting for transfers between devices, with_halo(): after = lax.ppermute(leading, axis, down)  29.6 us
    ppermute x8, starting transfers between devices, with_halo(): before = lax.ppermute(last, axis, up)  22.6 us
    all_gather x1, waiting for transfers between devices, per_device(): lax.all_gather(aligned, 'sta', axis=2, tiled=True)  22 us
  transfers between devices with their start and end apart: 18, of which 10 were waited for; matrix products, arithmetic and copies ran while one was open for 0% of the time, Pallas kernels for 0%

commit v1 on v0

--- a/solution.py
+++ b/solution.py
@@ -4,6 +4,8 @@
 import jax.numpy as jnp
 from jax import lax
 from jax.sharding import PartitionSpec as P
+from jax.experimental import pallas as pl
+from jax.experimental.pallas import tpu as pltpu
 
 STATIONS = 6144
 FREQS = 64
@@ -72,6 +74,95 @@
     return jnp.dot(left_side, right_side, preferred_element_type=jnp.float32)
 
 
+CHUNK = 256
+
+
+def exp_neg(angle):
+    return jnp.cos(angle), -jnp.sin(angle)
+
+
+def beam_kernel(omega_ref, aligned_ref, slow_ref, power_ref, acc_ref, left_ref, right_ref):
+    bins, stations = aligned_ref.shape[0], aligned_ref.shape[2]
+    width = CHUNK
+    rows8 = lax.broadcasted_iota(jnp.int32, (8, width), 0).astype(jnp.float32)
+    rows16 = lax.broadcasted_iota(jnp.int32, (16, width), 0).astype(jnp.float32)
+    power_ref[...] = jnp.zeros_like(power_ref)
+
+    def per_bin(f, carry):
+        omega = omega_ref[f]
+        acc_ref[...] = jnp.zeros_like(acc_ref)
+
+        def per_chunk(k, inner):
+            cols = pl.ds(pl.multiple_of(k * width, width), width)
+            turn_x = omega * slow_ref[0:1, cols].astype(jnp.float32)
+            turn_y = omega * slow_ref[1:2, cols].astype(jnp.float32)
+            turn_z = omega * slow_ref[2:3, cols].astype(jnp.float32)
+            real_in = aligned_ref[f, 0:1, cols].astype(jnp.float32)
+            imag_in = aligned_ref[f, 1:2, cols].astype(jnp.float32)
+            a_r, a_i = exp_neg(turn_x * (rows8 - 3.5))
+            b_r, b_i = exp_neg(turn_x * (8.0 * (rows8 - 1.5)))
+            y_r, y_i = exp_neg(turn_y * (rows8 - 3.5))
+            c_r, c_i = exp_neg(turn_z * (rows16 - 7.5))
+            d_r, d_i = exp_neg(turn_z * (16.0 * (rows8 - 3.5)))
+            for m in range(CX // 8):
+                bm_r, bm_i = b_r[m : m + 1], b_i[m : m + 1]
+                x_r = bm_r * a_r - bm_i * a_i
+                x_i = bm_r * a_i + bm_i * a_r
+                p_r = real_in * x_r - imag_in * x_i
+                p_i = real_in * x_i + imag_in * x_r
+                for j in range(0, 8, 2):
+                    parts_r, parts_i = [], []
+                    for jj in (j, j + 1):
+                        px_r, px_i = p_r[jj : jj + 1], p_i[jj : jj + 1]
+                        parts_r.append(px_r * y_r - px_i * y_i)
+                        parts_i.append(px_r * y_i + px_i * y_r)
+                    row = (8 * m + j) * CY
+                    left_ref[row : row + 16, 0:width] = jnp.concatenate(parts_r, axis=0).astype(jnp.bfloat16)
+                    left_ref[row : row + 16, width : 2 * width] = jnp.concatenate(parts_i, axis=0).astype(jnp.bfloat16)
+            for m in range(CZ // 16):
+                dm_r, dm_i = d_r[m : m + 1], d_i[m : m + 1]
+                z_r = dm_r * c_r - dm_i * c_i
+                z_i = dm_r * c_i + dm_i * c_r
+                cos_z = z_r.astype(jnp.bfloat16)
+                sin_z = (-z_i).astype(jnp.bfloat16)
+                row = 16 * m
+                right_ref[row : row + 16, 0:width] = cos_z
+                right_ref[row : row + 16, width : 2 * width] = sin_z
+                right_ref[CZ + row : CZ + row + 16, 0:width] = -sin_z
+                right_ref[CZ + row : CZ + row + 16, width : 2 * width] = cos_z
+            acc_ref[...] += lax.dot_general(
+                left_ref[...], right_ref[...], (((1,), (1,)), ((), ())), preferred_element_type=jnp.float32
+            )
+            return inner
+
+        lax.fori_loop(0, stations // width, per_chunk, 0)
+        beams = acc_ref[...]
+        squares = beams * beams
+        power_ref[...] += squares[:, :CZ] + squares[:, CZ:]
+        return carry
+
+    lax.fori_loop(0, bins, per_bin, 0)
+
+
+def beam_power(omegas, aligned_rows, slow_rows):
+    width = CHUNK
+    return pl.pallas_call(
+        beam_kernel,
+        out_shape=jax.ShapeDtypeStruct((CX * CY, CZ), jnp.float32),
+        in_specs=[
+            pl.BlockSpec(memory_space=pltpu.SMEM),
+            pl.BlockSpec(memory_space=pltpu.VMEM),
+            pl.BlockSpec(memory_space=pltpu.VMEM),
+        ],
+        out_specs=pl.BlockSpec(memory_space=pltpu.VMEM),
+        scratch_shapes=[
+            pltpu.VMEM((CX * CY, 2 * CZ), jnp.float32),
+            pltpu.VMEM((CX * CY, 2 * width), jnp.bfloat16),
+            pltpu.VMEM((2 * CZ, 2 * width), jnp.bfloat16),
+        ],
+    )(omegas, aligned_rows, slow_rows)
+
+
 def freq_beams(freq_ids, aligned_rows, slow_rows):
     return lax.map(lambda pair: beam_freq(pair[0], pair[1], slow_rows), (freq_ids, aligned_rows))
 
@@ -101,9 +192,8 @@
     rows = lax.dynamic_slice_in_dim(
         lax.all_gather(aligned, "sta", axis=2, tiled=True), first_bin, own_count, 0
     )
-    beams = freq_beams(own_ids, rows, lax.all_gather(slowness, "sta", axis=2, tiled=True)[0])
-    squares = jnp.sum(beams * beams, axis=0)
-    local_power = squares[:, :CZ] + squares[:, CZ:]
+    omegas = (F0 + own_ids).astype(jnp.float32) * (TWO_PI / NT)
+    local_power = beam_power(omegas, rows, lax.all_gather(slowness, "sta", axis=2, tiled=True)[0])
     summed = lax.psum(local_power, "sta")
     stacked = (summed / (FREQS * STATIONS) + BACKGROUND).reshape(CX, CY, CZ)
     square_y = band_matrix(spread_taps[1], CY)[:, HALF : HALF + CY]

time: 649 us -> 341 us (0.53)
  other arithmetic: 389 us -> 13.8 us
  Pallas kernels: 0 us -> 90 us
  matrix products: 23.3 us -> 7.87 us
    convert_element_type x24 -> x1, other arithmetic: 289 us -> 0.94 us  [align_rows(): real_in = spectra[:, 0, :].astype(jnp.float32)]
    neg x8 -> x0, other arithmetic: 92.1 us -> none  [beam_freq(): upper_rows = jnp.concatenate([depth_real, -depth_imag], axis=1)]
    pallas_call x0 -> x1, Pallas kernels: none -> 90 us  [beam_power(): pl.pallas_call(beam_kernel, out_shape=jax.ShapeDtypeStruct((CX * CY, CZ),...]
    dot_general x8 -> x0, matrix products: 14.6 us -> none  [beam_freq(): return jnp.dot(left_side, right_side, preferred_element_type=jnp.float32)]
    another operation x1, other arithmetic: 0.93 us -> 8.39 us
where the time goes in v1:
time: 341 us; the launch traced here: 334 us
  waiting for transfers between devices  133 us (39%)
  Pallas kernels  90 us (26%)
  starting transfers between devices  41.4 us (12%)
  blocking collectives  31.9 us (9%)
  between operations  14.6 us (4%)
  other arithmetic  13.8 us (4%)
  matrix products  7.87 us (2%)
    pallas_call x1, Pallas kernels, beam_power(): pl.pallas_call(beam_kernel, out_shape=jax.ShapeDtypeStruct((CX * CY, CZ),...  90 us
    psum x1, waiting for transfers between devices, per_device(): summed = lax.psum(local_power, 'sta')  78.5 us
    all_gather x1, blocking collectives, per_device(): lax.all_gather(slowness, 'sta', axis=2, tiled=True)[0]  31.9 us
    ppermute x8, waiting for transfers between devices, with_halo(): after = lax.ppermute(leading, axis, down)  29.8 us
    all_gather x1, waiting for transfers between devices, per_device(): lax.all_gather(aligned, 'sta', axis=2, tiled=True)  24.7 us
    ppermute x8, starting transfers between devices, with_halo(): before = lax.ppermute(last, axis, up)  22.6 us
    ppermute x8, starting transfers between devices, with_halo(): after = lax.ppermute(leading, axis, down)  18.7 us
    another operation x1, other arithmetic  8.39 us
  transfers between devices with their start and end apart: 18, of which 10 were waited for; matrix products, arithmetic and copies ran while one was open for 0% of the time, Pallas kernels for 0%

profile of v1, /device:TPU:1, one launch (start us, length us, event | category | flops | bytes accessed | tf_op | source)
XLA Modules:
  0.0 334.3 jit_solution(12145630546311299051)
XLA Ops:
  7.2 0.9 copy_convert_fusion.1
  8.2 0.7 reduce
  8.9 8.4 %add_convert_fusion = (bf16[64,1,768]{2,1,0:T(2,128)(2,1)S(1)}, bf16[64,1,768]{2,1,0:T(2,128)(2,1)S(1)}) fusion(f32[64,1,768]{2,0,1:T(8,128)S(1)} %copy_convert_fusion.1, bf16[64,2,768]{2,1,0:T(2,128)(2,1)} %param.4, s32[768]{0:T(1024)S(1)} %reduce, s32[64]{0:T(128)S(1)} %iota_add_fusion), kind=kLoop, calls=%fused_computation.30 | loop fusion | flops 884736 | bytes 494848 | tf_op jit(solution)/shard_map/convert
  17.3 1.1 pad_maximum_fusion
  18.4 0.0 all-reduce.2.cloned.1.call-start
  18.5 31.9 %all_gather.7 = bf16[1,3,6144]{2,1,0:T(4,128)(2,1)} all-gather(bf16[1,3,768]{2,1,0:T(4,128)(2,1)S(1)} %copy-done.1), channel_id=1, replica_groups=mesh['grid'=16,'sta'=8] {'sta'}, dimensions={2}, use_global_device_ids=true | all-gather | bytes 41472 | tf_op jit(solution)/shard_map/all_gather | solution.py:196
  50.4 0.5 convert_multiply_fusion.omega_ref
  50.9 0.2 select_reduce_fusion
  51.1 24.7 %all-gather.2.cloned.1.call-done = bf16[64,2,6144]{2,1,0:T(2,128)(2,1)} async-done(((bf16[64,2,768]{2,1,0:T(2,128)(2,1)}), bf16[64,2,6144]{2,1,0:T(2,128)(2,1)}) %all-gather.2.cloned.1.call-update) | async-done | bytes 1572880 | tf_op jit(solution)/shard_map/all_gather | solution.py:193
  75.8 1.7 constant_dynamic-slice_fusion.aligned_ref
  77.5 90.0 %shard_map.62 = f32[256,128]{1,0:T(8,128)} custom-call(f32[8]{0:T(128)} %convert_multiply_fusion.omega_ref, bf16[8,2,6144]{2,1,0:T(2,128)(2,1)} %constant_dynamic-slice_fusion.aligned_ref, bf16[3,6144]{1,0:T(4,128)(2,1)} %bitcast.107), custom_call_target="tpu_custom_call" | custom-call | tf_op jit(solution)/shard_map/pallas_call | solution.py:149
  167.5 0.1 select_reduce_fusion.1
  167.6 78.5 %all-reduce.2.cloned.1.call-done = f32[256,128]{1,0:T(8,128)} async-done(((f32[256,128]{1,0:T(8,128)}), f32[256,128]{1,0:T(8,128)}) %all-reduce.2.cloned.1.call-update) | async-done | bytes 131088 | tf_op jit(solution)/shard_map/psum | solution.py:197
  246.1 1.0 fusion.15
  247.1 9.1 %collective-permute-start = (bf16[8,8,128]{2,0,1:T(8,128)(2,1)S(1)}, bf16[8,8,128]{2,0,1:T(8,128)(2,1)S(1)}, u32[]{:S(2)}, u32[]{:S(2)}) collective-permute-start(bf16[8,8,128]{2,0,1:T(8,128)(2,1)S(1)} %get-tuple-element.18), channel_id=1, source_target_pairs={{0,8},{8,16},{16,24},{24,32},{32,40},{40,48},{48,56},{56,64},{64,7... | collective-permute-start | bytes 49160 | tf_op jit(solution)/shard_map/ppermute | solution.py:33
  256.3 1.9 collective-permute-start.1
  258.2 0.1 select_reduce_fusion.2
  258.3 3.0 collective-permute-done.1
  261.3 0.2 fusion.17
  261.5 0.3 convolution_bitcast_fusion.7
  261.9 1.2 fusion.1
  263.1 1.9 collective-permute-start.2
  265.0 2.4 collective-permute-start.3
  267.4 2.6 collective-permute-done.3
  270.1 0.2 fusion.35
  270.3 0.3 convolution_bitcast_fusion.6
  270.6 0.3 fusion.72
  270.9 1.9 collective-permute-start.4
  272.8 2.4 collective-permute-start.5
  275.3 2.7 collective-permute-done.5
  277.9 0.2 fusion.33
  278.1 0.3 convolution_bitcast_fusion.5
  278.5 0.3 fusion.2
  278.8 1.9 collective-permute-start.6
  280.7 2.4 collective-permute-start.7
  283.1 3.1 collective-permute-done.7
  286.2 0.2 fusion.31
  286.4 0.3 convolution_bitcast_fusion.4
  286.8 0.3 fusion.73
  287.0 1.9 collective-permute-start.8
  289.0 2.4 collective-permute-start.9
  291.4 4.8 %collective-permute-done.9 = bf16[8,8,128]{2,1,0:T(8,128)(2,1)S(1)} collective-permute-done((bf16[8,8,128]{2,1,0:T(8,128)(2,1)S(1)}, bf16[8,8,128]{2,1,0:T(8,128)(2,1)S(1)}, u32[]{:S(2)}, u32[]{:S(2)}) %collective-permute-start.9) | collective-permute-done | bytes 16416 | tf_op jit(solution)/shard_map/ppermute | solution.py:34
  296.2 0.2 fusion.29
  296.4 0.3 convolution_bitcast_fusion.3
  296.7 0.3 fusion.3
  297.0 1.9 collective-permute-start.10
  298.9 2.4 collective-permute-start.11
  301.3 4.8 %collective-permute-done.11 = bf16[8,8,128]{2,1,0:T(8,128)(2,1)S(1)} collective-permute-done((bf16[8,8,128]{2,1,0:T(8,128)(2,1)S(1)}, bf16[8,8,128]{2,1,0:T(8,128)(2,1)S(1)}, u32[]{:S(2)}, u32[]{:S(2)}) %collective-permute-start.11) | collective-permute-done | bytes 16416 | tf_op jit(solution)/shard_map/ppermute | solution.py:34
  306.1 0.2 fusion.27
  306.3 0.3 convolution_bitcast_fusion.2
  306.7 0.3 fusion.74
  306.9 1.9 collective-permute-start.12
  308.9 2.4 collective-permute-start.13
  311.3 4.8 %collective-permute-done.13 = bf16[8,8,128]{2,1,0:T(8,128)(2,1)S(1)} collective-permute-done((bf16[8,8,128]{2,1,0:T(8,128)(2,1)S(1)}, bf16[8,8,128]{2,1,0:T(8,128)(2,1)S(1)}, u32[]{:S(2)}, u32[]{:S(2)}) %collective-permute-start.13) | collective-permute-done | bytes 16416 | tf_op jit(solution)/shard_map/ppermute | solution.py:34
  316.1 0.2 fusion.25
  316.3 0.3 convolution_bitcast_fusion.1
  316.6 0.3 fusion.4
  316.9 1.9 collective-permute-start.14
  318.8 2.4 collective-permute-start.15
  321.2 0.7 fusion.16
  321.9 4.1 %collective-permute-done.15 = bf16[8,8,128]{2,1,0:T(8,128)(2,1)S(1)} collective-permute-done((bf16[8,8,128]{2,1,0:T(8,128)(2,1)S(1)}, bf16[8,8,128]{2,1,0:T(8,128)(2,1)S(1)}, u32[]{:S(2)}, u32[]{:S(2)}) %collective-permute-start.15) | collective-permute-done | bytes 16416 | tf_op jit(solution)/shard_map/ppermute | solution.py:34
  326.0 0.2 fusion.23
  326.2 0.3 convolution_bitcast_fusion
  326.6 0.9 fusion
  (38 shorter events, 0.3 us)
Async XLA Ops:
  7.2 11.3 %copy-start.1 = (bf16[1,3,768]{2,1,0:T(4,128)(2,1)S(1)}, bf16[1,3,768]{2,1,0:T(4,128)(2,1)}, u32[]{:S(2)}) copy-start(bf16[1,3,768]{2,1,0:T(4,128)(2,1)} %param.6) | copy-start | bytes 13828
  7.2 43.7 %copy-start.2 = (f32[3,17]{1,0:T(4,128)S(1)}, f32[3,17]{1,0:T(4,128)}, u32[]{:S(2)}) copy-start(f32[3,17]{1,0:T(4,128)} %param.7) | copy-start | bytes 616
  7.2 68.6 %all-gather.2.cloned.1.call-start = ((), (), s32[]{:S(2)}) async-start(), calls=%async_computation | async-start | bytes 1769472 | tf_op jit(solution)/shard_map/all_gather | solution.py:193
  18.4 227.7 %all-reduce.2.cloned.1.call-start = ((), (), s32[]{:S(2)}) async-start(), calls=%async_computation.1 | async-start | bytes 262144 | tf_op jit(solution)/shard_map/psum | solution.py:197
  246.1 24.5 %copy-start = (f32[256,128]{1,0:T(8,128)S(1)}, f32[256,128]{1,0:T(8,128)}, u32[]{:S(2)}) copy-start(f32[256,128]{1,0:T(8,128)} %all-reduce.2.cloned.1.call-done) | copy-start | bytes 393220
  247.1 11.2 %collective-permute-start = (bf16[8,8,128]{2,0,1:T(8,128)(2,1)S(1)}, bf16[8,8,128]{2,0,1:T(8,128)(2,1)S(1)}, u32[]{:S(2)}, u32[]{:S(2)}) collective-permute-start(bf16[8,8,128]{2,0,1:T(8,128)(2,1)S(1)} %get-tuple-element.18), channel_id=1, source_target_pairs={{0,8},{8,16},{16,24},{24,32},{32,40},{40,48},{48,56},{56,64},{64,7... | collective-permute-start | bytes 49160 | tf_op jit(solution)/shard_map/ppermute | solution.py:33
  256.3 5.1 %collective-permute-start.1 = (bf16[8,8,128]{2,0,1:T(8,128)(2,1)S(1)}, bf16[8,8,128]{2,0,1:T(8,128)(2,1)S(1)}, u32[]{:S(2)}, u32[]{:S(2)}) collective-permute-start(bf16[8,8,128]{2,0,1:T(8,128)(2,1)S(1)} %get-tuple-element.19), channel_id=1, source_target_pairs={{8,0},{16,8},{24,16},{32,24},{40,32},{48,40},{56,48},{64,56},{72,6... | collective-permute-start | bytes 49160 | tf_op jit(solution)/shard_map/ppermute | solution.py:34
  263.1 4.3 %collective-permute-start.2 = (bf16[8,8,128]{2,1,0:T(8,128)(2,1)S(1)}, bf16[8,8,128]{2,1,0:T(8,128)(2,1)S(1)}, u32[]{:S(2)}, u32[]{:S(2)}) collective-permute-start(bf16[8,8,128]{2,1,0:T(8,128)(2,1)S(1)} %get-tuple-element.16), channel_id=1, source_target_pairs={{0,8},{8,16},{16,24},{24,32},{32,40},{40,48},{48,56},{56,64},{64,7... | collective-permute-start | bytes 49160 | tf_op jit(solution)/shard_map/ppermute | solution.py:33
  265.0 5.1 %collective-permute-start.3 = (bf16[8,8,128]{2,1,0:T(8,128)(2,1)S(1)}, bf16[8,8,128]{2,1,0:T(8,128)(2,1)S(1)}, u32[]{:S(2)}, u32[]{:S(2)}) collective-permute-start(bf16[8,8,128]{2,1,0:T(8,128)(2,1)S(1)} %get-tuple-element.17), channel_id=1, source_target_pairs={{8,0},{16,8},{24,16},{32,24},{40,32},{48,40},{56,48},{64,56},{72,6... | collective-permute-start | bytes 49160 | tf_op jit(solution)/shard_map/ppermute | solution.py:34
  270.9 4.3 %collective-permute-start.4 = (bf16[8,8,128]{2,1,0:T(8,128)(2,1)S(1)}, bf16[8,8,128]{2,1,0:T(8,128)(2,1)S(1)}, u32[]{:S(2)}, u32[]{:S(2)}) collective-permute-start(bf16[8,8,128]{2,1,0:T(8,128)(2,1)S(1)} %get-tuple-element.14), channel_id=1, source_target_pairs={{0,8},{8,16},{16,24},{24,32},{32,40},{40,48},{48,56},{56,64},{64,7... | collective-permute-start | bytes 49160 | tf_op jit(solution)/shard_map/ppermute | solution.py:33
  272.8 5.1 %collective-permute-start.5 = (bf16[8,8,128]{2,1,0:T(8,128)(2,1)S(1)}, bf16[8,8,128]{2,1,0:T(8,128)(2,1)S(1)}, u32[]{:S(2)}, u32[]{:S(2)}) collective-permute-start(bf16[8,8,128]{2,1,0:T(8,128)(2,1)S(1)} %get-tuple-element.15), channel_id=1, source_target_pairs={{8,0},{16,8},{24,16},{32,24},{40,32},{48,40},{56,48},{64,56},{72,6... | collective-permute-start | bytes 49160 | tf_op jit(solution)/shard_map/ppermute | solution.py:34
  278.8 4.3 %collective-permute-start.6 = (bf16[8,8,128]{2,1,0:T(8,128)(2,1)S(1)}, bf16[8,8,128]{2,1,0:T(8,128)(2,1)S(1)}, u32[]{:S(2)}, u32[]{:S(2)}) collective-permute-start(bf16[8,8,128]{2,1,0:T(8,128)(2,1)S(1)} %get-tuple-element.12), channel_id=1, source_target_pairs={{0,8},{8,16},{16,24},{24,32},{32,40},{40,48},{48,56},{56,64},{64,7... | collective-permute-start | bytes 49160 | tf_op jit(solution)/shard_map/ppermute | solution.py:33
  280.7 5.5 %collective-permute-start.7 = (bf16[8,8,128]{2,1,0:T(8,128)(2,1)S(1)}, bf16[8,8,128]{2,1,0:T(8,128)(2,1)S(1)}, u32[]{:S(2)}, u32[]{:S(2)}) collective-permute-start(bf16[8,8,128]{2,1,0:T(8,128)(2,1)S(1)} %get-tuple-element.13), channel_id=1, source_target_pairs={{8,0},{16,8},{24,16},{32,24},{40,32},{48,40},{56,48},{64,56},{72,6... | collective-permute-start | bytes 49160 | tf_op jit(solution)/shard_map/ppermute | solution.py:34
  287.0 4.3 %collective-permute-start.8 = (bf16[8,8,128]{2,1,0:T(8,128)(2,1)S(1)}, bf16[8,8,128]{2,1,0:T(8,128)(2,1)S(1)}, u32[]{:S(2)}, u32[]{:S(2)}) collective-permute-start(bf16[8,8,128]{2,1,0:T(8,128)(2,1)S(1)} %get-tuple-element.10), channel_id=1, source_target_pairs={{0,8},{8,16},{16,24},{24,32},{32,40},{40,48},{48,56},{56,64},{64,7... | collective-permute-start | bytes 49160 | tf_op jit(solution)/shard_map/ppermute | solution.py:33
  289.0 7.2 %collective-permute-start.9 = (bf16[8,8,128]{2,1,0:T(8,128)(2,1)S(1)}, bf16[8,8,128]{2,1,0:T(8,128)(2,1)S(1)}, u32[]{:S(2)}, u32[]{:S(2)}) collective-permute-start(bf16[8,8,128]{2,1,0:T(8,128)(2,1)S(1)} %get-tuple-element.11), channel_id=1, source_target_pairs={{8,0},{16,8},{24,16},{32,24},{40,32},{48,40},{56,48},{64,56},{72,6... | collective-permute-start | bytes 49160 | tf_op jit(solution)/shard_map/ppermute | solution.py:34
  297.0 4.3 %collective-permute-start.10 = (bf16[8,8,128]{2,1,0:T(8,128)(2,1)S(1)}, bf16[8,8,128]{2,1,0:T(8,128)(2,1)S(1)}, u32[]{:S(2)}, u32[]{:S(2)}) collective-permute-start(bf16[8,8,128]{2,1,0:T(8,128)(2,1)S(1)} %get-tuple-element.8), channel_id=1, source_target_pairs={{0,8},{8,16},{16,24},{24,32},{32,40},{40,48},{48,56},{56,64},{64,7... | collective-permute-start | bytes 49160 | tf_op jit(solution)/shard_map/ppermute | solution.py:33
  298.9 7.2 %collective-permute-start.11 = (bf16[8,8,128]{2,1,0:T(8,128)(2,1)S(1)}, bf16[8,8,128]{2,1,0:T(8,128)(2,1)S(1)}, u32[]{:S(2)}, u32[]{:S(2)}) collective-permute-start(bf16[8,8,128]{2,1,0:T(8,128)(2,1)S(1)} %get-tuple-element.9), channel_id=1, source_target_pairs={{8,0},{16,8},{24,16},{32,24},{40,32},{48,40},{56,48},{64,56},{72,6... | collective-permute-start | bytes 49160 | tf_op jit(solution)/shard_map/ppermute | solution.py:34
  306.9 4.3 %collective-permute-start.12 = (bf16[8,8,128]{2,1,0:T(8,128)(2,1)S(1)}, bf16[8,8,128]{2,1,0:T(8,128)(2,1)S(1)}, u32[]{:S(2)}, u32[]{:S(2)}) collective-permute-start(bf16[8,8,128]{2,1,0:T(8,128)(2,1)S(1)} %get-tuple-element.6), channel_id=1, source_target_pairs={{0,8},{8,16},{16,24},{24,32},{32,40},{40,48},{48,56},{56,64},{64,7... | collective-permute-start | bytes 49160 | tf_op jit(solution)/shard_map/ppermute | solution.py:33
  308.9 7.2 %collective-permute-start.13 = (bf16[8,8,128]{2,1,0:T(8,128)(2,1)S(1)}, bf16[8,8,128]{2,1,0:T(8,128)(2,1)S(1)}, u32[]{:S(2)}, u32[]{:S(2)}) collective-permute-start(bf16[8,8,128]{2,1,0:T(8,128)(2,1)S(1)} %get-tuple-element.7), channel_id=1, source_target_pairs={{8,0},{16,8},{24,16},{32,24},{40,32},{48,40},{56,48},{64,56},{72,6... | collective-permute-start | bytes 49160 | tf_op jit(solution)/shard_map/ppermute | solution.py:34
  316.9 5.0 %collective-permute-start.14 = (bf16[8,8,128]{2,1,0:T(8,128)(2,1)S(1)}, bf16[8,8,128]{2,1,0:T(8,128)(2,1)S(1)}, u32[]{:S(2)}, u32[]{:S(2)}) collective-permute-start(bf16[8,8,128]{2,1,0:T(8,128)(2,1)S(1)} %get-tuple-element.4), channel_id=1, source_target_pairs={{0,8},{8,16},{16,24},{24,32},{32,40},{40,48},{48,56},{56,64},{64,7... | collective-permute-start | bytes 49160 | tf_op jit(solution)/shard_map/ppermute | solution.py:33
  318.8 7.2 %collective-permute-start.15 = (bf16[8,8,128]{2,1,0:T(8,128)(2,1)S(1)}, bf16[8,8,128]{2,1,0:T(8,128)(2,1)S(1)}, u32[]{:S(2)}, u32[]{:S(2)}) collective-permute-start(bf16[8,8,128]{2,1,0:T(8,128)(2,1)S(1)} %get-tuple-element.5), channel_id=1, source_target_pairs={{8,0},{16,8},{24,16},{32,24},{40,32},{48,40},{56,48},{64,56},{72,6... | collective-permute-start | bytes 49160 | tf_op jit(solution)/shard_map/ppermute | solution.py:34
Sparse Core Ops, SparseCore 0:
  18.6 57.1 all-gather.1
  167.6 78.4 all-reduce.1

commit v2 on v1

--- a/solution.py
+++ b/solution.py
@@ -163,6 +163,65 @@
     )(omegas, aligned_rows, slow_rows)
 
 
+def sum_kernel(part_ref, out_ref, recv_ref, local_sem, send_sem, recv_sem):
+    count = recv_ref.shape[0]
+    me = lax.axis_index("sta")
+    tile = lax.axis_index("grid")
+    barrier = pltpu.get_barrier_semaphore()
+    for shift in range(1, count):
+        peer = lax.rem(me + shift, count)
+        pl.semaphore_signal(barrier, inc=1, device_id=(tile, peer), device_id_type=pl.DeviceIdType.MESH)
+    pl.semaphore_wait(barrier, count - 1)
+    own = pltpu.make_async_copy(part_ref, recv_ref.at[me], local_sem.at[0])
+    own.start()
+    copies = []
+    for shift in range(1, count):
+        peer = lax.rem(me + shift, count)
+        copy = pltpu.make_async_remote_copy(
+            src_ref=part_ref,
+            dst_ref=recv_ref.at[me],
+            send_sem=send_sem.at[shift],
+            recv_sem=recv_sem.at[me],
+            device_id=(tile, peer),
+            device_id_type=pl.DeviceIdType.MESH,
+        )
+        copy.start()
+        copies.append(copy)
+    own.wait()
+    for shift in range(1, count):
+        copies[shift - 1].wait_send()
+        source = lax.rem(me + count - shift, count)
+        pltpu.make_async_remote_copy(
+            src_ref=part_ref,
+            dst_ref=recv_ref.at[source],
+            send_sem=send_sem.at[shift],
+            recv_sem=recv_sem.at[source],
+            device_id=(tile, source),
+            device_id_type=pl.DeviceIdType.MESH,
+        ).wait_recv()
+    total = recv_ref[0]
+    for source in range(1, count):
+        total = total + recv_ref[source]
+    out_ref[...] = total
+
+
+def sum_over_sta(part):
+    count = lax.axis_size("sta")
+    return pl.pallas_call(
+        sum_kernel,
+        out_shape=jax.ShapeDtypeStruct(part.shape, jnp.float32),
+        in_specs=[pl.BlockSpec(memory_space=pltpu.VMEM)],
+        out_specs=pl.BlockSpec(memory_space=pltpu.VMEM),
+        scratch_shapes=[
+            pltpu.VMEM((count,) + part.shape, jnp.float32),
+            pltpu.SemaphoreType.DMA((1,)),
+            pltpu.SemaphoreType.DMA((count,)),
+            pltpu.SemaphoreType.DMA((count,)),
+        ],
+        compiler_params=pltpu.CompilerParams(collective_id=0, has_side_effects=True),
+    )(part)
+
+
 def freq_beams(freq_ids, aligned_rows, slow_rows):
     return lax.map(lambda pair: beam_freq(pair[0], pair[1], slow_rows), (freq_ids, aligned_rows))
 
@@ -194,7 +253,7 @@
     )
     omegas = (F0 + own_ids).astype(jnp.float32) * (TWO_PI / NT)
     local_power = beam_power(omegas, rows, lax.all_gather(slowness, "sta", axis=2, tiled=True)[0])
-    summed = lax.psum(local_power, "sta")
+    summed = sum_over_sta(local_power)
     stacked = (summed / (FREQS * STATIONS) + BACKGROUND).reshape(CX, CY, CZ)
     square_y = band_matrix(spread_taps[1], CY)[:, HALF : HALF + CY]
     square_z = band_matrix(spread_taps[2], CZ)[:, HALF : HALF + CZ]

time: 341 us -> 276 us (0.81)
  the two profiles are of different devices: /device:TPU:1 before, /device:TPU:31 now
where the time goes in v2:
time: 276 us
  Pallas kernels  107 us (39%)
  waiting for transfers between devices  62.7 us (23%)
  starting transfers between devices  38.2 us (14%)
  blocking collectives  29.8 us (11%)
  between operations  14.6 us (5%)
  other arithmetic  13.8 us (5%)
  matrix products  7.87 us (3%)
    pallas_call x1, Pallas kernels, beam_power(): pl.pallas_call(beam_kernel, out_shape=jax.ShapeDtypeStruct((CX * CY, CZ),...  90 us
    ppermute x8, waiting for transfers between devices, with_halo(): after = lax.ppermute(leading, axis, down)  37.7 us
    all_gather x1, blocking collectives, per_device(): lax.all_gather(slowness, 'sta', axis=2, tiled=True)[0]  29.8 us
    all_gather x1, waiting for transfers between devices, per_device(): lax.all_gather(aligned, 'sta', axis=2, tiled=True)  24.9 us
    ppermute x8, starting transfers between devices, with_halo(): before = lax.ppermute(last, axis, up)  19.5 us
    ppermute x8, starting transfers between devices, with_halo(): after = lax.ppermute(leading, axis, down)  18.7 us
    pallas_call x1, Pallas kernels, sum_over_sta(): pl.pallas_call(sum_kernel, out_shape=jax.ShapeDtypeStruct(part.shape, jnp...  16.8 us
    another operation x1, other arithmetic  8.39 us
  transfers between devices with their start and end apart: 17, of which 9 were waited for; matrix products, arithmetic and copies ran while one was open for 1% of the time, Pallas kernels for 0%

profile of v2, /device:TPU:31, one launch (start us, length us, event | category | flops | bytes accessed | tf_op | source)
XLA Modules:
  0.0 275.6 jit_solution(16515717172305708677)
XLA Ops:
  7.2 0.0 all-gather.2.cloned.1.call-start
  7.2 0.9 copy_convert_fusion.1
  8.2 0.7 reduce
  8.9 8.4 %add_convert_fusion = (bf16[64,1,768]{2,1,0:T(2,128)(2,1)S(1)}, bf16[64,1,768]{2,1,0:T(2,128)(2,1)S(1)}) fusion(f32[64,1,768]{2,0,1:T(8,128)S(1)} %copy_convert_fusion.1, bf16[64,2,768]{2,1,0:T(2,128)(2,1)} %param.4, s32[768]{0:T(1024)S(1)} %reduce, s32[64]{0:T(128)S(1)} %iota_add_fusion), kind=kLoop, calls=%fused_computation.30 | loop fusion | flops 884736 | bytes 494848 | tf_op jit(solution)/shard_map/convert
  17.3 1.1 pad_maximum_fusion
  18.5 29.8 %all_gather.7 = bf16[1,3,6144]{2,1,0:T(4,128)(2,1)} all-gather(bf16[1,3,768]{2,1,0:T(4,128)(2,1)S(1)} %copy-done.1), channel_id=1, replica_groups=mesh['grid'=16,'sta'=8] {'sta'}, dimensions={2}, use_global_device_ids=true | all-gather | bytes 41472 | tf_op jit(solution)/shard_map/all_gather | solution.py:255
  48.3 0.5 convert_multiply_fusion.omega_ref
  48.8 0.1 select_reduce_fusion.1
  48.9 0.2 select_reduce_fusion
  49.1 24.9 %all-gather.2.cloned.1.call-done = bf16[64,2,6144]{2,1,0:T(2,128)(2,1)} async-done(((bf16[64,2,768]{2,1,0:T(2,128)(2,1)}), bf16[64,2,6144]{2,1,0:T(2,128)(2,1)}) %all-gather.2.cloned.1.call-update) | async-done | bytes 1572880 | tf_op jit(solution)/shard_map/all_gather | solution.py:252
  74.0 1.7 constant_dynamic-slice_fusion.aligned_ref
  75.8 90.0 %shard_map.62.part_ref = f32[256,128]{1,0:T(8,128)} custom-call(f32[8]{0:T(128)} %convert_multiply_fusion.omega_ref, bf16[8,2,6144]{2,1,0:T(2,128)(2,1)} %constant_dynamic-slice_fusion.aligned_ref, bf16[3,6144]{1,0:T(4,128)(2,1)} %bitcast.107), custom_call_target="tpu_custom_call" | custom-call | tf_op jit(solution)/shard_map/pallas_call | solution.py:149
  165.7 16.8 %shard_map.63 = f32[256,128]{1,0:T(8,128)} custom-call(f32[256,128]{1,0:T(8,128)} %shard_map.62.part_ref), custom_call_target="tpu_custom_call" | custom-call | tf_op jit(solution)/shard_map/pallas_call | solution.py:210
  182.6 1.0 fusion.15
  183.6 5.9 %collective-permute-start = (bf16[8,8,128]{2,0,1:T(8,128)(2,1)S(1)}, bf16[8,8,128]{2,0,1:T(8,128)(2,1)S(1)}, u32[]{:S(2)}, u32[]{:S(2)}) collective-permute-start(bf16[8,8,128]{2,0,1:T(8,128)(2,1)S(1)} %get-tuple-element.18), channel_id=1, source_target_pairs={{0,8},{8,16},{16,24},{24,32},{32,40},{40,48},{48,56},{56,64},{64,7... | collective-permute-start | bytes 49160 | tf_op jit(solution)/shard_map/ppermute | solution.py:33
  189.5 1.9 collective-permute-start.1
  191.5 0.1 select_reduce_fusion.2
  191.6 5.1 %collective-permute-done.1 = bf16[8,8,128]{2,0,1:T(8,128)(2,1)S(1)} collective-permute-done((bf16[8,8,128]{2,0,1:T(8,128)(2,1)S(1)}, bf16[8,8,128]{2,0,1:T(8,128)(2,1)S(1)}, u32[]{:S(2)}, u32[]{:S(2)}) %collective-permute-start.1) | collective-permute-done | bytes 16416 | tf_op jit(solution)/shard_map/ppermute | solution.py:34
  196.7 0.2 fusion.17
  196.9 0.3 convolution_bitcast_fusion.7
  197.2 1.2 fusion.1
  198.4 1.9 collective-permute-start.2
  200.4 2.4 collective-permute-start.3
  202.8 4.8 %collective-permute-done.3 = bf16[8,8,128]{2,1,0:T(8,128)(2,1)S(1)} collective-permute-done((bf16[8,8,128]{2,1,0:T(8,128)(2,1)S(1)}, bf16[8,8,128]{2,1,0:T(8,128)(2,1)S(1)}, u32[]{:S(2)}, u32[]{:S(2)}) %collective-permute-start.3) | collective-permute-done | bytes 16416 | tf_op jit(solution)/shard_map/ppermute | solution.py:34
  207.6 0.2 fusion.35
  207.8 0.3 convolution_bitcast_fusion.6
  208.1 0.3 fusion.72
  208.4 1.9 collective-permute-start.4
  210.3 2.4 collective-permute-start.5
  212.7 4.8 %collective-permute-done.5 = bf16[8,8,128]{2,1,0:T(8,128)(2,1)S(1)} collective-permute-done((bf16[8,8,128]{2,1,0:T(8,128)(2,1)S(1)}, bf16[8,8,128]{2,1,0:T(8,128)(2,1)S(1)}, u32[]{:S(2)}, u32[]{:S(2)}) %collective-permute-start.5) | collective-permute-done | bytes 16416 | tf_op jit(solution)/shard_map/ppermute | solution.py:34
  217.5 0.2 fusion.33
  217.7 0.3 convolution_bitcast_fusion.5
  218.1 0.3 fusion.2
  218.3 1.9 collective-permute-start.6
  220.3 2.4 collective-permute-start.7
  222.7 4.8 %collective-permute-done.7 = bf16[8,8,128]{2,1,0:T(8,128)(2,1)S(1)} collective-permute-done((bf16[8,8,128]{2,1,0:T(8,128)(2,1)S(1)}, bf16[8,8,128]{2,1,0:T(8,128)(2,1)S(1)}, u32[]{:S(2)}, u32[]{:S(2)}) %collective-permute-start.7) | collective-permute-done | bytes 16416 | tf_op jit(solution)/shard_map/ppermute | solution.py:34
  227.5 0.2 fusion.31
  227.7 0.3 convolution_bitcast_fusion.4
  228.0 0.3 fusion.73
  228.3 1.9 collective-permute-start.8
  230.2 2.4 collective-permute-start.9
  232.7 4.8 %collective-permute-done.9 = bf16[8,8,128]{2,1,0:T(8,128)(2,1)S(1)} collective-permute-done((bf16[8,8,128]{2,1,0:T(8,128)(2,1)S(1)}, bf16[8,8,128]{2,1,0:T(8,128)(2,1)S(1)}, u32[]{:S(2)}, u32[]{:S(2)}) %collective-permute-start.9) | collective-permute-done | bytes 16416 | tf_op jit(solution)/shard_map/ppermute | solution.py:34
  237.4 0.2 fusion.29
  237.6 0.3 convolution_bitcast_fusion.3
  238.0 0.3 fusion.3
  238.3 1.9 collective-permute-start.10
  240.2 2.4 collective-permute-start.11
  242.6 4.8 %collective-permute-done.11 = bf16[8,8,128]{2,1,0:T(8,128)(2,1)S(1)} collective-permute-done((bf16[8,8,128]{2,1,0:T(8,128)(2,1)S(1)}, bf16[8,8,128]{2,1,0:T(8,128)(2,1)S(1)}, u32[]{:S(2)}, u32[]{:S(2)}) %collective-permute-start.11) | collective-permute-done | bytes 16416 | tf_op jit(solution)/shard_map/ppermute | solution.py:34
  247.4 0.2 fusion.27
  247.6 0.3 convolution_bitcast_fusion.2
  247.9 0.3 fusion.74
  248.2 1.9 collective-permute-start.12
  250.1 2.4 collective-permute-start.13
  252.6 4.8 %collective-permute-done.13 = bf16[8,8,128]{2,1,0:T(8,128)(2,1)S(1)} collective-permute-done((bf16[8,8,128]{2,1,0:T(8,128)(2,1)S(1)}, bf16[8,8,128]{2,1,0:T(8,128)(2,1)S(1)}, u32[]{:S(2)}, u32[]{:S(2)}) %collective-permute-start.13) | collective-permute-done | bytes 16416 | tf_op jit(solution)/shard_map/ppermute | solution.py:34
  257.3 0.2 fusion.25
  257.5 0.3 convolution_bitcast_fusion.1
  257.9 0.3 fusion.4
  258.2 1.9 collective-permute-start.14
  260.1 2.4 collective-permute-start.15
  262.5 0.7 fusion.16
  263.2 4.1 %collective-permute-done.15 = bf16[8,8,128]{2,1,0:T(8,128)(2,1)S(1)} collective-permute-done((bf16[8,8,128]{2,1,0:T(8,128)(2,1)S(1)}, bf16[8,8,128]{2,1,0:T(8,128)(2,1)S(1)}, u32[]{:S(2)}, u32[]{:S(2)}) %collective-permute-start.15) | collective-permute-done | bytes 16416 | tf_op jit(solution)/shard_map/ppermute | solution.py:34
  267.3 0.2 fusion.23
  267.5 0.3 convolution_bitcast_fusion
  267.8 0.9 fusion
  (36 shorter events, 0.2 us)
Async XLA Ops:
  7.2 11.3 %copy-start.1 = (bf16[1,3,768]{2,1,0:T(4,128)(2,1)S(1)}, bf16[1,3,768]{2,1,0:T(4,128)(2,1)}, u32[]{:S(2)}) copy-start(bf16[1,3,768]{2,1,0:T(4,128)(2,1)} %param.6) | copy-start | bytes 13828
  7.2 41.6 %copy-start.2 = (f32[3,17]{1,0:T(4,128)S(1)}, f32[3,17]{1,0:T(4,128)}, u32[]{:S(2)}) copy-start(f32[3,17]{1,0:T(4,128)} %param.7) | copy-start | bytes 616
  7.2 66.9 %all-gather.2.cloned.1.call-start = ((), (), s32[]{:S(2)}) async-start(), calls=%async_computation | async-start | bytes 1769472 | tf_op jit(solution)/shard_map/all_gather | solution.py:252
  182.6 25.5 %copy-start = (f32[256,128]{1,0:T(8,128)S(1)}, f32[256,128]{1,0:T(8,128)}, u32[]{:S(2)}) copy-start(f32[256,128]{1,0:T(8,128)} %shard_map.63) | copy-start | bytes 393220
  183.6 8.0 %collective-permute-start = (bf16[8,8,128]{2,0,1:T(8,128)(2,1)S(1)}, bf16[8,8,128]{2,0,1:T(8,128)(2,1)S(1)}, u32[]{:S(2)}, u32[]{:S(2)}) collective-permute-start(bf16[8,8,128]{2,0,1:T(8,128)(2,1)S(1)} %get-tuple-element.18), channel_id=1, source_target_pairs={{0,8},{8,16},{16,24},{24,32},{32,40},{40,48},{48,56},{56,64},{64,7... | collective-permute-start | bytes 49160 | tf_op jit(solution)/shard_map/ppermute | solution.py:33
  189.5 7.2 %collective-permute-start.1 = (bf16[8,8,128]{2,0,1:T(8,128)(2,1)S(1)}, bf16[8,8,128]{2,0,1:T(8,128)(2,1)S(1)}, u32[]{:S(2)}, u32[]{:S(2)}) collective-permute-start(bf16[8,8,128]{2,0,1:T(8,128)(2,1)S(1)} %get-tuple-element.19), channel_id=1, source_target_pairs={{8,0},{16,8},{24,16},{32,24},{40,32},{48,40},{56,48},{64,56},{72,6... | collective-permute-start | bytes 49160 | tf_op jit(solution)/shard_map/ppermute | solution.py:34
  198.4 4.3 %collective-permute-start.2 = (bf16[8,8,128]{2,1,0:T(8,128)(2,1)S(1)}, bf16[8,8,128]{2,1,0:T(8,128)(2,1)S(1)}, u32[]{:S(2)}, u32[]{:S(2)}) collective-permute-start(bf16[8,8,128]{2,1,0:T(8,128)(2,1)S(1)} %get-tuple-element.16), channel_id=1, source_target_pairs={{0,8},{8,16},{16,24},{24,32},{32,40},{40,48},{48,56},{56,64},{64,7... | collective-permute-start | bytes 49160 | tf_op jit(solution)/shard_map/ppermute | solution.py:33
  200.4 7.2 %collective-permute-start.3 = (bf16[8,8,128]{2,1,0:T(8,128)(2,1)S(1)}, bf16[8,8,128]{2,1,0:T(8,128)(2,1)S(1)}, u32[]{:S(2)}, u32[]{:S(2)}) collective-permute-start(bf16[8,8,128]{2,1,0:T(8,128)(2,1)S(1)} %get-tuple-element.17), channel_id=1, source_target_pairs={{8,0},{16,8},{24,16},{32,24},{40,32},{48,40},{56,48},{64,56},{72,6... | collective-permute-start | bytes 49160 | tf_op jit(solution)/shard_map/ppermute | solution.py:34
  208.4 4.3 %collective-permute-start.4 = (bf16[8,8,128]{2,1,0:T(8,128)(2,1)S(1)}, bf16[8,8,128]{2,1,0:T(8,128)(2,1)S(1)}, u32[]{:S(2)}, u32[]{:S(2)}) collective-permute-start(bf16[8,8,128]{2,1,0:T(8,128)(2,1)S(1)} %get-tuple-element.14), channel_id=1, source_target_pairs={{0,8},{8,16},{16,24},{24,32},{32,40},{40,48},{48,56},{56,64},{64,7... | collective-permute-start | bytes 49160 | tf_op jit(solution)/shard_map/ppermute | solution.py:33
  210.3 7.2 %collective-permute-start.5 = (bf16[8,8,128]{2,1,0:T(8,128)(2,1)S(1)}, bf16[8,8,128]{2,1,0:T(8,128)(2,1)S(1)}, u32[]{:S(2)}, u32[]{:S(2)}) collective-permute-start(bf16[8,8,128]{2,1,0:T(8,128)(2,1)S(1)} %get-tuple-element.15), channel_id=1, source_target_pairs={{8,0},{16,8},{24,16},{32,24},{40,32},{48,40},{56,48},{64,56},{72,6... | collective-permute-start | bytes 49160 | tf_op jit(solution)/shard_map/ppermute | solution.py:34
  218.3 4.3 %collective-permute-start.6 = (bf16[8,8,128]{2,1,0:T(8,128)(2,1)S(1)}, bf16[8,8,128]{2,1,0:T(8,128)(2,1)S(1)}, u32[]{:S(2)}, u32[]{:S(2)}) collective-permute-start(bf16[8,8,128]{2,1,0:T(8,128)(2,1)S(1)} %get-tuple-element.12), channel_id=1, source_target_pairs={{0,8},{8,16},{16,24},{24,32},{32,40},{40,48},{48,56},{56,64},{64,7... | collective-permute-start | bytes 49160 | tf_op jit(solution)/shard_map/ppermute | solution.py:33
  220.3 7.2 %collective-permute-start.7 = (bf16[8,8,128]{2,1,0:T(8,128)(2,1)S(1)}, bf16[8,8,128]{2,1,0:T(8,128)(2,1)S(1)}, u32[]{:S(2)}, u32[]{:S(2)}) collective-permute-start(bf16[8,8,128]{2,1,0:T(8,128)(2,1)S(1)} %get-tuple-element.13), channel_id=1, source_target_pairs={{8,0},{16,8},{24,16},{32,24},{40,32},{48,40},{56,48},{64,56},{72,6... | collective-permute-start | bytes 49160 | tf_op jit(solution)/shard_map/ppermute | solution.py:34
  228.3 4.3 %collective-permute-start.8 = (bf16[8,8,128]{2,1,0:T(8,128)(2,1)S(1)}, bf16[8,8,128]{2,1,0:T(8,128)(2,1)S(1)}, u32[]{:S(2)}, u32[]{:S(2)}) collective-permute-start(bf16[8,8,128]{2,1,0:T(8,128)(2,1)S(1)} %get-tuple-element.10), channel_id=1, source_target_pairs={{0,8},{8,16},{16,24},{24,32},{32,40},{40,48},{48,56},{56,64},{64,7... | collective-permute-start | bytes 49160 | tf_op jit(solution)/shard_map/ppermute | solution.py:33
  230.2 7.2 %collective-permute-start.9 = (bf16[8,8,128]{2,1,0:T(8,128)(2,1)S(1)}, bf16[8,8,128]{2,1,0:T(8,128)(2,1)S(1)}, u32[]{:S(2)}, u32[]{:S(2)}) collective-permute-start(bf16[8,8,128]{2,1,0:T(8,128)(2,1)S(1)} %get-tuple-element.11), channel_id=1, source_target_pairs={{8,0},{16,8},{24,16},{32,24},{40,32},{48,40},{56,48},{64,56},{72,6... | collective-permute-start | bytes 49160 | tf_op jit(solution)/shard_map/ppermute | solution.py:34
  238.3 4.3 %collective-permute-start.10 = (bf16[8,8,128]{2,1,0:T(8,128)(2,1)S(1)}, bf16[8,8,128]{2,1,0:T(8,128)(2,1)S(1)}, u32[]{:S(2)}, u32[]{:S(2)}) collective-permute-start(bf16[8,8,128]{2,1,0:T(8,128)(2,1)S(1)} %get-tuple-element.8), channel_id=1, source_target_pairs={{0,8},{8,16},{16,24},{24,32},{32,40},{40,48},{48,56},{56,64},{64,7... | collective-permute-start | bytes 49160 | tf_op jit(solution)/shard_map/ppermute | solution.py:33
  240.2 7.2 %collective-permute-start.11 = (bf16[8,8,128]{2,1,0:T(8,128)(2,1)S(1)}, bf16[8,8,128]{2,1,0:T(8,128)(2,1)S(1)}, u32[]{:S(2)}, u32[]{:S(2)}) collective-permute-start(bf16[8,8,128]{2,1,0:T(8,128)(2,1)S(1)} %get-tuple-element.9), channel_id=1, source_target_pairs={{8,0},{16,8},{24,16},{32,24},{40,32},{48,40},{56,48},{64,56},{72,6... | collective-permute-start | bytes 49160 | tf_op jit(solution)/shard_map/ppermute | solution.py:34
  248.2 4.3 %collective-permute-start.12 = (bf16[8,8,128]{2,1,0:T(8,128)(2,1)S(1)}, bf16[8,8,128]{2,1,0:T(8,128)(2,1)S(1)}, u32[]{:S(2)}, u32[]{:S(2)}) collective-permute-start(bf16[8,8,128]{2,1,0:T(8,128)(2,1)S(1)} %get-tuple-element.6), channel_id=1, source_target_pairs={{0,8},{8,16},{16,24},{24,32},{32,40},{40,48},{48,56},{56,64},{64,7... | collective-permute-start | bytes 49160 | tf_op jit(solution)/shard_map/ppermute | solution.py:33
  250.1 7.2 %collective-permute-start.13 = (bf16[8,8,128]{2,1,0:T(8,128)(2,1)S(1)}, bf16[8,8,128]{2,1,0:T(8,128)(2,1)S(1)}, u32[]{:S(2)}, u32[]{:S(2)}) collective-permute-start(bf16[8,8,128]{2,1,0:T(8,128)(2,1)S(1)} %get-tuple-element.7), channel_id=1, source_target_pairs={{8,0},{16,8},{24,16},{32,24},{40,32},{48,40},{56,48},{64,56},{72,6... | collective-permute-start | bytes 49160 | tf_op jit(solution)/shard_map/ppermute | solution.py:34
  258.2 5.0 %collective-permute-start.14 = (bf16[8,8,128]{2,1,0:T(8,128)(2,1)S(1)}, bf16[8,8,128]{2,1,0:T(8,128)(2,1)S(1)}, u32[]{:S(2)}, u32[]{:S(2)}) collective-permute-start(bf16[8,8,128]{2,1,0:T(8,128)(2,1)S(1)} %get-tuple-element.4), channel_id=1, source_target_pairs={{0,8},{8,16},{16,24},{24,32},{32,40},{40,48},{48,56},{56,64},{64,7... | collective-permute-start | bytes 49160 | tf_op jit(solution)/shard_map/ppermute | solution.py:33
  260.1 7.2 %collective-permute-start.15 = (bf16[8,8,128]{2,1,0:T(8,128)(2,1)S(1)}, bf16[8,8,128]{2,1,0:T(8,128)(2,1)S(1)}, u32[]{:S(2)}, u32[]{:S(2)}) collective-permute-start(bf16[8,8,128]{2,1,0:T(8,128)(2,1)S(1)} %get-tuple-element.5), channel_id=1, source_target_pairs={{8,0},{16,8},{24,16},{32,24},{40,32},{48,40},{56,48},{64,56},{72,6... | collective-permute-start | bytes 49160 | tf_op jit(solution)/shard_map/ppermute | solution.py:34
Sparse Core Ops, SparseCore 0:
  18.6 55.4 all-gather.1

commit v3 on v2

--- a/solution.py
+++ b/solution.py
@@ -242,6 +242,47 @@
     return jnp.einsum("xyw,kw->xyk", along_y, square_z, precision=lax.Precision.HIGHEST)
 
 
+def blur_narrowing(volume, taps, square_y, square_z):
+    band_x = band_matrix(taps, volume.shape[0] - 2 * HALF)
+    along_x = jnp.einsum("ip,pyz->iyz", band_x, volume, precision=lax.Precision.HIGHEST)
+    along_y = jnp.einsum("jq,xqz->xjz", square_y, along_x, precision=lax.Precision.HIGHEST)
+    return jnp.einsum("xyw,kw->xyk", along_y, square_z, precision=lax.Precision.HIGHEST)
+
+
+def deblur(stacked, spread_taps):
+    tiles = lax.axis_size("grid")
+    me = lax.axis_index("grid")
+    reach = ITERS * 2 * HALF
+    halo_tiles = -(-reach // CX)
+    before = [
+        lax.ppermute(stacked, "grid", [(i, i + k) for i in range(tiles - k)])
+        for k in range(halo_tiles, 0, -1)
+    ]
+    after = [
+        lax.ppermute(stacked, "grid", [(i + k, i) for i in range(tiles - k)])
+        for k in range(1, halo_tiles + 1)
+    ]
+    cut = halo_tiles * CX - reach
+    observed = jnp.concatenate(before + [stacked] + after, axis=0)
+    observed = observed[cut : observed.shape[0] - cut]
+    width = observed.shape[0]
+    cell = (me - halo_tiles) * CX + cut + jnp.arange(width, dtype=jnp.int32)
+    inside = (cell >= 0) & (cell < tiles * CX)
+    square_y = band_matrix(spread_taps[1], CY)[:, HALF : HALF + CY]
+    square_z = band_matrix(spread_taps[2], CZ)[:, HALF : HALF + CZ]
+    estimate = observed
+    for sweep in range(ITERS):
+        low = 2 * HALF * sweep + HALF
+        blurred = blur_narrowing(estimate, spread_taps[0], square_y, square_z)
+        ratio = jnp.where(
+            inside[low : width - low, None, None], observed[low : width - low] / blurred, 0.0
+        )
+        estimate = estimate[2 * HALF : estimate.shape[0] - 2 * HALF] * blur_narrowing(
+            ratio, spread_taps[0], square_y, square_z
+        )
+    return estimate
+
+
 def per_device(spectra, lag_samples, slowness, spread_taps):
     groups = lax.axis_size("sta")
     own_count = FREQS // groups
@@ -255,13 +296,7 @@
     local_power = beam_power(omegas, rows, lax.all_gather(slowness, "sta", axis=2, tiled=True)[0])
     summed = sum_over_sta(local_power)
     stacked = (summed / (FREQS * STATIONS) + BACKGROUND).reshape(CX, CY, CZ)
-    square_y = band_matrix(spread_taps[1], CY)[:, HALF : HALF + CY]
-    square_z = band_matrix(spread_taps[2], CZ)[:, HALF : HALF + CZ]
-    bands = (band_matrix(spread_taps[0], CX), square_y, square_z)
-    estimate = stacked
-    for sweep in range(ITERS):
-        blurred = blur(estimate, bands)
-        estimate = estimate * blur(stacked / blurred, bands)
+    estimate = deblur(stacked, spread_taps)
     return (stacked[None], estimate[None])
 
 

time: 276 us -> 225 us (0.82)
  the two profiles are of different devices: /device:TPU:31 before, /device:TPU:1 now
where the time goes in v3:
time: 225 us; the launch traced here: 224 us
  Pallas kernels  108 us (48%)
  blocking collectives  31.6 us (14%)
  waiting for transfers between devices  28.9 us (13%)
  other arithmetic  14.9 us (7%)
  between operations  14.5 us (6%)
  matrix products  12.1 us (5%)
  starting transfers between devices  11.2 us (5%)
  local copies, waits for them, and re-layouts  2.89 us (1%)
    pallas_call x1, Pallas kernels, beam_power(): pl.pallas_call(beam_kernel, out_shape=jax.ShapeDtypeStruct((CX * CY, CZ),...  90 us
    all_gather x1, blocking collectives, per_device(): lax.all_gather(slowness, 'sta', axis=2, tiled=True)[0]  31.6 us
    all_gather x1, waiting for transfers between devices, per_device(): lax.all_gather(aligned, 'sta', axis=2, tiled=True)  23.5 us
    pallas_call x1, Pallas kernels, sum_over_sta(): pl.pallas_call(sum_kernel, out_shape=jax.ShapeDtypeStruct(part.shape, jnp...  17.9 us
    another operation x1, other arithmetic  8.39 us
    ppermute x2, starting transfers between devices, deblur(): lax.ppermute(stacked, 'grid', [(i, i + k) for i in range(tiles - k)])  7.79 us
    ppermute x2, waiting for transfers between devices, deblur(): lax.ppermute(stacked, 'grid', [(i + k, i) for i in range(tiles - k)])  5.39 us
    dot_general x8, matrix products, blur_narrowing(): jnp.einsum('jq,xqz->xjz', square_y, along_x, precision=lax.Precision.HIGH...  4.7 us
  transfers between devices with their start and end apart: 5, of which 3 were waited for; matrix products, arithmetic and copies ran while one was open for 1% of the time, Pallas kernels for 0%

profile of v3, /device:TPU:1, one launch (start us, length us, event | category | flops | bytes accessed | tf_op | source)
XLA Modules:
  0.0 224.0 jit_solution(11549888628466982071)
XLA Ops:
  7.2 0.0 copy-start
  7.2 0.0 copy-start.1
  7.2 0.0 all-gather.2.cloned.1.call-start
  7.2 0.9 copy_convert_fusion
  8.2 0.7 reduce
  8.9 8.4 %add_convert_fusion = (bf16[64,1,768]{2,1,0:T(2,128)(2,1)S(1)}, bf16[64,1,768]{2,1,0:T(2,128)(2,1)S(1)}) fusion(f32[64,1,768]{2,0,1:T(8,128)S(1)} %copy_convert_fusion, bf16[64,2,768]{2,1,0:T(2,128)(2,1)} %param.4, s32[768]{0:T(1024)S(1)} %reduce, s32[64]{0:T(128)S(1)} %iota_add_fusion), kind=kLoop, calls=%fused_computation.70 | loop fusion | flops 884736 | bytes 494848 | tf_op jit(solution)/shard_map/convert
  17.3 1.1 pad_maximum_fusion
  18.4 0.0 all-gather.2.cloned.1.call-update
  18.4 0.0 copy-done
  18.5 31.6 %all_gather.7 = bf16[1,3,6144]{2,1,0:T(4,128)(2,1)} all-gather(bf16[1,3,768]{2,1,0:T(4,128)(2,1)S(1)} %copy-done), channel_id=1, replica_groups=mesh['grid'=16,'sta'=8] {'sta'}, dimensions={2}, use_global_device_ids=true | all-gather | bytes 41472 | tf_op jit(solution)/shard_map/all_gather | solution.py:296
  50.1 0.5 convert_multiply_fusion.omega_ref
  50.7 0.0 copy-done.1
  50.7 0.1 select_reduce_fusion.8
  50.8 0.1 select_reduce_fusion.7
  51.0 0.1 select_reduce_fusion.6
  51.1 0.2 select_reduce_fusion.5
  51.3 0.2 select_reduce_fusion.4
  51.4 0.2 select_reduce_fusion.3
  51.6 0.3 select_reduce_fusion.2
  51.9 0.4 select_reduce_fusion
  52.3 23.5 %all-gather.2.cloned.1.call-done = bf16[64,2,6144]{2,1,0:T(2,128)(2,1)} async-done(((bf16[64,2,768]{2,1,0:T(2,128)(2,1)}), bf16[64,2,6144]{2,1,0:T(2,128)(2,1)}) %all-gather.2.cloned.1.call-update) | async-done | bytes 1572880 | tf_op jit(solution)/shard_map/all_gather | solution.py:293
  75.8 1.7 constant_dynamic-slice_fusion.aligned_ref
  77.5 90.0 %shard_map.62.part_ref = f32[256,128]{1,0:T(8,128)} custom-call(f32[8]{0:T(128)} %convert_multiply_fusion.omega_ref, bf16[8,2,6144]{2,1,0:T(2,128)(2,1)} %constant_dynamic-slice_fusion.aligned_ref, bf16[3,6144]{1,0:T(4,128)(2,1)} %bitcast.95), custom_call_target="tpu_custom_call" | custom-call | tf_op jit(solution)/shard_map/pallas_call | solution.py:149
  167.5 17.9 %shard_map.63 = f32[256,128]{1,0:T(8,128)} custom-call(f32[256,128]{1,0:T(8,128)} %shard_map.62.part_ref), custom_call_target="tpu_custom_call" | custom-call | tf_op jit(solution)/shard_map/pallas_call | solution.py:210
  185.4 1.6 fusion.49
  187.0 3.1 %collective-permute-start = (f32[32,8,128]{2,0,1:T(8,128)S(1)}, f32[32,8,128]{2,0,1:T(8,128)S(1)}, u32[]{:S(2)}, u32[]{:S(2)}) collective-permute-start(f32[32,8,128]{2,0,1:T(8,128)S(1)} %copy.54), channel_id=1, source_target_pairs={{0,16},{8,24},{16,32},{24,40},{32,48},{40,56},{48,64},{56,72},{64,... | collective-permute-start | bytes 393224 | tf_op jit(solution)/shard_map/ppermute | solution.py:258
  190.1 0.1 select_reduce_fusion.9
  190.2 4.7 %collective-permute-start.1 = (f32[32,8,128]{2,0,1:T(8,128)S(1)}, f32[32,8,128]{2,0,1:T(8,128)S(1)}, u32[]{:S(2)}, u32[]{:S(2)}) collective-permute-start(f32[32,8,128]{2,0,1:T(8,128)S(1)} %copy.54), channel_id=1, source_target_pairs={{0,8},{8,16},{16,24},{24,32},{32,40},{40,48},{48,56},{56,64},{64,7... | collective-permute-start | bytes 393224 | tf_op jit(solution)/shard_map/ppermute | solution.py:258
  194.9 0.1 slice.70
  195.0 0.1 slice.77
  195.1 0.1 slice.80
  195.1 0.1 slice.83
  195.2 1.9 collective-permute-start.2
  197.1 1.5 collective-permute-start.3
  198.6 0.0 collective-permute-done
  198.6 0.0 collective-permute-done.1
  198.7 2.8 %collective-permute-done.2 = f32[32,8,128]{2,0,1:T(8,128)S(1)} collective-permute-done((f32[32,8,128]{2,0,1:T(8,128)S(1)}, f32[32,8,128]{2,0,1:T(8,128)S(1)}, u32[]{:S(2)}, u32[]{:S(2)}) %collective-permute-start.2) | collective-permute-done | bytes 131104 | tf_op jit(solution)/shard_map/ppermute | solution.py:262
  201.5 2.6 %collective-permute-done.3 = f32[32,8,128]{2,0,1:T(8,128)S(1)} collective-permute-done((f32[32,8,128]{2,0,1:T(8,128)S(1)}, f32[32,8,128]{2,0,1:T(8,128)S(1)}, u32[]{:S(2)}, u32[]{:S(2)}) %collective-permute-start.3) | collective-permute-done | bytes 131104 | tf_op jit(solution)/shard_map/ppermute | solution.py:262
  204.1 0.6 fusion.45
  204.8 0.8 convolution_bitcast_fusion
  205.6 0.6 fusion.4
  206.2 0.7 fusion.2
  206.9 0.9 convolution_bitcast_fusion.1
  207.8 0.6 slice_multiply_fusion
  208.4 0.5 fusion.52
  208.9 0.6 convolution_bitcast_fusion.2
  209.6 0.5 fusion.15
  210.1 0.6 fusion.13
  210.6 0.7 convolution_bitcast_fusion.3
  211.3 0.5 slice_multiply_fusion.1
  211.8 0.4 fusion.55
  212.2 0.5 convolution_bitcast_fusion.4
  212.7 0.4 fusion.26
  213.2 0.5 fusion.24
  213.6 0.5 convolution_bitcast_fusion.5
  214.1 0.4 convolution_multiply_fusion
  214.5 0.3 fusion.58
  214.8 0.4 convolution_bitcast_fusion.6
  215.2 0.3 fusion.37
  215.5 0.2 fusion.60
  215.8 0.3 convolution_bitcast_fusion.7
  216.1 0.3 fusion
  216.4 0.7 copy.77
  (18 shorter events, 0.2 us)
Async XLA Ops:
  7.2 11.3 %copy-start = (bf16[1,3,768]{2,1,0:T(4,128)(2,1)S(1)}, bf16[1,3,768]{2,1,0:T(4,128)(2,1)}, u32[]{:S(2)}) copy-start(bf16[1,3,768]{2,1,0:T(4,128)(2,1)} %param.6) | copy-start | bytes 13828
  7.2 43.5 %copy-start.1 = (f32[3,17]{1,0:T(4,128)S(1)}, f32[3,17]{1,0:T(4,128)}, u32[]{:S(2)}) copy-start(f32[3,17]{1,0:T(4,128)} %param.7) | copy-start | bytes 616
  7.2 68.6 %all-gather.2.cloned.1.call-start = ((), (), s32[]{:S(2)}) async-start(), calls=%async_computation | async-start | bytes 1769472 | tf_op jit(solution)/shard_map/all_gather | solution.py:293
  187.0 11.6 %collective-permute-start = (f32[32,8,128]{2,0,1:T(8,128)S(1)}, f32[32,8,128]{2,0,1:T(8,128)S(1)}, u32[]{:S(2)}, u32[]{:S(2)}) collective-permute-start(f32[32,8,128]{2,0,1:T(8,128)S(1)} %copy.54), channel_id=1, source_target_pairs={{0,16},{8,24},{16,32},{24,40},{32,48},{40,56},{48,64},{56,72},{64,... | collective-permute-start | bytes 393224 | tf_op jit(solution)/shard_map/ppermute | solution.py:258
  190.2 8.4 %collective-permute-start.1 = (f32[32,8,128]{2,0,1:T(8,128)S(1)}, f32[32,8,128]{2,0,1:T(8,128)S(1)}, u32[]{:S(2)}, u32[]{:S(2)}) collective-permute-start(f32[32,8,128]{2,0,1:T(8,128)S(1)} %copy.54), channel_id=1, source_target_pairs={{0,8},{8,16},{16,24},{24,32},{32,40},{40,48},{48,56},{56,64},{64,7... | collective-permute-start | bytes 393224 | tf_op jit(solution)/shard_map/ppermute | solution.py:258
  195.2 6.3 %collective-permute-start.2 = (f32[32,8,128]{2,0,1:T(8,128)S(1)}, f32[32,8,128]{2,0,1:T(8,128)S(1)}, u32[]{:S(2)}, u32[]{:S(2)}) collective-permute-start(f32[32,8,128]{2,0,1:T(8,128)S(1)} %copy.54), channel_id=1, source_target_pairs={{8,0},{16,8},{24,16},{32,24},{40,32},{48,40},{56,48},{64,56},{72,6... | collective-permute-start | bytes 393224 | tf_op jit(solution)/shard_map/ppermute | solution.py:262
  197.1 7.0 %collective-permute-start.3 = (f32[32,8,128]{2,0,1:T(8,128)S(1)}, f32[32,8,128]{2,0,1:T(8,128)S(1)}, u32[]{:S(2)}, u32[]{:S(2)}) collective-permute-start(f32[32,8,128]{2,0,1:T(8,128)S(1)} %copy.54), channel_id=1, source_target_pairs={{16,0},{24,8},{32,16},{40,24},{48,32},{56,40},{64,48},{72,56},{80,... | collective-permute-start | bytes 393224 | tf_op jit(solution)/shard_map/ppermute | solution.py:262
Sparse Core Ops, SparseCore 0:
  18.6 57.1 all-gather.1

commit v4 on v3

--- a/solution.py
+++ b/solution.py
@@ -81,24 +81,99 @@
     return jnp.cos(angle), -jnp.sin(angle)
 
 
-def beam_kernel(omega_ref, aligned_ref, slow_ref, power_ref, acc_ref, left_ref, right_ref):
-    bins, stations = aligned_ref.shape[0], aligned_ref.shape[2]
+def exchange_inputs(spec_ref, lag_ref, slow_ref, spec_in, lag_in, slow_in, local_sem, send_sem, recv_sem):
+    count = spec_in.shape[0]
+    me = lax.axis_index("sta")
+    tile = lax.axis_index("grid")
+    mesh_ids = pl.DeviceIdType.MESH
+    barrier = pltpu.get_barrier_semaphore()
+    for shift in range(1, count):
+        peer = lax.rem(me + shift, count)
+        pl.semaphore_signal(barrier, inc=1, device_id=(tile, peer), device_id_type=mesh_ids)
+    pl.semaphore_wait(barrier, count - 1)
+    pairs = ((spec_ref, spec_in), (lag_ref, lag_in), (slow_ref, slow_in))
+    local = []
+    for kind, (source, target) in enumerate(pairs):
+        own = source.at[me] if kind == 0 else source
+        copy = pltpu.make_async_copy(own, target.at[me], local_sem.at[kind])
+        copy.start()
+        local.append(copy)
+    sends = []
+    for shift in range(1, count):
+        peer = lax.rem(me + shift, count)
+        for kind, (source, target) in enumerate(pairs):
+            part = source.at[peer] if kind == 0 else source
+            copy = pltpu.make_async_remote_copy(
+                src_ref=part,
+                dst_ref=target.at[me],
+                send_sem=send_sem.at[kind, shift],
+                recv_sem=recv_sem.at[kind, me],
+                device_id=(tile, peer),
+                device_id_type=mesh_ids,
+            )
+            copy.start()
+            sends.append(copy)
+    for copy in local:
+        copy.wait()
+    for copy in sends:
+        copy.wait_send()
+    for shift in range(1, count):
+        source_id = lax.rem(me + count - shift, count)
+        for kind, (source, target) in enumerate(pairs):
+            part = source.at[source_id] if kind == 0 else source
+            pltpu.make_async_remote_copy(
+                src_ref=part,
+                dst_ref=target.at[source_id],
+                send_sem=send_sem.at[kind, shift],
+                recv_sem=recv_sem.at[kind, source_id],
+                device_id=(tile, source_id),
+                device_id_type=mesh_ids,
+            ).wait_recv()
+
+
+def align_inputs(spec_in, lag_in, slow_in, real_ref, imag_ref, turn_ref):
+    count, bins, block = spec_in.shape[0], spec_in.shape[2], spec_in.shape[3]
+    first_bin = lax.axis_index("sta") * bins
+    bin_rows = (F0 + first_bin + lax.broadcasted_iota(jnp.int32, (bins, block), 0)).astype(jnp.float32)
+    for source in range(count):
+        cols = slice(source * block, (source + 1) * block)
+        product = bin_rows * lag_in[source].astype(jnp.float32)
+        whole = jnp.floor(product * (1.0 / NT))
+        left = product - whole * NT
+        left = jnp.where(left < 0.0, left + NT, left)
+        left = jnp.where(left >= NT, left - NT, left)
+        turned = left * (TWO_PI / NT)
+        cosine = jnp.cos(turned)
+        sine = jnp.sin(turned)
+        real_in = spec_in[source, 0].astype(jnp.float32)
+        imag_in = spec_in[source, 1].astype(jnp.float32)
+        real_ref[:, cols] = (real_in * cosine + imag_in * sine).astype(jnp.bfloat16).astype(jnp.float32)
+        imag_ref[:, cols] = (imag_in * cosine - real_in * sine).astype(jnp.bfloat16).astype(jnp.float32)
+        turn_ref[:, cols] = slow_in[source].astype(jnp.float32)
+
+
+def beam_kernel(spec_ref, lag_ref, slow_ref, power_ref, spec_in, lag_in, slow_in, local_sem, send_sem, recv_sem,
+                real_ref, imag_ref, turn_ref, acc_ref, left_ref, right_ref):
+    exchange_inputs(spec_ref, lag_ref, slow_ref, spec_in, lag_in, slow_in, local_sem, send_sem, recv_sem)
+    align_inputs(spec_in, lag_in, slow_in, real_ref, imag_ref, turn_ref)
+    bins, stations = real_ref.shape
+    first_bin = lax.axis_index("sta") * bins
     width = CHUNK
     rows8 = lax.broadcasted_iota(jnp.int32, (8, width), 0).astype(jnp.float32)
     rows16 = lax.broadcasted_iota(jnp.int32, (16, width), 0).astype(jnp.float32)
     power_ref[...] = jnp.zeros_like(power_ref)
 
     def per_bin(f, carry):
-        omega = omega_ref[f]
+        omega = (F0 + first_bin + f).astype(jnp.float32) * (TWO_PI / NT)
         acc_ref[...] = jnp.zeros_like(acc_ref)
 
         def per_chunk(k, inner):
             cols = pl.ds(pl.multiple_of(k * width, width), width)
-            turn_x = omega * slow_ref[0:1, cols].astype(jnp.float32)
-            turn_y = omega * slow_ref[1:2, cols].astype(jnp.float32)
-            turn_z = omega * slow_ref[2:3, cols].astype(jnp.float32)
-            real_in = aligned_ref[f, 0:1, cols].astype(jnp.float32)
-            imag_in = aligned_ref[f, 1:2, cols].astype(jnp.float32)
+            turn_x = omega * turn_ref[0:1, cols]
+            turn_y = omega * turn_ref[1:2, cols]
+            turn_z = omega * turn_ref[2:3, cols]
+            real_in = real_ref[pl.ds(f, 1), cols]
+            imag_in = imag_ref[pl.ds(f, 1), cols]
             a_r, a_i = exp_neg(turn_x * (rows8 - 3.5))
             b_r, b_i = exp_neg(turn_x * (8.0 * (rows8 - 1.5)))
             y_r, y_i = exp_neg(turn_y * (rows8 - 3.5))
@@ -144,23 +219,33 @@
     lax.fori_loop(0, bins, per_bin, 0)
 
 
-def beam_power(omegas, aligned_rows, slow_rows):
+def beam_power(spec_send, lag_row, slow_rows):
+    count = spec_send.shape[0]
+    bins, block = spec_send.shape[2], spec_send.shape[3]
     width = CHUNK
+    stations = count * block
+    vmem = pl.BlockSpec(memory_space=pltpu.VMEM)
     return pl.pallas_call(
         beam_kernel,
         out_shape=jax.ShapeDtypeStruct((CX * CY, CZ), jnp.float32),
-        in_specs=[
-            pl.BlockSpec(memory_space=pltpu.SMEM),
-            pl.BlockSpec(memory_space=pltpu.VMEM),
-            pl.BlockSpec(memory_space=pltpu.VMEM),
-        ],
-        out_specs=pl.BlockSpec(memory_space=pltpu.VMEM),
+        in_specs=[vmem, vmem, vmem],
+        out_specs=vmem,
         scratch_shapes=[
+            pltpu.VMEM((count,) + spec_send.shape[1:], jnp.bfloat16),
+            pltpu.VMEM((count,) + lag_row.shape, jnp.int32),
+            pltpu.VMEM((count,) + slow_rows.shape, jnp.bfloat16),
+            pltpu.SemaphoreType.DMA((3,)),
+            pltpu.SemaphoreType.DMA((3, count)),
+            pltpu.SemaphoreType.DMA((3, count)),
+            pltpu.VMEM((bins, stations), jnp.float32),
+            pltpu.VMEM((bins, stations), jnp.float32),
+            pltpu.VMEM((slow_rows.shape[0], stations), jnp.float32),
             pltpu.VMEM((CX * CY, 2 * CZ), jnp.float32),
             pltpu.VMEM((CX * CY, 2 * width), jnp.bfloat16),
             pltpu.VMEM((2 * CZ, 2 * width), jnp.bfloat16),
         ],
-    )(omegas, aligned_rows, slow_rows)
+        compiler_params=pltpu.CompilerParams(collective_id=1, has_side_effects=True),
+    )(spec_send, lag_row, slow_rows)
 
 
 def sum_kernel(part_ref, out_ref, recv_ref, local_sem, send_sem, recv_sem):
@@ -287,13 +372,9 @@
     groups = lax.axis_size("sta")
     own_count = FREQS // groups
     first_bin = lax.axis_index("sta") * own_count
-    aligned = align_rows(spectra, lag_samples[0])
-    own_ids = first_bin + jnp.arange(own_count, dtype=jnp.int32)
-    rows = lax.dynamic_slice_in_dim(
-        lax.all_gather(aligned, "sta", axis=2, tiled=True), first_bin, own_count, 0
-    )
-    omegas = (F0 + own_ids).astype(jnp.float32) * (TWO_PI / NT)
-    local_power = beam_power(omegas, rows, lax.all_gather(slowness, "sta", axis=2, tiled=True)[0])
+    block = spectra.shape[2]
+    spec_send = spectra.reshape(groups, own_count, 2, block).transpose(0, 2, 1, 3)
+    local_power = beam_power(spec_send, lag_samples, slowness[0])
     summed = sum_over_sta(local_power)
     stacked = (summed / (FREQS * STATIONS) + BACKGROUND).reshape(CX, CY, CZ)
     estimate = deblur(stacked, spread_taps)

time: 225 us -> 156 us (0.69)
  blocking collectives: 31.6 us -> 0 us
  waiting for transfers between devices: 28.9 us -> 3.29 us
  Pallas kernels: 108 us -> 122 us
  between operations: 14.5 us -> 1.07 us
  other arithmetic: 14.9 us -> 3.23 us
    all_gather x1 -> x0, blocking collectives: 31.6 us -> none  [per_device(): lax.all_gather(slowness, 'sta', axis=2, tiled=True)[0]]
    all_gather x1 -> x0, waiting for transfers between devices: 23.5 us -> none  [per_device(): lax.all_gather(aligned, 'sta', axis=2, tiled=True)]
    pallas_call x1, Pallas kernels: 90 us -> 103 us  [beam_power(): pl.pallas_call(beam_kernel, out_shape=jax.ShapeDtypeStruct((CX * CY, CZ),...]
    another operation x2 -> x0, other arithmetic: 9.51 us -> none
  transfers between devices with their start and end apart: 5 -> 4, of which waited for: 3 -> 2; matrix products, arithmetic and copies ran while one was open for 1% -> 1% of each run, Pallas kernels for 0% -> 0%
where the time goes in v4:
time: 156 us; the launch traced here: 155 us
  Pallas kernels  122 us (78%)
  matrix products  12 us (8%)
  starting transfers between devices  11.3 us (7%)
  waiting for transfers between devices  3.29 us (2%)
  other arithmetic  3.23 us (2%)
  local copies, waits for them, and re-layouts  2.78 us (2%)
    pallas_call x1, Pallas kernels, beam_power(): pl.pallas_call(beam_kernel, out_shape=jax.ShapeDtypeStruct((CX * CY, CZ),...  103 us
    pallas_call x1, Pallas kernels, sum_over_sta(): pl.pallas_call(sum_kernel, out_shape=jax.ShapeDtypeStruct(part.shape, jnp...  19 us
    ppermute x2, starting transfers between devices, deblur(): lax.ppermute(stacked, 'grid', [(i, i + k) for i in range(tiles - k)])  7.89 us
    dot_general x8, matrix products, blur_narrowing(): jnp.einsum('jq,xqz->xjz', square_y, along_x, precision=lax.Precision.HIGH...  4.69 us
    dot_general x8, matrix products, blur_narrowing(): jnp.einsum('ip,pyz->iyz', band_x, volume, precision=lax.Precision.HIGHEST)  3.85 us
    dot_general x8, matrix products, blur_narrowing(): jnp.einsum('xyw,kw->xyk', along_y, square_z, precision=lax.Precision.HIGH...  3.51 us
    ppermute x2, starting transfers between devices, deblur(): lax.ppermute(stacked, 'grid', [(i + k, i) for i in range(tiles - k)])  3.39 us
    ppermute x2, waiting for transfers between devices, deblur(): lax.ppermute(stacked, 'grid', [(i + k, i) for i in range(tiles - k)])  3.29 us
  transfers between devices with their start and end apart: 4, of which 2 were waited for; matrix products, arithmetic and copies ran while one was open for 1% of the time, Pallas kernels for 0%

profile of v4, /device:TPU:1, one launch (start us, length us, event | category | flops | bytes accessed | tf_op | source)
XLA Modules:
  0.0 155.4 jit_solution(5978168758653110915)
XLA Ops:
  0.6 1.6 %copy.112 = bf16[8,8,2,768]{3,1,2,0:T(8,128)(2,1)} copy(bf16[8,8,2,768]{3,2,1,0:T(2,128)(2,1)} %bitcast.98) | data formatting | bytes 393216 | tf_op jit(solution)/shard_map/reshape | solution.py:376
  2.2 102.8 %shard_map.59.part_ref = f32[256,128]{1,0:T(8,128)} custom-call(bf16[8,2,8,768]{3,2,1,0:T(8,128)(2,1)} %bitcast.97, s32[1,768]{1,0:T(1,128)} %lag_ref.1, bf16[3,768]{1,0:T(4,128)(2,1)} %bitcast.99), custom_call_target="tpu_custom_call" | custom-call | tf_op jit(solution)/shard_map/pallas_call | solution.py:228
  105.0 0.0 copy-start
  105.0 19.0 %shard_map.60 = f32[256,128]{1,0:T(8,128)} custom-call(f32[256,128]{1,0:T(8,128)} %shard_map.59.part_ref), custom_call_target="tpu_custom_call" | custom-call | tf_op jit(solution)/shard_map/pallas_call | solution.py:295
  124.0 1.6 %fusion.47 = (f32[32,8,128]{2,1,0:T(8,128)S(1)}, f32[1,32,8,128]{3,2,1,0:T(8,128)}) fusion(f32[256,128]{1,0:T(8,128)} %shard_map.60), kind=kLoop, calls=%fused_computation.74 | loop fusion | flops 65536 | bytes 393216 | tf_op jit(solution)/shard_map/reshape | solution.py:379
  125.6 4.7 %collective-permute-start.1 = (f32[32,8,128]{2,0,1:T(8,128)S(1)}, f32[32,8,128]{2,0,1:T(8,128)S(1)}, u32[]{:S(2)}, u32[]{:S(2)}) collective-permute-start(f32[32,8,128]{2,0,1:T(8,128)S(1)} %copy.30), channel_id=1, source_target_pairs={{0,8},{8,16},{16,24},{24,32},{32,40},{40,48},{48,56},{56,64},{64,7... | collective-permute-start | bytes 393224 | tf_op jit(solution)/shard_map/ppermute | solution.py:343
  130.3 3.2 %collective-permute-start = (f32[32,8,128]{2,0,1:T(8,128)S(1)}, f32[32,8,128]{2,0,1:T(8,128)S(1)}, u32[]{:S(2)}, u32[]{:S(2)}) collective-permute-start(f32[32,8,128]{2,0,1:T(8,128)S(1)} %copy.30), channel_id=1, source_target_pairs={{0,16},{8,24},{16,32},{24,40},{32,48},{40,56},{48,64},{56,72},{64,... | collective-permute-start | bytes 393224 | tf_op jit(solution)/shard_map/ppermute | solution.py:343
  133.5 1.9 %collective-permute-start.2 = (f32[32,8,128]{2,0,1:T(8,128)S(1)}, f32[32,8,128]{2,0,1:T(8,128)S(1)}, u32[]{:S(2)}, u32[]{:S(2)}) collective-permute-start(f32[32,8,128]{2,0,1:T(8,128)S(1)} %copy.30), channel_id=1, source_target_pairs={{8,0},{16,8},{24,16},{32,24},{40,32},{48,40},{56,48},{64,56},{72,6... | collective-permute-start | bytes 393224 | tf_op jit(solution)/shard_map/ppermute | solution.py:347
  135.4 1.5 collective-permute-start.3
  137.1 0.0 copy-done
  137.1 0.4 select_reduce_fusion
  137.4 0.2 select_reduce_fusion.3
  137.6 0.2 select_reduce_fusion.4
  137.8 0.2 select_reduce_fusion.5
  137.9 0.1 select_reduce_fusion.6
  138.1 0.1 select_reduce_fusion.7
  138.2 0.1 select_reduce_fusion.8
  138.3 0.3 select_reduce_fusion.2
  138.6 0.1 select_reduce_fusion.9
  138.7 0.1 slice.62
  138.8 0.1 slice.69
  138.9 0.1 slice.72
  139.0 0.1 slice.75
  139.0 0.0 collective-permute-done
  139.0 0.0 collective-permute-done.1
  139.1 0.7 collective-permute-done.2
  139.8 2.6 %collective-permute-done.3 = f32[32,8,128]{2,0,1:T(8,128)S(1)} collective-permute-done((f32[32,8,128]{2,0,1:T(8,128)S(1)}, f32[32,8,128]{2,0,1:T(8,128)S(1)}, u32[]{:S(2)}, u32[]{:S(2)}) %collective-permute-start.3) | collective-permute-done | bytes 131104 | tf_op jit(solution)/shard_map/ppermute | solution.py:347
  142.4 0.6 fusion.43
  143.1 0.8 convolution_bitcast_fusion
  143.9 0.6 fusion.4
  144.5 0.7 fusion.2
  145.2 0.9 convolution_bitcast_fusion.1
  146.1 0.6 slice_multiply_fusion
  146.7 0.5 fusion.50
  147.2 0.6 convolution_bitcast_fusion.2
  147.9 0.5 fusion.15
  148.4 0.6 fusion.13
  148.9 0.7 convolution_bitcast_fusion.3
  149.6 0.5 slice_multiply_fusion.1
  150.1 0.4 fusion.53
  150.5 0.5 convolution_bitcast_fusion.4
  151.1 0.4 fusion.26
  151.5 0.4 fusion.24
  151.9 0.5 convolution_bitcast_fusion.5
  152.4 0.4 convolution_multiply_fusion
  152.8 0.3 fusion.56
  153.1 0.4 convolution_bitcast_fusion.6
  153.5 0.3 fusion.35
  153.8 0.2 fusion.58
  154.1 0.3 convolution_bitcast_fusion.7
  154.4 0.3 fusion
  154.7 0.7 copy.53
  (17 shorter events, 0.2 us)
Async XLA Ops:
  105.0 32.1 %copy-start = (f32[3,17]{1,0:T(4,128)S(1)}, f32[3,17]{1,0:T(4,128)}, u32[]{:S(2)}) copy-start(f32[3,17]{1,0:T(4,128)} %param.7) | copy-start | bytes 616
  125.6 13.4 %collective-permute-start.1 = (f32[32,8,128]{2,0,1:T(8,128)S(1)}, f32[32,8,128]{2,0,1:T(8,128)S(1)}, u32[]{:S(2)}, u32[]{:S(2)}) collective-permute-start(f32[32,8,128]{2,0,1:T(8,128)S(1)} %copy.30), channel_id=1, source_target_pairs={{0,8},{8,16},{16,24},{24,32},{32,40},{40,48},{48,56},{56,64},{64,7... | collective-permute-start | bytes 393224 | tf_op jit(solution)/shard_map/ppermute | solution.py:343
  130.3 8.7 %collective-permute-start = (f32[32,8,128]{2,0,1:T(8,128)S(1)}, f32[32,8,128]{2,0,1:T(8,128)S(1)}, u32[]{:S(2)}, u32[]{:S(2)}) collective-permute-start(f32[32,8,128]{2,0,1:T(8,128)S(1)} %copy.30), channel_id=1, source_target_pairs={{0,16},{8,24},{16,32},{24,40},{32,48},{40,56},{48,64},{56,72},{64,... | collective-permute-start | bytes 393224 | tf_op jit(solution)/shard_map/ppermute | solution.py:343
  133.5 6.3 %collective-permute-start.2 = (f32[32,8,128]{2,0,1:T(8,128)S(1)}, f32[32,8,128]{2,0,1:T(8,128)S(1)}, u32[]{:S(2)}, u32[]{:S(2)}) collective-permute-start(f32[32,8,128]{2,0,1:T(8,128)S(1)} %copy.30), channel_id=1, source_target_pairs={{8,0},{16,8},{24,16},{32,24},{40,32},{48,40},{56,48},{64,56},{72,6... | collective-permute-start | bytes 393224 | tf_op jit(solution)/shard_map/ppermute | solution.py:347
  135.4 7.0 %collective-permute-start.3 = (f32[32,8,128]{2,0,1:T(8,128)S(1)}, f32[32,8,128]{2,0,1:T(8,128)S(1)}, u32[]{:S(2)}, u32[]{:S(2)}) collective-permute-start(f32[32,8,128]{2,0,1:T(8,128)S(1)} %copy.30), channel_id=1, source_target_pairs={{16,0},{24,8},{32,16},{40,24},{48,32},{56,40},{64,48},{72,56},{80,... | collective-permute-start | bytes 393224 | tf_op jit(solution)/shard_map/ppermute | solution.py:347

commit v5 on v4

--- a/solution.py
+++ b/solution.py
@@ -152,6 +152,20 @@
         turn_ref[:, cols] = slow_in[source].astype(jnp.float32)
 
 
+def complex_times(left, right):
+    return left[0] * right[0] - left[1] * right[1], left[0] * right[1] + left[1] * right[0]
+
+
+def factor_rows(turn_x, turn_y, turn_z, rows8, rows16):
+    return (
+        exp_neg(turn_x * (rows8 - 3.5)),
+        exp_neg(turn_x * (8.0 * (rows8 - 1.5))),
+        exp_neg(turn_y * (rows8 - 3.5)),
+        exp_neg(turn_z * (rows16 - 7.5)),
+        exp_neg(turn_z * (16.0 * (rows8 - 3.5))),
+    )
+
+
 def beam_kernel(spec_ref, lag_ref, slow_ref, power_ref, spec_in, lag_in, slow_in, local_sem, send_sem, recv_sem,
                 real_ref, imag_ref, turn_ref, acc_ref, left_ref, right_ref):
     exchange_inputs(spec_ref, lag_ref, slow_ref, spec_in, lag_in, slow_in, local_sem, send_sem, recv_sem)
@@ -161,43 +175,39 @@
     width = CHUNK
     rows8 = lax.broadcasted_iota(jnp.int32, (8, width), 0).astype(jnp.float32)
     rows16 = lax.broadcasted_iota(jnp.int32, (16, width), 0).astype(jnp.float32)
-    power_ref[...] = jnp.zeros_like(power_ref)
-
-    def per_bin(f, carry):
-        omega = (F0 + first_bin + f).astype(jnp.float32) * (TWO_PI / NT)
-        acc_ref[...] = jnp.zeros_like(acc_ref)
-
-        def per_chunk(k, inner):
-            cols = pl.ds(pl.multiple_of(k * width, width), width)
-            turn_x = omega * turn_ref[0:1, cols]
-            turn_y = omega * turn_ref[1:2, cols]
-            turn_z = omega * turn_ref[2:3, cols]
+    omega0 = (F0 + first_bin).astype(jnp.float32) * (TWO_PI / NT)
+    step = TWO_PI / NT
+    acc_ref[...] = jnp.zeros_like(acc_ref)
+
+    def per_chunk(k, carry):
+        cols = pl.ds(pl.multiple_of(k * width, width), width)
+        slow_x = turn_ref[0:1, cols]
+        slow_y = turn_ref[1:2, cols]
+        slow_z = turn_ref[2:3, cols]
+        start = factor_rows(omega0 * slow_x, omega0 * slow_y, omega0 * slow_z, rows8, rows16)
+        ratio = factor_rows(step * slow_x, step * slow_y, step * slow_z, rows8, rows16)
+
+        def per_bin(f, state):
+            (a_r, a_i), (b_r, b_i), (y_r, y_i), (c_r, c_i), (d_r, d_i) = state
             real_in = real_ref[pl.ds(f, 1), cols]
             imag_in = imag_ref[pl.ds(f, 1), cols]
-            a_r, a_i = exp_neg(turn_x * (rows8 - 3.5))
-            b_r, b_i = exp_neg(turn_x * (8.0 * (rows8 - 1.5)))
-            y_r, y_i = exp_neg(turn_y * (rows8 - 3.5))
-            c_r, c_i = exp_neg(turn_z * (rows16 - 7.5))
-            d_r, d_i = exp_neg(turn_z * (16.0 * (rows8 - 3.5)))
+            groups_r, groups_i = [], []
             for m in range(CX // 8):
-                bm_r, bm_i = b_r[m : m + 1], b_i[m : m + 1]
-                x_r = bm_r * a_r - bm_i * a_i
-                x_i = bm_r * a_i + bm_i * a_r
-                p_r = real_in * x_r - imag_in * x_i
-                p_i = real_in * x_i + imag_in * x_r
-                for j in range(0, 8, 2):
+                x_r, x_i = complex_times((b_r[m : m + 1], b_i[m : m + 1]), (a_r, a_i))
+                groups_r.append(real_in * x_r - imag_in * x_i)
+                groups_i.append(real_in * x_i + imag_in * x_r)
+            for y in range(CY):
+                yy_r, yy_i = y_r[y : y + 1], y_i[y : y + 1]
+                for m in range(0, CX // 8, 2):
                     parts_r, parts_i = [], []
-                    for jj in (j, j + 1):
-                        px_r, px_i = p_r[jj : jj + 1], p_i[jj : jj + 1]
-                        parts_r.append(px_r * y_r - px_i * y_i)
-                        parts_i.append(px_r * y_i + px_i * y_r)
-                    row = (8 * m + j) * CY
+                    for mm in (m, m + 1):
+                        parts_r.append(groups_r[mm] * yy_r - groups_i[mm] * yy_i)
+                        parts_i.append(groups_r[mm] * yy_i + groups_i[mm] * yy_r)
+                    row = y * CX + 8 * m
                     left_ref[row : row + 16, 0:width] = jnp.concatenate(parts_r, axis=0).astype(jnp.bfloat16)
                     left_ref[row : row + 16, width : 2 * width] = jnp.concatenate(parts_i, axis=0).astype(jnp.bfloat16)
             for m in range(CZ // 16):
-                dm_r, dm_i = d_r[m : m + 1], d_i[m : m + 1]
-                z_r = dm_r * c_r - dm_i * c_i
-                z_i = dm_r * c_i + dm_i * c_r
+                z_r, z_i = complex_times((d_r[m : m + 1], d_i[m : m + 1]), (c_r, c_i))
                 cos_z = z_r.astype(jnp.bfloat16)
                 sin_z = (-z_i).astype(jnp.bfloat16)
                 row = 16 * m
@@ -205,18 +215,21 @@
                 right_ref[row : row + 16, width : 2 * width] = sin_z
                 right_ref[CZ + row : CZ + row + 16, 0:width] = -sin_z
                 right_ref[CZ + row : CZ + row + 16, width : 2 * width] = cos_z
-            acc_ref[...] += lax.dot_general(
+            acc_ref[f] += lax.dot_general(
                 left_ref[...], right_ref[...], (((1,), (1,)), ((), ())), preferred_element_type=jnp.float32
             )
-            return inner
-
-        lax.fori_loop(0, stations // width, per_chunk, 0)
-        beams = acc_ref[...]
+            return tuple(complex_times(now, turn) for now, turn in zip(state, ratio))
+
+        lax.fori_loop(0, bins, per_bin, start)
+        return carry
+
+    lax.fori_loop(0, stations // width, per_chunk, 0)
+    total = jnp.zeros(power_ref.shape, jnp.float32)
+    for f in range(bins):
+        beams = acc_ref[f]
         squares = beams * beams
-        power_ref[...] += squares[:, :CZ] + squares[:, CZ:]
-        return carry
-
-    lax.fori_loop(0, bins, per_bin, 0)
+        total = total + squares[:, :CZ] + squares[:, CZ:]
+    power_ref[...] = total
 
 
 def beam_power(spec_send, lag_row, slow_rows):
@@ -240,7 +253,7 @@
             pltpu.VMEM((bins, stations), jnp.float32),
             pltpu.VMEM((bins, stations), jnp.float32),
             pltpu.VMEM((slow_rows.shape[0], stations), jnp.float32),
-            pltpu.VMEM((CX * CY, 2 * CZ), jnp.float32),
+            pltpu.VMEM((bins, CX * CY, 2 * CZ), jnp.float32),
             pltpu.VMEM((CX * CY, 2 * width), jnp.bfloat16),
             pltpu.VMEM((2 * CZ, 2 * width), jnp.bfloat16),
         ],
@@ -376,7 +389,7 @@
     spec_send = spectra.reshape(groups, own_count, 2, block).transpose(0, 2, 1, 3)
     local_power = beam_power(spec_send, lag_samples, slowness[0])
     summed = sum_over_sta(local_power)
-    stacked = (summed / (FREQS * STATIONS) + BACKGROUND).reshape(CX, CY, CZ)
+    stacked = (summed / (FREQS * STATIONS) + BACKGROUND).reshape(CY, CX, CZ).transpose(1, 0, 2)
     estimate = deblur(stacked, spread_taps)
     return (stacked[None], estimate[None])
 

time: 156 us -> 131 us (0.84)
  Pallas kernels: 122 us -> 97.6 us
    pallas_call x1, Pallas kernels: 103 us -> 78.7 us  [beam_power(): pl.pallas_call(beam_kernel, out_shape=jax.ShapeDtypeStruct((CX * CY, CZ),...]
    reshape x1 -> x0, other arithmetic: 1.58 us -> none  [per_device(): stacked = (summed / (FREQS * STATIONS) + BACKGROUND).reshape(CX, CY, CZ)]
  transfers between devices with their start and end apart: 4 -> 4, of which waited for: 2 -> 1; matrix products, arithmetic and copies ran while one was open for 1% -> 2% of each run, Pallas kernels for 0% -> 0%
where the time goes in v5:
time: 131 us
  Pallas kernels  97.6 us (75%)
  matrix products  12.1 us (9%)
  starting transfers between devices  11.3 us (9%)
  local copies, waits for them, and re-layouts  3.45 us (3%)
  other arithmetic  2.6 us (2%)
  waiting for transfers between devices  2.58 us (2%)
    pallas_call x1, Pallas kernels, beam_power(): pl.pallas_call(beam_kernel, out_shape=jax.ShapeDtypeStruct((CX * CY, CZ),...  78.7 us
    pallas_call x1, Pallas kernels, sum_over_sta(): pl.pallas_call(sum_kernel, out_shape=jax.ShapeDtypeStruct(part.shape, jnp...  19 us
    ppermute x2, starting transfers between devices, deblur(): lax.ppermute(stacked, 'grid', [(i, i + k) for i in range(tiles - k)])  7.89 us
    dot_general x8, matrix products, blur_narrowing(): jnp.einsum('jq,xqz->xjz', square_y, along_x, precision=lax.Precision.HIGH...  4.69 us
    dot_general x8, matrix products, blur_narrowing(): jnp.einsum('ip,pyz->iyz', band_x, volume, precision=lax.Precision.HIGHEST)  3.85 us
    dot_general x8, matrix products, blur_narrowing(): jnp.einsum('xyw,kw->xyk', along_y, square_z, precision=lax.Precision.HIGH...  3.52 us
    ppermute x2, starting transfers between devices, deblur(): lax.ppermute(stacked, 'grid', [(i + k, i) for i in range(tiles - k)])  3.39 us
  transfers between devices with their start and end apart: 4, of which 1 were waited for; matrix products, arithmetic and copies ran while one was open for 2% of the time, Pallas kernels for 0%

profile of v5, /device:TPU:1, one launch (start us, length us, event | category | flops | bytes accessed | tf_op | source)
XLA Modules:
  0.0 130.7 jit_solution(3612855840166897664)
XLA Ops:
  0.6 1.6 %copy.95 = bf16[8,8,2,768]{3,1,2,0:T(8,128)(2,1)} copy(bf16[8,8,2,768]{3,2,1,0:T(2,128)(2,1)} %bitcast.106) | data formatting | bytes 393216 | tf_op jit(solution)/shard_map/reshape | solution.py:389
  2.2 0.0 copy-start
  2.2 78.7 %shard_map.59.part_ref = f32[256,128]{1,0:T(8,128)} custom-call(bf16[8,2,8,768]{3,2,1,0:T(8,128)(2,1)} %bitcast.105, s32[1,768]{1,0:T(1,128)} %lag_ref.1, bf16[3,768]{1,0:T(4,128)(2,1)} %bitcast.107), custom_call_target="tpu_custom_call" | custom-call | tf_op jit(solution)/shard_map/pallas_call | solution.py:241
  80.9 19.0 %shard_map.60 = f32[256,128]{1,0:T(8,128)} custom-call(f32[256,128]{1,0:T(8,128)} %shard_map.59.part_ref), custom_call_target="tpu_custom_call" | custom-call | tf_op jit(solution)/shard_map/pallas_call | solution.py:308
  99.9 0.9 multiply_add_fusion
  100.8 4.7 %collective-permute-start.1 = (f32[32,8,128]{2,0,1:T(8,128)S(1)}, f32[32,8,128]{2,0,1:T(8,128)S(1)}, u32[]{:S(2)}, u32[]{:S(2)}) collective-permute-start(f32[32,8,128]{2,0,1:T(8,128)S(1)} %bitcast.98), channel_id=1, source_target_pairs={{0,8},{8,16},{16,24},{24,32},{32,40},{40,48},{48,56},{56,64},{64,7... | collective-permute-start | bytes 393224 | tf_op jit(solution)/shard_map/ppermute | solution.py:356
  105.5 3.2 %collective-permute-start = (f32[32,8,128]{2,0,1:T(8,128)S(1)}, f32[32,8,128]{2,0,1:T(8,128)S(1)}, u32[]{:S(2)}, u32[]{:S(2)}) collective-permute-start(f32[32,8,128]{2,0,1:T(8,128)S(1)} %bitcast.99), channel_id=1, source_target_pairs={{0,16},{8,24},{16,32},{24,40},{32,48},{40,56},{48,64},{56,72},{64,... | collective-permute-start | bytes 393224 | tf_op jit(solution)/shard_map/ppermute | solution.py:356
  108.7 1.9 %collective-permute-start.2 = (f32[32,8,128]{2,0,1:T(8,128)S(1)}, f32[32,8,128]{2,0,1:T(8,128)S(1)}, u32[]{:S(2)}, u32[]{:S(2)}) collective-permute-start(f32[32,8,128]{2,0,1:T(8,128)S(1)} %bitcast.100), channel_id=1, source_target_pairs={{8,0},{16,8},{24,16},{32,24},{40,32},{48,40},{56,48},{64,56},{72,6... | collective-permute-start | bytes 393224 | tf_op jit(solution)/shard_map/ppermute | solution.py:360
  110.7 1.5 %collective-permute-start.3 = (f32[32,8,128]{2,0,1:T(8,128)S(1)}, f32[32,8,128]{2,0,1:T(8,128)S(1)}, u32[]{:S(2)}, u32[]{:S(2)}) collective-permute-start(f32[32,8,128]{2,0,1:T(8,128)S(1)} %bitcast.101), channel_id=1, source_target_pairs={{16,0},{24,8},{32,16},{40,24},{48,32},{56,40},{64,48},{72,56},{80,... | collective-permute-start | bytes 393224 | tf_op jit(solution)/shard_map/ppermute | solution.py:360
  112.3 0.0 copy-done
  112.3 0.4 select_reduce_fusion
  112.6 0.2 select_reduce_fusion.3
  112.8 0.2 select_reduce_fusion.4
  113.0 0.2 select_reduce_fusion.5
  113.2 0.1 select_reduce_fusion.6
  113.3 0.1 select_reduce_fusion.7
  113.4 0.1 select_reduce_fusion.8
  113.5 0.3 select_reduce_fusion.2
  113.8 0.1 select_reduce_fusion.9
  113.9 0.1 slice.62
  114.0 0.1 slice.69
  114.1 0.1 slice.72
  114.2 0.1 slice.75
  114.2 0.7 copy.37
  115.0 0.0 collective-permute-done
  115.0 0.0 collective-permute-done.1
  115.0 0.0 collective-permute-done.2
  115.1 2.6 %collective-permute-done.3 = f32[32,8,128]{2,0,1:T(8,128)S(1)} collective-permute-done((f32[32,8,128]{2,0,1:T(8,128)S(1)}, f32[32,8,128]{2,0,1:T(8,128)S(1)}, u32[]{:S(2)}, u32[]{:S(2)}) %collective-permute-start.3) | collective-permute-done | bytes 131104 | tf_op jit(solution)/shard_map/ppermute | solution.py:360
  117.7 0.6 fusion.43
  118.3 0.8 convolution_bitcast_fusion
  119.1 0.6 fusion.4
  119.7 0.7 fusion.2
  120.5 0.9 convolution_bitcast_fusion.1
  121.3 0.6 slice_multiply_fusion
  121.9 0.5 fusion.48
  122.4 0.6 convolution_bitcast_fusion.2
  123.1 0.5 fusion.15
  123.6 0.6 fusion.13
  124.2 0.7 convolution_bitcast_fusion.3
  124.9 0.5 slice_multiply_fusion.1
  125.3 0.4 fusion.51
  125.8 0.5 convolution_bitcast_fusion.4
  126.3 0.4 fusion.26
  126.7 0.4 fusion.24
  127.2 0.5 convolution_bitcast_fusion.5
  127.7 0.4 convolution_multiply_fusion
  128.1 0.3 fusion.54
  128.4 0.4 convolution_bitcast_fusion.6
  128.8 0.3 fusion.35
  129.1 0.2 fusion.56
  129.3 0.3 convolution_bitcast_fusion.7
  129.7 0.3 fusion
  129.9 0.7 copy.38
  (17 shorter events, 0.2 us)
Async XLA Ops:
  2.2 110.0 %copy-start = (f32[3,17]{1,0:T(4,128)S(1)}, f32[3,17]{1,0:T(4,128)}, u32[]{:S(2)}) copy-start(f32[3,17]{1,0:T(4,128)} %param.7) | copy-start | bytes 616
  100.8 14.2 %collective-permute-start.1 = (f32[32,8,128]{2,0,1:T(8,128)S(1)}, f32[32,8,128]{2,0,1:T(8,128)S(1)}, u32[]{:S(2)}, u32[]{:S(2)}) collective-permute-start(f32[32,8,128]{2,0,1:T(8,128)S(1)} %bitcast.98), channel_id=1, source_target_pairs={{0,8},{8,16},{16,24},{24,32},{32,40},{40,48},{48,56},{56,64},{64,7... | collective-permute-start | bytes 393224 | tf_op jit(solution)/shard_map/ppermute | solution.py:356
  105.5 9.5 %collective-permute-start = (f32[32,8,128]{2,0,1:T(8,128)S(1)}, f32[32,8,128]{2,0,1:T(8,128)S(1)}, u32[]{:S(2)}, u32[]{:S(2)}) collective-permute-start(f32[32,8,128]{2,0,1:T(8,128)S(1)} %bitcast.99), channel_id=1, source_target_pairs={{0,16},{8,24},{16,32},{24,40},{32,48},{40,56},{48,64},{56,72},{64,... | collective-permute-start | bytes 393224 | tf_op jit(solution)/shard_map/ppermute | solution.py:356
  108.7 6.3 %collective-permute-start.2 = (f32[32,8,128]{2,0,1:T(8,128)S(1)}, f32[32,8,128]{2,0,1:T(8,128)S(1)}, u32[]{:S(2)}, u32[]{:S(2)}) collective-permute-start(f32[32,8,128]{2,0,1:T(8,128)S(1)} %bitcast.100), channel_id=1, source_target_pairs={{8,0},{16,8},{24,16},{32,24},{40,32},{48,40},{56,48},{64,56},{72,6... | collective-permute-start | bytes 393224 | tf_op jit(solution)/shard_map/ppermute | solution.py:360
  110.7 7.0 %collective-permute-start.3 = (f32[32,8,128]{2,0,1:T(8,128)S(1)}, f32[32,8,128]{2,0,1:T(8,128)S(1)}, u32[]{:S(2)}, u32[]{:S(2)}) collective-permute-start(f32[32,8,128]{2,0,1:T(8,128)S(1)} %bitcast.101), channel_id=1, source_target_pairs={{16,0},{24,8},{32,16},{40,24},{48,32},{56,40},{64,48},{72,56},{80,... | collective-permute-start | bytes 393224 | tf_op jit(solution)/shard_map/ppermute | solution.py:360

commit v6 on v5

--- a/solution.py
+++ b/solution.py
@@ -261,60 +261,142 @@
     )(spec_send, lag_row, slow_rows)
 
 
-def sum_kernel(part_ref, out_ref, recv_ref, local_sem, send_sem, recv_sem):
-    count = recv_ref.shape[0]
+def share_kernel(part_ref, out_ref, pieces, send_rs, recv_rs, send_ag, recv_ag, local_sem):
+    count = pieces.shape[0]
+    slots = out_ref.shape[0]
+    reach = slots // 2
+    rows = pieces.shape[1]
     me = lax.axis_index("sta")
     tile = lax.axis_index("grid")
+    tiles = lax.axis_size("grid")
+    mesh_ids = pl.DeviceIdType.MESH
     barrier = pltpu.get_barrier_semaphore()
     for shift in range(1, count):
-        peer = lax.rem(me + shift, count)
-        pl.semaphore_signal(barrier, inc=1, device_id=(tile, peer), device_id_type=pl.DeviceIdType.MESH)
-    pl.semaphore_wait(barrier, count - 1)
-    own = pltpu.make_async_copy(part_ref, recv_ref.at[me], local_sem.at[0])
+        pl.semaphore_signal(barrier, inc=1, device_id=(tile, lax.rem(me + shift, count)), device_id_type=mesh_ids)
+    neighbours = jnp.int32(0)
+    for k in range(-reach, reach + 1):
+        if k == 0:
+            continue
+        there = (tile + k >= 0) & (tile + k < tiles)
+        neighbours = neighbours + there.astype(jnp.int32)
+
+        @pl.when(there)
+        def _():
+            for peer in range(count):
+                pl.semaphore_signal(barrier, inc=1, device_id=(tile + k, peer), device_id_type=mesh_ids)
+
+    pl.semaphore_wait(barrier, count - 1 + count * neighbours)
+    own = pltpu.make_async_copy(part_ref.at[pl.ds(pl.multiple_of(me * rows, 8), rows)], pieces.at[me], local_sem.at[0])
     own.start()
-    copies = []
+    sends = []
     for shift in range(1, count):
         peer = lax.rem(me + shift, count)
         copy = pltpu.make_async_remote_copy(
-            src_ref=part_ref,
-            dst_ref=recv_ref.at[me],
-            send_sem=send_sem.at[shift],
-            recv_sem=recv_sem.at[me],
+            src_ref=part_ref.at[pl.ds(pl.multiple_of(peer * rows, 8), rows)],
+            dst_ref=pieces.at[me],
+            send_sem=send_rs.at[shift],
+            recv_sem=recv_rs.at[me],
             device_id=(tile, peer),
-            device_id_type=pl.DeviceIdType.MESH,
+            device_id_type=mesh_ids,
         )
         copy.start()
-        copies.append(copy)
+        sends.append(copy)
     own.wait()
-    for shift in range(1, count):
-        copies[shift - 1].wait_send()
+    for copy in sends:
+        copy.wait_send()
+    for shift in range(1, count):
         source = lax.rem(me + count - shift, count)
         pltpu.make_async_remote_copy(
-            src_ref=part_ref,
-            dst_ref=recv_ref.at[source],
-            send_sem=send_sem.at[shift],
-            recv_sem=recv_sem.at[source],
+            src_ref=pieces.at[source],
+            dst_ref=pieces.at[source],
+            send_sem=send_rs.at[shift],
+            recv_sem=recv_rs.at[source],
             device_id=(tile, source),
-            device_id_type=pl.DeviceIdType.MESH,
+            device_id_type=mesh_ids,
         ).wait_recv()
-    total = recv_ref[0]
+    total = pieces[0]
     for source in range(1, count):
-        total = total + recv_ref[source]
-    out_ref[...] = total
-
-
-def sum_over_sta(part):
+        total = total + pieces[source]
+    mine = pl.ds(pl.multiple_of(me * rows, 8), rows)
+    out_ref[reach, mine] = total
+    block = out_ref.at[reach, mine]
+
+    def gather_copy(k, peer, slot):
+        return pltpu.make_async_remote_copy(
+            src_ref=block,
+            dst_ref=out_ref.at[slot, mine],
+            send_sem=send_ag.at[slot, peer],
+            recv_sem=recv_ag.at[slot, me],
+            device_id=(tile + k, peer),
+            device_id_type=mesh_ids,
+        )
+
+    peers = []
+    for shift in range(1, count):
+        copy = gather_copy(0, lax.rem(me + shift, count), reach)
+        copy.start()
+        peers.append(copy)
+    for k in range(-reach, reach + 1):
+        if k == 0:
+            continue
+        there = (tile + k >= 0) & (tile + k < tiles)
+
+        @pl.when(there)
+        def _():
+            for peer in range(count):
+                gather_copy(k, peer, reach - k).start()
+
+        @pl.when(jnp.logical_not(there))
+        def _():
+            out_ref[reach + k] = jnp.zeros(out_ref.shape[1:], out_ref.dtype)
+
+    for copy in peers:
+        copy.wait_send()
+    for shift in range(1, count):
+        source = lax.rem(me + count - shift, count)
+        pltpu.make_async_remote_copy(
+            src_ref=block,
+            dst_ref=out_ref.at[reach, pl.ds(pl.multiple_of(source * rows, 8), rows)],
+            send_sem=send_ag.at[reach, source],
+            recv_sem=recv_ag.at[reach, source],
+            device_id=(tile, source),
+            device_id_type=mesh_ids,
+        ).wait_recv()
+    for k in range(-reach, reach + 1):
+        if k == 0:
+            continue
+        there = (tile + k >= 0) & (tile + k < tiles)
+
+        @pl.when(there)
+        def _():
+            for peer in range(count):
+                gather_copy(k, peer, reach - k).wait_send()
+                pltpu.make_async_remote_copy(
+                    src_ref=block,
+                    dst_ref=out_ref.at[reach + k, pl.ds(peer * rows, rows)],
+                    send_sem=send_ag.at[reach + k, peer],
+                    recv_sem=recv_ag.at[reach + k, peer],
+                    device_id=(tile + k, peer),
+                    device_id_type=mesh_ids,
+                ).wait_recv()
+
+
+def share_power(part, reach):
     count = lax.axis_size("sta")
+    rows = part.shape[0] // count
+    slots = 2 * reach + 1
     return pl.pallas_call(
-        sum_kernel,
-        out_shape=jax.ShapeDtypeStruct(part.shape, jnp.float32),
+        share_kernel,
+        out_shape=jax.ShapeDtypeStruct((slots,) + part.shape, jnp.float32),
         in_specs=[pl.BlockSpec(memory_space=pltpu.VMEM)],
         out_specs=pl.BlockSpec(memory_space=pltpu.VMEM),
         scratch_shapes=[
-            pltpu.VMEM((count,) + part.shape, jnp.float32),
-            pltpu.SemaphoreType.DMA((1,)),
+            pltpu.VMEM((count, rows, part.shape[1]), jnp.float32),
             pltpu.SemaphoreType.DMA((count,)),
             pltpu.SemaphoreType.DMA((count,)),
+            pltpu.SemaphoreType.DMA((slots, count)),
+            pltpu.SemaphoreType.DMA((slots, count)),
+            pltpu.SemaphoreType.DMA((1,)),
         ],
         compiler_params=pltpu.CompilerParams(collective_id=0, has_side_effects=True),
     )(part)
@@ -347,28 +429,18 @@
     return jnp.einsum("xyw,kw->xyk", along_y, square_z, precision=lax.Precision.HIGHEST)
 
 
-def deblur(stacked, spread_taps):
+def deblur(observed, halo_tiles, spread_taps):
     tiles = lax.axis_size("grid")
     me = lax.axis_index("grid")
     reach = ITERS * 2 * HALF
-    halo_tiles = -(-reach // CX)
-    before = [
-        lax.ppermute(stacked, "grid", [(i, i + k) for i in range(tiles - k)])
-        for k in range(halo_tiles, 0, -1)
-    ]
-    after = [
-        lax.ppermute(stacked, "grid", [(i + k, i) for i in range(tiles - k)])
-        for k in range(1, halo_tiles + 1)
-    ]
     cut = halo_tiles * CX - reach
-    observed = jnp.concatenate(before + [stacked] + after, axis=0)
     observed = observed[cut : observed.shape[0] - cut]
     width = observed.shape[0]
     cell = (me - halo_tiles) * CX + cut + jnp.arange(width, dtype=jnp.int32)
     inside = (cell >= 0) & (cell < tiles * CX)
     square_y = band_matrix(spread_taps[1], CY)[:, HALF : HALF + CY]
     square_z = band_matrix(spread_taps[2], CZ)[:, HALF : HALF + CZ]
-    estimate = observed
+    estimate = jnp.where(inside[:, None, None], observed, 0.0)
     for sweep in range(ITERS):
         low = 2 * HALF * sweep + HALF
         blurred = blur_narrowing(estimate, spread_taps[0], square_y, square_z)
@@ -388,9 +460,11 @@
     block = spectra.shape[2]
     spec_send = spectra.reshape(groups, own_count, 2, block).transpose(0, 2, 1, 3)
     local_power = beam_power(spec_send, lag_samples, slowness[0])
-    summed = sum_over_sta(local_power)
-    stacked = (summed / (FREQS * STATIONS) + BACKGROUND).reshape(CY, CX, CZ).transpose(1, 0, 2)
-    estimate = deblur(stacked, spread_taps)
+    halo_tiles = -(-(ITERS * 2 * HALF) // CX)
+    summed = share_power(local_power, halo_tiles)
+    observed = (summed / (FREQS * STATIONS) + BACKGROUND).reshape(-1, CY, CX, CZ).transpose(0, 2, 1, 3)
+    stacked = observed[halo_tiles]
+    estimate = deblur(observed.reshape(-1, CY, CZ), halo_tiles, spread_taps)
     return (stacked[None], estimate[None])
 
 

time: 131 us -> 124 us (0.947)
  starting transfers between devices: 11.3 us -> 0 us
  Pallas kernels: 97.6 us -> 102 us
  waiting for transfers between devices: 2.58 us -> 0 us
    ppermute x4 -> x0, starting transfers between devices: 11.3 us -> none  [the longest x2 7.89 us: deblur(): lax.ppermute(stacked, 'grid', [(i, i + k) for i in range(tiles - k)])]
    pallas_call x1, Pallas kernels: 19 us -> 23.6 us  [share_power(): pl.pallas_call(share_kernel, out_shape=jax.ShapeDtypeStruct((slots,) + pa...]
    ppermute x4 -> x0, waiting for transfers between devices: 2.58 us -> none  [the longest x2 2.58 us: deblur(): lax.ppermute(stacked, 'grid', [(i + k, i) for i in range(tiles - k)])]
    unnamed x8 -> x0, local copies, waits for them, and re-layouts: 1.52 us -> none
  transfers between devices with their start and end apart: 4 -> 0, of which waited for: 1 -> 0; matrix products, arithmetic and copies ran while one was open for 2% -> 0% of each run, Pallas kernels for 0% -> 0%
where the time goes in v6:
time: 124 us; the launch traced here: 123 us
  Pallas kernels  102 us (82%)
  matrix products  13 us (10%)
  local copies, waits for them, and re-layouts  3.76 us (3%)
  other arithmetic  3.06 us (2%)
    pallas_call x1, Pallas kernels, beam_power(): pl.pallas_call(beam_kernel, out_shape=jax.ShapeDtypeStruct((CX * CY, CZ),...  78.6 us
    pallas_call x1, Pallas kernels, share_power(): pl.pallas_call(share_kernel, out_shape=jax.ShapeDtypeStruct((slots,) + pa...  23.6 us
    dot_general x8, matrix products, blur_narrowing(): jnp.einsum('jq,xqz->xjz', square_y, along_x, precision=lax.Precision.HIGH...  4.69 us
    dot_general x8, matrix products, blur_narrowing(): jnp.einsum('xyw,kw->xyk', along_y, square_z, precision=lax.Precision.HIGH...  4.19 us
    dot_general x8, matrix products, blur_narrowing(): jnp.einsum('ip,pyz->iyz', band_x, volume, precision=lax.Precision.HIGHEST)  4.08 us

profile of v6, /device:TPU:1, one launch (start us, length us, event | category | flops | bytes accessed | tf_op | source)
XLA Modules:
  0.0 123.0 jit_solution(4360264909242085400)
XLA Ops:
  0.6 0.8 slice_bitcast_fusion.9
  1.4 0.4 select_reduce_fusion
  1.8 1.6 %copy.82 = bf16[8,8,2,768]{3,1,2,0:T(8,128)(2,1)} copy(bf16[8,8,2,768]{3,2,1,0:T(2,128)(2,1)} %bitcast.109) | data formatting | bytes 393216 | tf_op jit(solution)/shard_map/reshape | solution.py:461
  3.4 78.6 %shard_map.59.part_ref = f32[256,128]{1,0:T(8,128)} custom-call(bf16[8,2,8,768]{3,2,1,0:T(8,128)(2,1)} %bitcast.108, s32[1,768]{1,0:T(1,128)} %lag_ref.1, bf16[3,768]{1,0:T(4,128)(2,1)} %bitcast.110), custom_call_target="tpu_custom_call" | custom-call | tf_op jit(solution)/shard_map/pallas_call | solution.py:241
  82.1 23.6 %shard_map.60 = f32[5,256,128]{2,1,0:T(8,128)} custom-call(f32[256,128]{1,0:T(8,128)} %shard_map.59.part_ref), custom_call_target="tpu_custom_call" | custom-call | tf_op jit(solution)/shard_map/pallas_call | solution.py:388
  105.7 1.2 multiply_add_fusion
  106.9 0.4 copy.83
  107.3 0.2 broadcast_select_fusion
  107.5 0.7 fusion.5
  108.3 0.1 select_reduce_fusion.9
  108.3 0.8 convolution_bitcast_fusion
  109.2 0.3 select_reduce_fusion.2
  109.4 0.1 slice.64
  109.5 0.6 fusion
  110.1 0.7 fusion.7
  110.8 0.9 convolution_bitcast_fusion.1
  111.7 0.6 convolution_multiply_fusion
  112.3 0.2 select_reduce_fusion.3
  112.4 0.6 fusion.10
  113.1 0.6 convolution_bitcast_fusion.2
  113.7 0.1 slice.71
  113.8 0.5 fusion.1
  114.3 0.2 select_reduce_fusion.4
  114.5 0.5 fusion.13
  115.1 0.7 convolution_bitcast_fusion.3
  115.8 0.5 convolution_multiply_fusion.1
  116.2 0.2 select_reduce_fusion.5
  116.4 0.5 fusion.16
  116.9 0.5 convolution_bitcast_fusion.4
  117.4 0.1 slice.74
  117.5 0.4 fusion.2
  117.9 0.1 select_reduce_fusion.6
  118.1 0.4 fusion.19
  118.5 0.5 convolution_bitcast_fusion.5
  119.0 0.4 convolution_multiply_fusion.2
  119.4 0.1 select_reduce_fusion.7
  119.5 0.4 fusion.22
  119.9 0.4 convolution_bitcast_fusion.6
  120.3 0.1 slice.77
  120.3 0.3 fusion.3
  120.7 0.1 select_reduce_fusion.8
  120.8 0.3 fusion.25
  121.1 0.3 convolution_bitcast_fusion.7
  121.4 0.9 fusion.4
  122.3 0.7 slice.79
  (10 shorter events, 0.1 us)

commit v7 on v6

--- a/solution.py
+++ b/solution.py
@@ -81,7 +81,7 @@
     return jnp.cos(angle), -jnp.sin(angle)
 
 
-def exchange_inputs(spec_ref, lag_ref, slow_ref, spec_in, lag_in, slow_in, local_sem, send_sem, recv_sem):
+def exchange_inputs(spec_ref, lag_ref, slow_ref, spec_in, lag_in, slow_in, local_sem, send_sem, recv_sem, then):
     count = spec_in.shape[0]
     me = lax.axis_index("sta")
     tile = lax.axis_index("grid")
@@ -113,6 +113,7 @@
             )
             copy.start()
             sends.append(copy)
+    then()
     for copy in local:
         copy.wait()
     for copy in sends:
@@ -131,25 +132,24 @@
             ).wait_recv()
 
 
-def align_inputs(spec_in, lag_in, slow_in, real_ref, imag_ref, turn_ref):
-    count, bins, block = spec_in.shape[0], spec_in.shape[2], spec_in.shape[3]
+def align_block(spec, lag, slow, source, real_ref, imag_ref, turn_ref):
+    bins, block = spec.shape[1], spec.shape[2]
     first_bin = lax.axis_index("sta") * bins
     bin_rows = (F0 + first_bin + lax.broadcasted_iota(jnp.int32, (bins, block), 0)).astype(jnp.float32)
-    for source in range(count):
-        cols = slice(source * block, (source + 1) * block)
-        product = bin_rows * lag_in[source].astype(jnp.float32)
-        whole = jnp.floor(product * (1.0 / NT))
-        left = product - whole * NT
-        left = jnp.where(left < 0.0, left + NT, left)
-        left = jnp.where(left >= NT, left - NT, left)
-        turned = left * (TWO_PI / NT)
-        cosine = jnp.cos(turned)
-        sine = jnp.sin(turned)
-        real_in = spec_in[source, 0].astype(jnp.float32)
-        imag_in = spec_in[source, 1].astype(jnp.float32)
-        real_ref[:, cols] = (real_in * cosine + imag_in * sine).astype(jnp.bfloat16).astype(jnp.float32)
-        imag_ref[:, cols] = (imag_in * cosine - real_in * sine).astype(jnp.bfloat16).astype(jnp.float32)
-        turn_ref[:, cols] = slow_in[source].astype(jnp.float32)
+    cols = pl.ds(pl.multiple_of(source * block, 128), block)
+    product = bin_rows * lag.astype(jnp.float32)
+    whole = jnp.floor(product * (1.0 / NT))
+    left = product - whole * NT
+    left = jnp.where(left < 0.0, left + NT, left)
+    left = jnp.where(left >= NT, left - NT, left)
+    turned = left * (TWO_PI / NT)
+    cosine = jnp.cos(turned)
+    sine = jnp.sin(turned)
+    real_in = spec[0].astype(jnp.float32)
+    imag_in = spec[1].astype(jnp.float32)
+    real_ref[:, cols] = (real_in * cosine + imag_in * sine).astype(jnp.bfloat16).astype(jnp.float32)
+    imag_ref[:, cols] = (imag_in * cosine - real_in * sine).astype(jnp.bfloat16).astype(jnp.float32)
+    turn_ref[:, cols] = slow.astype(jnp.float32)
 
 
 def complex_times(left, right):
@@ -168,11 +168,12 @@
 
 def beam_kernel(spec_ref, lag_ref, slow_ref, power_ref, spec_in, lag_in, slow_in, local_sem, send_sem, recv_sem,
                 real_ref, imag_ref, turn_ref, acc_ref, left_ref, right_ref):
-    exchange_inputs(spec_ref, lag_ref, slow_ref, spec_in, lag_in, slow_in, local_sem, send_sem, recv_sem)
-    align_inputs(spec_in, lag_in, slow_in, real_ref, imag_ref, turn_ref)
-    bins, stations = real_ref.shape
-    first_bin = lax.axis_index("sta") * bins
+    count, bins, block = spec_in.shape[0], spec_in.shape[2], spec_in.shape[3]
+    me = lax.axis_index("sta")
+    first_bin = me * bins
     width = CHUNK
+    per_block = block // width
+    half_z = CZ // 2
     rows8 = lax.broadcasted_iota(jnp.int32, (8, width), 0).astype(jnp.float32)
     rows16 = lax.broadcasted_iota(jnp.int32, (16, width), 0).astype(jnp.float32)
     omega0 = (F0 + first_bin).astype(jnp.float32) * (TWO_PI / NT)
@@ -180,7 +181,8 @@
     acc_ref[...] = jnp.zeros_like(acc_ref)
 
     def per_chunk(k, carry):
-        cols = pl.ds(pl.multiple_of(k * width, width), width)
+        source = lax.rem(me + k // per_block, count)
+        cols = pl.ds(pl.multiple_of(source * block + lax.rem(k, per_block) * width, 128), width)
         slow_x = turn_ref[0:1, cols]
         slow_y = turn_ref[1:2, cols]
         slow_z = turn_ref[2:3, cols]
@@ -204,17 +206,13 @@
                         parts_r.append(groups_r[mm] * yy_r - groups_i[mm] * yy_i)
                         parts_i.append(groups_r[mm] * yy_i + groups_i[mm] * yy_r)
                     row = y * CX + 8 * m
-                    left_ref[row : row + 16, 0:width] = jnp.concatenate(parts_r, axis=0).astype(jnp.bfloat16)
-                    left_ref[row : row + 16, width : 2 * width] = jnp.concatenate(parts_i, axis=0).astype(jnp.bfloat16)
-            for m in range(CZ // 16):
+                    left_ref[row : row + 16, :] = jnp.concatenate(parts_r, axis=0).astype(jnp.bfloat16)
+                    left_ref[CX * CY + row : CX * CY + row + 16, :] = jnp.concatenate(parts_i, axis=0).astype(jnp.bfloat16)
+            for m in range(half_z // 16):
                 z_r, z_i = complex_times((d_r[m : m + 1], d_i[m : m + 1]), (c_r, c_i))
-                cos_z = z_r.astype(jnp.bfloat16)
-                sin_z = (-z_i).astype(jnp.bfloat16)
                 row = 16 * m
-                right_ref[row : row + 16, 0:width] = cos_z
-                right_ref[row : row + 16, width : 2 * width] = sin_z
-                right_ref[CZ + row : CZ + row + 16, 0:width] = -sin_z
-                right_ref[CZ + row : CZ + row + 16, width : 2 * width] = cos_z
+                right_ref[row : row + 16, :] = z_r.astype(jnp.bfloat16)
+                right_ref[half_z + row : half_z + row + 16, :] = z_i.astype(jnp.bfloat16)
             acc_ref[f] += lax.dot_general(
                 left_ref[...], right_ref[...], (((1,), (1,)), ((), ())), preferred_element_type=jnp.float32
             )
@@ -223,13 +221,30 @@
         lax.fori_loop(0, bins, per_bin, start)
         return carry
 
-    lax.fori_loop(0, stations // width, per_chunk, 0)
-    total = jnp.zeros(power_ref.shape, jnp.float32)
+    def own_block():
+        align_block(spec_ref[me], lag_ref[...], slow_ref[...], me, real_ref, imag_ref, turn_ref)
+        lax.fori_loop(0, per_block, per_chunk, 0)
+
+    exchange_inputs(spec_ref, lag_ref, slow_ref, spec_in, lag_in, slow_in, local_sem, send_sem, recv_sem, own_block)
+
+    def align_other(shift, carry):
+        source = lax.rem(me + shift, count)
+        align_block(spec_in[source], lag_in[source], slow_in[source], source, real_ref, imag_ref, turn_ref)
+        return carry
+
+    lax.fori_loop(1, count, align_other, 0)
+    lax.fori_loop(per_block, count * per_block, per_chunk, 0)
+    cells = CX * CY
+    low = jnp.zeros((cells, half_z), jnp.float32)
+    high = jnp.zeros((cells, half_z), jnp.float32)
     for f in range(bins):
-        beams = acc_ref[f]
-        squares = beams * beams
-        total = total + squares[:, :CZ] + squares[:, CZ:]
-    power_ref[...] = total
+        sums = acc_ref[f]
+        u, w = sums[:cells, :half_z], sums[:cells, half_z:]
+        x, v = sums[cells:, :half_z], sums[cells:, half_z:]
+        low = low + ((u - v) * (u - v) + (w + x) * (w + x))
+        high = high + ((u + v) * (u + v) + (x - w) * (x - w))
+    power_ref[:, :half_z] = low
+    power_ref[:, half_z:] = high
 
 
 def beam_power(spec_send, lag_row, slow_rows):
@@ -253,9 +268,9 @@
             pltpu.VMEM((bins, stations), jnp.float32),
             pltpu.VMEM((bins, stations), jnp.float32),
             pltpu.VMEM((slow_rows.shape[0], stations), jnp.float32),
-            pltpu.VMEM((bins, CX * CY, 2 * CZ), jnp.float32),
-            pltpu.VMEM((CX * CY, 2 * width), jnp.bfloat16),
-            pltpu.VMEM((2 * CZ, 2 * width), jnp.bfloat16),
+            pltpu.VMEM((bins, 2 * CX * CY, CZ), jnp.float32),
+            pltpu.VMEM((2 * CX * CY, width), jnp.bfloat16),
+            pltpu.VMEM((CZ, width), jnp.bfloat16),
         ],
         compiler_params=pltpu.CompilerParams(collective_id=1, has_side_effects=True),
     )(spec_send, lag_row, slow_rows)
@@ -462,6 +477,7 @@
     local_power = beam_power(spec_send, lag_samples, slowness[0])
     halo_tiles = -(-(ITERS * 2 * HALF) // CX)
     summed = share_power(local_power, halo_tiles)
+    summed = jnp.concatenate([summed[..., : CZ // 2], summed[..., CZ // 2 :][..., ::-1]], axis=-1)
     observed = (summed / (FREQS * STATIONS) + BACKGROUND).reshape(-1, CY, CX, CZ).transpose(0, 2, 1, 3)
     stacked = observed[halo_tiles]
     estimate = deblur(observed.reshape(-1, CY, CZ), halo_tiles, spread_taps)

time: 124 us -> 112 us (0.903)
  Pallas kernels: 102 us -> 88.3 us
  local copies, waits for them, and re-layouts: 3.76 us -> 6.35 us
    pallas_call x1, Pallas kernels: 78.6 us -> 68.1 us  [beam_power(): pl.pallas_call(beam_kernel, out_shape=jax.ShapeDtypeStruct((CX * CY, CZ),...]
    pallas_call x1, Pallas kernels: 23.6 us -> 20.2 us  [share_power(): pl.pallas_call(share_kernel, out_shape=jax.ShapeDtypeStruct((slots,) + pa...]
    slice x0 -> x1, local copies, waits for them, and re-layouts: none -> 1.52 us  [per_device(): summed[..., :CZ // 2]]
where the time goes in v7:
time: 112 us; the launch traced here: 111 us
  Pallas kernels  88.3 us (79%)
  matrix products  13.2 us (12%)
  local copies, waits for them, and re-layouts  6.35 us (6%)
  other arithmetic  2.36 us (2%)
    pallas_call x1, Pallas kernels, beam_power(): pl.pallas_call(beam_kernel, out_shape=jax.ShapeDtypeStruct((CX * CY, CZ),...  68.1 us
    pallas_call x1, Pallas kernels, share_power(): pl.pallas_call(share_kernel, out_shape=jax.ShapeDtypeStruct((slots,) + pa...  20.2 us
    dot_general x8, matrix products, blur_narrowing(): jnp.einsum('jq,xqz->xjz', square_y, along_x, precision=lax.Precision.HIGH...  4.69 us
    dot_general x8, matrix products, blur_narrowing(): jnp.einsum('ip,pyz->iyz', band_x, volume, precision=lax.Precision.HIGHEST)  4.3 us
    dot_general x8, matrix products, blur_narrowing(): jnp.einsum('xyw,kw->xyk', along_y, square_z, precision=lax.Precision.HIGH...  4.19 us

profile of v7, /device:TPU:1, one launch (start us, length us, event | category | flops | bytes accessed | tf_op | source)
XLA Modules:
  0.0 111.2 jit_solution(7437561151718717549)
XLA Ops:
  0.6 1.6 %copy.83 = bf16[8,8,2,768]{3,1,2,0:T(8,128)(2,1)} copy(bf16[8,8,2,768]{3,2,1,0:T(2,128)(2,1)} %bitcast.110) | data formatting | bytes 393216 | tf_op jit(solution)/shard_map/reshape | solution.py:476
  2.2 68.1 %shard_map.59.part_ref = f32[256,128]{1,0:T(8,128)} custom-call(bf16[8,2,8,768]{3,2,1,0:T(8,128)(2,1)} %bitcast.109, s32[1,768]{1,0:T(1,128)} %lag_ref.1, bf16[3,768]{1,0:T(4,128)(2,1)} %bitcast.111), custom_call_target="tpu_custom_call" | custom-call | tf_op jit(solution)/shard_map/pallas_call | solution.py:256
  70.3 20.2 %shard_map.60 = f32[5,256,128]{2,1,0:T(8,128)} custom-call(f32[256,128]{1,0:T(8,128)} %shard_map.59.part_ref), custom_call_target="tpu_custom_call" | custom-call | tf_op jit(solution)/shard_map/pallas_call | solution.py:403
  90.6 1.5 %fusion.54 = (f32[5,256,64]{2,1,0:T(8,128)S(1)}, f32[5,256,64]{2,1,0:T(8,128)S(1)}) fusion(f32[5,256,128]{2,1,0:T(8,128)} %shard_map.60), kind=kLoop, calls=%fused_computation.106 | loop fusion | bytes 1310720 | tf_op jit(solution)/shard_map/slice | solution.py:480
  92.1 1.1 rev.3
  93.2 0.4 copy.25
  93.5 0.4 copy.24
  93.9 0.2 fusion.63
  94.2 0.7 slice.87
  94.8 0.2 fusion.5
  95.1 0.0 copy-start
  95.1 0.2 broadcast_select_fusion
  95.3 0.4 copy-done
  95.8 0.4 select_reduce_fusion
  96.2 0.7 fusion.6
  96.9 0.1 select_reduce_fusion.9
  97.0 0.8 convolution_bitcast_fusion
  97.8 0.1 slice.72
  97.9 0.3 select_reduce_fusion.2
  98.2 0.6 fusion
  98.8 0.7 fusion.8
  99.5 0.9 convolution_bitcast_fusion.1
  100.3 0.6 convolution_multiply_fusion
  100.9 0.2 select_reduce_fusion.3
  101.1 0.6 fusion.11
  101.7 0.6 convolution_bitcast_fusion.2
  102.4 0.1 slice.79
  102.4 0.5 fusion.1
  103.0 0.2 select_reduce_fusion.4
  103.2 0.5 fusion.14
  103.7 0.7 convolution_bitcast_fusion.3
  104.4 0.5 convolution_multiply_fusion.1
  104.9 0.2 select_reduce_fusion.5
  105.1 0.5 fusion.17
  105.5 0.5 convolution_bitcast_fusion.4
  106.0 0.1 slice.82
  106.1 0.4 fusion.2
  106.6 0.1 select_reduce_fusion.6
  106.7 0.6 fusion.20
  107.4 0.5 convolution_bitcast_fusion.5
  107.9 0.4 convolution_multiply_fusion.2
  108.3 0.1 select_reduce_fusion.7
  108.4 0.4 fusion.23
  108.7 0.4 convolution_bitcast_fusion.6
  109.1 0.1 slice.85
  109.2 0.3 fusion.3
  109.5 0.1 select_reduce_fusion.8
  109.6 0.3 fusion.26
  109.9 0.3 convolution_bitcast_fusion.7
  110.3 0.9 fusion.4
  (11 shorter events, 0.1 us)
Async XLA Ops:
  95.1 0.7 copy-start

commit v8 on v7

--- a/solution.py
+++ b/solution.py
@@ -468,6 +468,62 @@
     return estimate
 
 
+def deblur_kernel(taps_ref, obs_ref, kx_ref, kz_ref, out_ref):
+    tiles = lax.axis_size("grid")
+    me = lax.axis_index("grid")
+    planes, width, depth = obs_ref.shape
+    halo_tiles = (width - CX) // (2 * CX)
+    highest = lax.Precision.HIGHEST
+
+    def inside(low, size):
+        cell = (me - halo_tiles) * CX + low + lax.broadcasted_iota(jnp.int32, (size, depth), 0)
+        return (cell >= 0) & (cell < tiles * CX)
+
+    def blur(volume):
+        size_in = volume[0].shape[0]
+        size_out = size_in - 2 * HALF
+        band = kx_ref[0:size_out, 0:size_in]
+        along_x = [jnp.dot(band, plane, precision=highest, preferred_element_type=jnp.float32) for plane in volume]
+        along_y = []
+        for y in range(planes):
+            total = None
+            for q in range(planes):
+                term = taps_ref[1, q - y + HALF] * along_x[q]
+                total = term if total is None else total + term
+            along_y.append(total)
+        joined = jnp.concatenate(along_y, axis=0)
+        along_z = jnp.dot(joined, kz_ref[...], precision=highest, preferred_element_type=jnp.float32)
+        return [along_z[y * size_out : (y + 1) * size_out] for y in range(planes)]
+
+    observed = [obs_ref[y] for y in range(planes)]
+    mask = inside(0, width)
+    estimate = [jnp.where(mask, plane, 0.0) for plane in observed]
+    for sweep in range(ITERS):
+        low = 2 * HALF * sweep + HALF
+        blurred = blur(estimate)
+        size = blurred[0].shape[0]
+        mask = inside(low, size)
+        ratio = [jnp.where(mask, observed[y][low : low + size] / blurred[y], 0.0) for y in range(planes)]
+        spread = blur(ratio)
+        estimate = [estimate[y][2 * HALF : 2 * HALF + spread[y].shape[0]] * spread[y] for y in range(planes)]
+    for y in range(planes):
+        out_ref[y] = estimate[y]
+
+
+def deblur_tile(observed, spread_taps, order):
+    planes, width, depth = observed.shape
+    band_x = band_matrix(spread_taps[0], width - 2 * HALF)
+    square_z = band_matrix(spread_taps[2], CZ)[:, HALF : HALF + CZ]
+    band_z = square_z[order][:, order].T
+    vmem = pl.BlockSpec(memory_space=pltpu.VMEM)
+    return pl.pallas_call(
+        deblur_kernel,
+        out_shape=jax.ShapeDtypeStruct((planes, CX, depth), jnp.float32),
+        in_specs=[pl.BlockSpec(memory_space=pltpu.SMEM), vmem, vmem, vmem],
+        out_specs=vmem,
+    )(spread_taps, observed, band_x, band_z)
+
+
 def per_device(spectra, lag_samples, slowness, spread_taps):
     groups = lax.axis_size("sta")
     own_count = FREQS // groups
@@ -477,10 +533,14 @@
     local_power = beam_power(spec_send, lag_samples, slowness[0])
     halo_tiles = -(-(ITERS * 2 * HALF) // CX)
     summed = share_power(local_power, halo_tiles)
-    summed = jnp.concatenate([summed[..., : CZ // 2], summed[..., CZ // 2 :][..., ::-1]], axis=-1)
-    observed = (summed / (FREQS * STATIONS) + BACKGROUND).reshape(-1, CY, CX, CZ).transpose(0, 2, 1, 3)
-    stacked = observed[halo_tiles]
-    estimate = deblur(observed.reshape(-1, CY, CZ), halo_tiles, spread_taps)
+    order = jnp.concatenate([jnp.arange(CZ // 2), jnp.arange(CZ - 1, CZ // 2 - 1, -1)])
+    observed = summed / (FREQS * STATIONS) + BACKGROUND
+    slots = observed.shape[0]
+    planes = observed.reshape(slots, CY, CX, CZ).transpose(1, 0, 2, 3).reshape(CY, slots * CX, CZ)
+    estimate = deblur_tile(planes, spread_taps, order)
+    both = jnp.stack([observed[halo_tiles].reshape(CY, CX, CZ), estimate])
+    both = jnp.concatenate([both[..., : CZ // 2], both[..., CZ // 2 :][..., ::-1]], axis=-1).transpose(0, 2, 1, 3)
+    stacked, estimate = both[0], both[1]
     return (stacked[None], estimate[None])
 
 

time: 112 us -> 113 us (level)
  matrix products: 13.2 us -> 0 us
  Pallas kernels: 88.3 us -> 101 us
  other arithmetic: 2.36 us -> 3.72 us
    dot_general x24 -> x0, matrix products: 13.2 us -> none  [the longest x8 4.69 us: blur_narrowing(): jnp.einsum('jq,xqz->xjz', square_y, along_x, precision=lax.Precision.HIGH...]
    pallas_call x0 -> x1, Pallas kernels: none -> 13.1 us  [deblur_tile(): pl.pallas_call(deblur_kernel, out_shape=jax.ShapeDtypeStruct((planes, CX,...]
    slice x6 -> x3, local copies, waits for them, and re-layouts: 2.49 us -> 0.04 us  [the longest x1 0.02 us: per_device(): stacked, estimate = (both[0], both[1])]
    gather x0 -> x3, local copies, waits for them, and re-layouts: none -> 1.99 us  [deblur_tile(): band_z = square_z[order][:, order].T]
where the time goes in v8:
time: 113 us; the launch traced here: 112 us
  Pallas kernels  101 us (89%)
  local copies, waits for them, and re-layouts  6.04 us (5%)
  other arithmetic  3.72 us (3%)
    pallas_call x1, Pallas kernels, beam_power(): pl.pallas_call(beam_kernel, out_shape=jax.ShapeDtypeStruct((CX * CY, CZ),...  68.1 us
    pallas_call x1, Pallas kernels, share_power(): pl.pallas_call(share_kernel, out_shape=jax.ShapeDtypeStruct((slots,) + pa...  20.2 us
    pallas_call x1, Pallas kernels, deblur_tile(): pl.pallas_call(deblur_kernel, out_shape=jax.ShapeDtypeStruct((planes, CX,...  13.1 us

profile of v8, /device:TPU:1, one launch (start us, length us, event | category | flops | bytes accessed | tf_op | source)
XLA Modules:
  0.0 112.0 jit_solution(3654553326701794077)
XLA Ops:
  0.7 0.1 fusion
  0.7 0.8 slice_bitcast_fusion
  1.5 0.2 select_reduce_fusion.1
  1.7 0.1 copy.25
  1.8 0.7 gather_fusion
  2.5 0.0 copy-start
  2.5 0.1 copy.20
  2.6 1.2 %gather_fusion.1 = f32[128,128]{1,0:T(8,128)} fusion(f32[128,128]{0,1:T(8,128)S(1)} %copy.20, s32[1024]{0:T(1024)S(1)} %pad_clamp_fusion), kind=kCustom, calls=%fused_computation.1 | custom fusion | bytes 131584 | tf_op jit(solution)/shard_map/gather | solution.py:517
  3.8 1.0 select_reduce_fusion.kx_ref
  4.8 0.0 copy-done
  4.8 0.7 copy.27
  5.5 68.1 %shard_map.59.part_ref = f32[256,128]{1,0:T(8,128)} custom-call(bf16[8,2,8,768]{3,2,1,0:T(8,128)(2,1)} %bitcast.23, s32[1,768]{1,0:T(1,128)} %lag_ref.1, bf16[3,768]{1,0:T(4,128)(2,1)} %bitcast.27), custom_call_target="tpu_custom_call" | custom-call | tf_op jit(solution)/shard_map/pallas_call | solution.py:256
  73.6 20.2 %shard_map.60 = f32[5,256,128]{2,1,0:T(8,128)} custom-call(f32[256,128]{1,0:T(8,128)} %shard_map.59.part_ref), custom_call_target="tpu_custom_call" | custom-call | tf_op jit(solution)/shard_map/pallas_call | solution.py:403
  93.9 1.2 %multiply_add_fusion = f32[5,256,128]{2,1,0:T(8,128)S(1)} fusion(f32[5,256,128]{2,1,0:T(8,128)} %shard_map.60), kind=kLoop, calls=%fused_computation.6 | loop fusion | flops 327680 | bytes 1310720 | tf_op jit(solution)/shard_map/add | solution.py:537
  95.1 0.9 copy.18
  96.0 13.1 %shard_map.61 = f32[8,32,128]{2,1,0:T(8,128)} custom-call(f32[3,17]{1,0:T(4,128)} %taps_ref.1, f32[8,160,128]{2,1,0:T(8,128)} %bitcast.22, f32[144,160]{1,0:T(8,128)} %select_reduce_fusion.kx_ref, f32[128,128]{1,0:T(8,128)} %gather_fusion.1), custom_call_target="tpu_custom_call" | custom-call | tf_op jit(solution)/shard_map/pallas_call | solution.py:519
  109.1 1.1 slice_maximum_fusion
  110.2 0.1 rev.3
  110.3 0.1 maximum_bitcast_fusion
  110.5 0.7 copy.22
  111.2 0.7 copy.21
  (8 shorter events, 0.1 us)
Async XLA Ops:
  2.5 2.4 %copy-start = (bf16[64,2,768]{2,1,0:T(2,128)(2,1)S(1)}, bf16[64,2,768]{2,1,0:T(2,128)(2,1)}, u32[]{:S(2)}) copy-start(bf16[64,2,768]{2,1,0:T(2,128)(2,1)} %param.4) | copy-start | bytes 589828

commit v9 on v8

--- a/solution.py
+++ b/solution.py
@@ -193,21 +193,26 @@
             (a_r, a_i), (b_r, b_i), (y_r, y_i), (c_r, c_i), (d_r, d_i) = state
             real_in = real_ref[pl.ds(f, 1), cols]
             imag_in = imag_ref[pl.ds(f, 1), cols]
-            groups_r, groups_i = [], []
-            for m in range(CX // 8):
-                x_r, x_i = complex_times((b_r[m : m + 1], b_i[m : m + 1]), (a_r, a_i))
-                groups_r.append(real_in * x_r - imag_in * x_i)
-                groups_i.append(real_in * x_i + imag_in * x_r)
+            q_r = real_in * y_r - imag_in * y_i
+            q_i = real_in * y_i + imag_in * y_r
+            near = [complex_times((b_r[m : m + 1], b_i[m : m + 1]), (a_r, a_i)) for m in range(CX // 16)]
+            cells = CX * CY
             for y in range(CY):
-                yy_r, yy_i = y_r[y : y + 1], y_i[y : y + 1]
-                for m in range(0, CX // 8, 2):
-                    parts_r, parts_i = [], []
-                    for mm in (m, m + 1):
-                        parts_r.append(groups_r[mm] * yy_r - groups_i[mm] * yy_i)
-                        parts_i.append(groups_r[mm] * yy_i + groups_i[mm] * yy_r)
-                    row = y * CX + 8 * m
-                    left_ref[row : row + 16, :] = jnp.concatenate(parts_r, axis=0).astype(jnp.bfloat16)
-                    left_ref[CX * CY + row : CX * CY + row + 16, :] = jnp.concatenate(parts_i, axis=0).astype(jnp.bfloat16)
+                qq_r, qq_i = q_r[y : y + 1], q_i[y : y + 1]
+                lo_r, lo_i, hi_r, hi_i = [], [], [], []
+                for x_r, x_i in near:
+                    t1, t2 = qq_r * x_r, qq_i * x_i
+                    t3, t4 = qq_r * x_i, qq_i * x_r
+                    lo_r.append(t1 - t2)
+                    lo_i.append(t3 + t4)
+                    hi_r.append(t1 + t2)
+                    hi_i.append(t4 - t3)
+                row = y * CX
+                half = CX // 2
+                left_ref[row : row + half, :] = jnp.concatenate(lo_r, axis=0).astype(jnp.bfloat16)
+                left_ref[row + half : row + CX, :] = jnp.concatenate(hi_r, axis=0).astype(jnp.bfloat16)
+                left_ref[cells + row : cells + row + half, :] = jnp.concatenate(lo_i, axis=0).astype(jnp.bfloat16)
+                left_ref[cells + row + half : cells + row + CX, :] = jnp.concatenate(hi_i, axis=0).astype(jnp.bfloat16)
             for m in range(half_z // 16):
                 z_r, z_i = complex_times((d_r[m : m + 1], d_i[m : m + 1]), (c_r, c_i))
                 row = 16 * m
@@ -536,9 +541,11 @@
     order = jnp.concatenate([jnp.arange(CZ // 2), jnp.arange(CZ - 1, CZ // 2 - 1, -1)])
     observed = summed / (FREQS * STATIONS) + BACKGROUND
     slots = observed.shape[0]
-    planes = observed.reshape(slots, CY, CX, CZ).transpose(1, 0, 2, 3).reshape(CY, slots * CX, CZ)
+    observed = observed.reshape(slots, CY, CX, CZ)
+    observed = jnp.concatenate([observed[:, :, : CX // 2], observed[:, :, CX // 2 :][:, :, ::-1]], axis=2)
+    planes = observed.transpose(1, 0, 2, 3).reshape(CY, slots * CX, CZ)
     estimate = deblur_tile(planes, spread_taps, order)
-    both = jnp.stack([observed[halo_tiles].reshape(CY, CX, CZ), estimate])
+    both = jnp.stack([observed[halo_tiles], estimate])
     both = jnp.concatenate([both[..., : CZ // 2], both[..., CZ // 2 :][..., ::-1]], axis=-1).transpose(0, 2, 1, 3)
     stacked, estimate = both[0], both[1]
     return (stacked[None], estimate[None])

time: 113 us -> 112 us (level)
  no operation moved by 1% of the time
where the time goes in v9:
time: 112 us
  Pallas kernels  101 us (90%)
  local copies, waits for them, and re-layouts  6.14 us (5%)
  other arithmetic  3.81 us (3%)
    pallas_call x1, Pallas kernels, beam_power(): pl.pallas_call(beam_kernel, out_shape=jax.ShapeDtypeStruct((CX * CY, CZ),...  68 us
    pallas_call x1, Pallas kernels, share_power(): pl.pallas_call(share_kernel, out_shape=jax.ShapeDtypeStruct((slots,) + pa...  20 us
    pallas_call x1, Pallas kernels, deblur_tile(): pl.pallas_call(deblur_kernel, out_shape=jax.ShapeDtypeStruct((planes, CX,...  13.1 us

profile of v9, /device:TPU:1, one launch (start us, length us, event | category | flops | bytes accessed | tf_op | source)
XLA Modules:
  0.0 111.8 jit_solution(13481467656271249870)
XLA Ops:
  0.7 0.1 fusion.2
  0.7 0.8 slice_bitcast_fusion
  1.5 0.2 select_reduce_fusion.1
  1.7 0.1 copy.25
  1.8 0.7 gather_fusion
  2.5 0.0 copy-start
  2.5 0.1 copy.20
  2.6 1.2 %gather_fusion.1 = f32[128,128]{1,0:T(8,128)} fusion(f32[128,128]{0,1:T(8,128)S(1)} %copy.20, s32[1024]{0:T(1024)S(1)} %pad_clamp_fusion), kind=kCustom, calls=%fused_computation.1 | custom fusion | bytes 131584 | tf_op jit(solution)/shard_map/gather | solution.py:522
  3.8 1.0 select_reduce_fusion.kx_ref
  4.8 0.0 copy-done
  4.8 0.7 copy.27
  5.5 68.0 %shard_map.59.part_ref = f32[256,128]{1,0:T(8,128)} custom-call(bf16[8,2,8,768]{3,2,1,0:T(8,128)(2,1)} %bitcast.22, s32[1,768]{1,0:T(1,128)} %lag_ref.1, bf16[3,768]{1,0:T(4,128)(2,1)} %bitcast.25), custom_call_target="tpu_custom_call" | custom-call | tf_op jit(solution)/shard_map/pallas_call | solution.py:261
  73.6 20.0 %shard_map.60 = f32[5,256,128]{2,1,0:T(8,128)} custom-call(f32[256,128]{1,0:T(8,128)} %shard_map.59.part_ref), custom_call_target="tpu_custom_call" | custom-call | tf_op jit(solution)/shard_map/pallas_call | solution.py:408
  93.5 1.2 %multiply_add_fusion = f32[5,256,128]{2,1,0:T(8,128)S(1)} fusion(f32[5,256,128]{2,1,0:T(8,128)} %shard_map.60), kind=kLoop, calls=%fused_computation.10 | loop fusion | flops 327680 | bytes 1310720 | tf_op jit(solution)/shard_map/add | solution.py:542
  94.7 0.1 fusion.3
  94.8 0.1 fusion
  94.9 0.9 copy.18
  95.8 13.1 %shard_map.61 = f32[8,32,128]{2,1,0:T(8,128)} custom-call(f32[3,17]{1,0:T(4,128)} %taps_ref.1, f32[8,160,128]{2,1,0:T(8,128)} %bitcast.21, f32[144,160]{1,0:T(8,128)} %select_reduce_fusion.kx_ref, f32[128,128]{1,0:T(8,128)} %gather_fusion.1), custom_call_target="tpu_custom_call" | custom-call | tf_op jit(solution)/shard_map/pallas_call | solution.py:524
  108.9 1.1 slice_maximum_fusion
  110.0 0.1 rev.7
  110.1 0.1 maximum_bitcast_fusion
  110.3 0.7 copy.22
  111.1 0.7 copy.21
  (9 shorter events, 0.1 us)
Async XLA Ops:
  2.5 2.4 %copy-start = (bf16[64,2,768]{2,1,0:T(2,128)(2,1)S(1)}, bf16[64,2,768]{2,1,0:T(2,128)(2,1)}, u32[]{:S(2)}) copy-start(bf16[64,2,768]{2,1,0:T(2,128)(2,1)} %param.4) | copy-start | bytes 589828

commit v10 on v9

--- a/solution.py
+++ b/solution.py
@@ -302,10 +302,9 @@
 
         @pl.when(there)
         def _():
-            for peer in range(count):
-                pl.semaphore_signal(barrier, inc=1, device_id=(tile + k, peer), device_id_type=mesh_ids)
-
-    pl.semaphore_wait(barrier, count - 1 + count * neighbours)
+            pl.semaphore_signal(barrier, inc=1, device_id=(tile + k, me), device_id_type=mesh_ids)
+
+    pl.semaphore_wait(barrier, count - 1 + neighbours)
     own = pltpu.make_async_copy(part_ref.at[pl.ds(pl.multiple_of(me * rows, 8), rows)], pieces.at[me], local_sem.at[0])
     own.start()
     sends = []
@@ -359,14 +358,8 @@
     for k in range(-reach, reach + 1):
         if k == 0:
             continue
-        there = (tile + k >= 0) & (tile + k < tiles)
-
-        @pl.when(there)
-        def _():
-            for peer in range(count):
-                gather_copy(k, peer, reach - k).start()
-
-        @pl.when(jnp.logical_not(there))
+
+        @pl.when(jnp.logical_not((tile + k >= 0) & (tile + k < tiles)))
         def _():
             out_ref[reach + k] = jnp.zeros(out_ref.shape[1:], out_ref.dtype)
 
@@ -382,23 +375,40 @@
             device_id=(tile, source),
             device_id_type=mesh_ids,
         ).wait_recv()
+
+    def halo_copy(k):
+        return pltpu.make_async_remote_copy(
+            src_ref=out_ref.at[reach],
+            dst_ref=out_ref.at[reach - k],
+            send_sem=send_ag.at[reach - k, me],
+            recv_sem=recv_ag.at[reach - k, me],
+            device_id=(tile + k, me),
+            device_id_type=mesh_ids,
+        )
+
     for k in range(-reach, reach + 1):
         if k == 0:
             continue
-        there = (tile + k >= 0) & (tile + k < tiles)
-
-        @pl.when(there)
+
+        @pl.when((tile + k >= 0) & (tile + k < tiles))
         def _():
-            for peer in range(count):
-                gather_copy(k, peer, reach - k).wait_send()
-                pltpu.make_async_remote_copy(
-                    src_ref=block,
-                    dst_ref=out_ref.at[reach + k, pl.ds(peer * rows, rows)],
-                    send_sem=send_ag.at[reach + k, peer],
-                    recv_sem=recv_ag.at[reach + k, peer],
-                    device_id=(tile + k, peer),
-                    device_id_type=mesh_ids,
-                ).wait_recv()
+            halo_copy(k).start()
+
+    for k in range(-reach, reach + 1):
+        if k == 0:
+            continue
+
+        @pl.when((tile + k >= 0) & (tile + k < tiles))
+        def _():
+            halo_copy(k).wait_send()
+            pltpu.make_async_remote_copy(
+                src_ref=out_ref.at[reach],
+                dst_ref=out_ref.at[reach + k],
+                send_sem=send_ag.at[reach + k, me],
+                recv_sem=recv_ag.at[reach + k, me],
+                device_id=(tile + k, me),
+                device_id_type=mesh_ids,
+            ).wait_recv()
 
 
 def share_power(part, reach):

time: 112 us -> 113 us (level)
  no operation moved by 1% of the time
where the time goes in v10:
time: 113 us
  Pallas kernels  102 us (90%)
  local copies, waits for them, and re-layouts  6.14 us (5%)
  other arithmetic  3.81 us (3%)
    pallas_call x1, Pallas kernels, beam_power(): pl.pallas_call(beam_kernel, out_shape=jax.ShapeDtypeStruct((CX * CY, CZ),...  68 us
    pallas_call x1, Pallas kernels, share_power(): pl.pallas_call(share_kernel, out_shape=jax.ShapeDtypeStruct((slots,) + pa...  20.7 us
    pallas_call x1, Pallas kernels, deblur_tile(): pl.pallas_call(deblur_kernel, out_shape=jax.ShapeDtypeStruct((planes, CX,...  13.1 us

profile of v10, /device:TPU:1, one launch (start us, length us, event | category | flops | bytes accessed | tf_op | source)
XLA Modules:
  0.0 112.5 jit_solution(1786819505273796522)
XLA Ops:
  0.7 0.1 fusion.2
  0.7 0.8 slice_bitcast_fusion
  1.5 0.2 select_reduce_fusion.1
  1.7 0.1 copy.25
  1.8 0.7 gather_fusion
  2.5 0.0 copy-start
  2.5 0.1 copy.20
  2.6 1.2 %gather_fusion.1 = f32[128,128]{1,0:T(8,128)} fusion(f32[128,128]{0,1:T(8,128)S(1)} %copy.20, s32[1024]{0:T(1024)S(1)} %pad_clamp_fusion), kind=kCustom, calls=%fused_computation.1 | custom fusion | bytes 131584 | tf_op jit(solution)/shard_map/gather | solution.py:532
  3.8 1.0 select_reduce_fusion.kx_ref
  4.8 0.0 copy-done
  4.8 0.7 copy.27
  5.5 68.0 %shard_map.59.part_ref = f32[256,128]{1,0:T(8,128)} custom-call(bf16[8,2,8,768]{3,2,1,0:T(8,128)(2,1)} %bitcast.22, s32[1,768]{1,0:T(1,128)} %lag_ref.1, bf16[3,768]{1,0:T(4,128)(2,1)} %bitcast.25), custom_call_target="tpu_custom_call" | custom-call | tf_op jit(solution)/shard_map/pallas_call | solution.py:261
  73.6 20.7 %shard_map.60 = f32[5,256,128]{2,1,0:T(8,128)} custom-call(f32[256,128]{1,0:T(8,128)} %shard_map.59.part_ref), custom_call_target="tpu_custom_call" | custom-call | tf_op jit(solution)/shard_map/pallas_call | solution.py:418
  94.3 1.2 %multiply_add_fusion = f32[5,256,128]{2,1,0:T(8,128)S(1)} fusion(f32[5,256,128]{2,1,0:T(8,128)} %shard_map.60), kind=kLoop, calls=%fused_computation.10 | loop fusion | flops 327680 | bytes 1310720 | tf_op jit(solution)/shard_map/add | solution.py:552
  95.4 0.1 fusion.3
  95.6 0.1 fusion
  95.6 0.9 copy.18
  96.5 13.1 %shard_map.61 = f32[8,32,128]{2,1,0:T(8,128)} custom-call(f32[3,17]{1,0:T(4,128)} %taps_ref.1, f32[8,160,128]{2,1,0:T(8,128)} %bitcast.21, f32[144,160]{1,0:T(8,128)} %select_reduce_fusion.kx_ref, f32[128,128]{1,0:T(8,128)} %gather_fusion.1), custom_call_target="tpu_custom_call" | custom-call | tf_op jit(solution)/shard_map/pallas_call | solution.py:534
  109.6 1.1 slice_maximum_fusion
  110.7 0.1 rev.7
  110.9 0.1 maximum_bitcast_fusion
  111.0 0.7 copy.22
  111.8 0.7 copy.21
  (9 shorter events, 0.1 us)
Async XLA Ops:
  2.5 2.4 %copy-start = (bf16[64,2,768]{2,1,0:T(2,128)(2,1)S(1)}, bf16[64,2,768]{2,1,0:T(2,128)(2,1)}, u32[]{:S(2)}) copy-start(bf16[64,2,768]{2,1,0:T(2,128)(2,1)} %param.4) | copy-start | bytes 589828

commit v11 on v10

--- a/solution.py
+++ b/solution.py
@@ -483,10 +483,33 @@
     return estimate
 
 
-def deblur_kernel(taps_ref, obs_ref, kx_ref, kz_ref, out_ref):
+def band_of(taps_ref, axis, rows, cols):
+    offset = cols - rows + HALF
+    band = jnp.zeros(offset.shape, jnp.float32)
+    for tap in range(TAPS):
+        band = jnp.where(offset == tap, taps_ref[axis, tap], band)
+    return band
+
+
+def mirror(index, length):
+    return jnp.where(index < length // 2, index, 3 * (length // 2) - 1 - index)
+
+
+def deblur_kernel(taps_ref, obs_ref, out_ref, kx_ref, kz_ref):
     tiles = lax.axis_size("grid")
     me = lax.axis_index("grid")
     planes, width, depth = obs_ref.shape
+    shape_x = kx_ref.shape
+    kx_ref[...] = band_of(
+        taps_ref, 0, lax.broadcasted_iota(jnp.int32, shape_x, 0) + HALF, lax.broadcasted_iota(jnp.int32, shape_x, 1)
+    )
+    shape_z = kz_ref.shape
+    kz_ref[...] = band_of(
+        taps_ref,
+        2,
+        mirror(lax.broadcasted_iota(jnp.int32, shape_z, 1), depth),
+        mirror(lax.broadcasted_iota(jnp.int32, shape_z, 0), depth),
+    )
     halo_tiles = (width - CX) // (2 * CX)
     highest = lax.Precision.HIGHEST
 
@@ -525,18 +548,19 @@
         out_ref[y] = estimate[y]
 
 
-def deblur_tile(observed, spread_taps, order):
+def deblur_tile(observed, spread_taps):
     planes, width, depth = observed.shape
-    band_x = band_matrix(spread_taps[0], width - 2 * HALF)
-    square_z = band_matrix(spread_taps[2], CZ)[:, HALF : HALF + CZ]
-    band_z = square_z[order][:, order].T
     vmem = pl.BlockSpec(memory_space=pltpu.VMEM)
     return pl.pallas_call(
         deblur_kernel,
         out_shape=jax.ShapeDtypeStruct((planes, CX, depth), jnp.float32),
-        in_specs=[pl.BlockSpec(memory_space=pltpu.SMEM), vmem, vmem, vmem],
+        in_specs=[pl.BlockSpec(memory_space=pltpu.SMEM), vmem],
         out_specs=vmem,
-    )(spread_taps, observed, band_x, band_z)
+        scratch_shapes=[
+            pltpu.VMEM((width - 2 * HALF, width), jnp.float32),
+            pltpu.VMEM((depth, depth), jnp.float32),
+        ],
+    )(spread_taps, observed)
 
 
 def per_device(spectra, lag_samples, slowness, spread_taps):
@@ -548,13 +572,12 @@
     local_power = beam_power(spec_send, lag_samples, slowness[0])
     halo_tiles = -(-(ITERS * 2 * HALF) // CX)
     summed = share_power(local_power, halo_tiles)
-    order = jnp.concatenate([jnp.arange(CZ // 2), jnp.arange(CZ - 1, CZ // 2 - 1, -1)])
     observed = summed / (FREQS * STATIONS) + BACKGROUND
     slots = observed.shape[0]
     observed = observed.reshape(slots, CY, CX, CZ)
     observed = jnp.concatenate([observed[:, :, : CX // 2], observed[:, :, CX // 2 :][:, :, ::-1]], axis=2)
     planes = observed.transpose(1, 0, 2, 3).reshape(CY, slots * CX, CZ)
-    estimate = deblur_tile(planes, spread_taps, order)
+    estimate = deblur_tile(planes, spread_taps)
     both = jnp.stack([observed[halo_tiles], estimate])
     both = jnp.concatenate([both[..., : CZ // 2], both[..., CZ // 2 :][..., ::-1]], axis=-1).transpose(0, 2, 1, 3)
     stacked, estimate = both[0], both[1]

time: 113 us -> 110 us (0.973)
  local copies, waits for them, and re-layouts: 6.14 us -> 4.22 us
  other arithmetic: 3.81 us -> 2.51 us
    gather x3 -> x0, local copies, waits for them, and re-layouts: 1.99 us -> none  [deblur_tile(): band_z = square_z[order][:, order].T]
    reduce_sum x2 -> x0, other arithmetic: 1.19 us -> none  [band_matrix(): jnp.sum(jnp.where(offset[None] == picks, taps[:, None, None], 0.0), axis=0)]
where the time goes in v11:
time: 110 us; the launch traced here: 109 us
  Pallas kernels  102 us (93%)
  local copies, waits for them, and re-layouts  4.22 us (4%)
  other arithmetic  2.51 us (2%)
    pallas_call x1, Pallas kernels, beam_power(): pl.pallas_call(beam_kernel, out_shape=jax.ShapeDtypeStruct((CX * CY, CZ),...  68 us
    pallas_call x1, Pallas kernels, share_power(): pl.pallas_call(share_kernel, out_shape=jax.ShapeDtypeStruct((slots,) + pa...  20.7 us
    pallas_call x1, Pallas kernels, deblur_tile(): pl.pallas_call(deblur_kernel, out_shape=jax.ShapeDtypeStruct((planes, CX,...  13.3 us

profile of v11, /device:TPU:1, one launch (start us, length us, event | category | flops | bytes accessed | tf_op | source)
XLA Modules:
  0.0 109.4 jit_solution(13134090489388804615)
XLA Ops:
  0.6 1.6 %copy.17 = bf16[8,8,2,768]{3,1,2,0:T(8,128)(2,1)} copy(bf16[8,8,2,768]{3,2,1,0:T(2,128)(2,1)} %bitcast.16) | data formatting | bytes 393216 | tf_op jit(solution)/shard_map/reshape | solution.py:571
  2.2 68.0 %shard_map.59.part_ref = f32[256,128]{1,0:T(8,128)} custom-call(bf16[8,2,8,768]{3,2,1,0:T(8,128)(2,1)} %bitcast.14, s32[1,768]{1,0:T(1,128)} %lag_ref.1, bf16[3,768]{1,0:T(4,128)(2,1)} %bitcast.17), custom_call_target="tpu_custom_call" | custom-call | tf_op jit(solution)/shard_map/pallas_call | solution.py:261
  70.2 20.7 %shard_map.60 = f32[5,256,128]{2,1,0:T(8,128)} custom-call(f32[256,128]{1,0:T(8,128)} %shard_map.59.part_ref), custom_call_target="tpu_custom_call" | custom-call | tf_op jit(solution)/shard_map/pallas_call | solution.py:418
  91.0 1.2 %multiply_add_fusion = f32[5,256,128]{2,1,0:T(8,128)S(1)} fusion(f32[5,256,128]{2,1,0:T(8,128)} %shard_map.60), kind=kLoop, calls=%fused_computation.4 | loop fusion | flops 327680 | bytes 1310720 | tf_op jit(solution)/shard_map/add | solution.py:575
  92.1 0.1 fusion.2
  92.3 0.1 fusion
  92.3 0.9 copy.11
  93.2 13.3 %shard_map.61 = f32[8,32,128]{2,1,0:T(8,128)} custom-call(f32[3,17]{1,0:T(4,128)} %taps_ref.1, f32[8,160,128]{2,1,0:T(8,128)} %bitcast.13), custom_call_target="tpu_custom_call" | custom-call | tf_op jit(solution)/shard_map/pallas_call | solution.py:554
  106.5 1.1 %slice_maximum_fusion = (f32[2,8,32,64]{3,2,1,0:T(8,128)S(1)}, f32[2,8,32,64]{3,2,1,0:T(8,128)S(1)}) fusion(f32[1,8,32,128]{3,2,1,0:T(8,128)} %bitcast.15, f32[1,8,32,128]{3,2,1,0:T(8,128)S(1)} %fusion.1), kind=kLoop, calls=%fused_computation.6 | loop fusion | flops 65536 | bytes 524288 | tf_op jit(solution)/shard_map/stack | solution.py:581
  107.6 0.1 rev.7
  107.8 0.1 maximum_bitcast_fusion
  107.9 0.7 copy.13
  108.7 0.7 copy.12
  (3 shorter events, 0.1 us)

commit v12 on v11

--- a/solution.py
+++ b/solution.py
@@ -81,16 +81,34 @@
     return jnp.cos(angle), -jnp.sin(angle)
 
 
-def exchange_inputs(spec_ref, lag_ref, slow_ref, spec_in, lag_in, slow_in, local_sem, send_sem, recv_sem, then):
+def enter_barrier(count, reach):
+    me = lax.axis_index("sta")
+    tile = lax.axis_index("grid")
+    tiles = lax.axis_size("grid")
+    mesh_ids = pl.DeviceIdType.MESH
+    barrier = pltpu.get_barrier_semaphore()
+    for shift in range(1, count):
+        pl.semaphore_signal(barrier, inc=1, device_id=(tile, lax.rem(me + shift, count)), device_id_type=mesh_ids)
+    neighbours = jnp.int32(0)
+    for k in range(-reach, reach + 1):
+        if k == 0:
+            continue
+        there = (tile + k >= 0) & (tile + k < tiles)
+        neighbours = neighbours + there.astype(jnp.int32)
+
+        @pl.when(there)
+        def _():
+            pl.semaphore_signal(barrier, inc=1, device_id=(tile + k, me), device_id_type=mesh_ids)
+
+    pl.semaphore_wait(barrier, count - 1 + neighbours)
+
+
+def exchange_inputs(spec_ref, lag_ref, slow_ref, spec_in, lag_in, slow_in, local_sem, send_sem, recv_sem, then, reach):
     count = spec_in.shape[0]
     me = lax.axis_index("sta")
     tile = lax.axis_index("grid")
     mesh_ids = pl.DeviceIdType.MESH
-    barrier = pltpu.get_barrier_semaphore()
-    for shift in range(1, count):
-        peer = lax.rem(me + shift, count)
-        pl.semaphore_signal(barrier, inc=1, device_id=(tile, peer), device_id_type=mesh_ids)
-    pl.semaphore_wait(barrier, count - 1)
+    enter_barrier(count, reach)
     pairs = ((spec_ref, spec_in), (lag_ref, lag_in), (slow_ref, slow_in))
     local = []
     for kind, (source, target) in enumerate(pairs):
@@ -166,8 +184,9 @@
     )
 
 
-def beam_kernel(spec_ref, lag_ref, slow_ref, power_ref, spec_in, lag_in, slow_in, local_sem, send_sem, recv_sem,
-                real_ref, imag_ref, turn_ref, acc_ref, left_ref, right_ref):
+def beam_kernel(spec_ref, lag_ref, slow_ref, out_ref, spec_in, lag_in, slow_in, local_sem, send_sem, recv_sem,
+                real_ref, imag_ref, turn_ref, acc_ref, left_ref, right_ref, power_ref, pieces, send_rs, recv_rs,
+                send_ag, recv_ag, share_sem):
     count, bins, block = spec_in.shape[0], spec_in.shape[2], spec_in.shape[3]
     me = lax.axis_index("sta")
     first_bin = me * bins
@@ -230,7 +249,9 @@
         align_block(spec_ref[me], lag_ref[...], slow_ref[...], me, real_ref, imag_ref, turn_ref)
         lax.fori_loop(0, per_block, per_chunk, 0)
 
-    exchange_inputs(spec_ref, lag_ref, slow_ref, spec_in, lag_in, slow_in, local_sem, send_sem, recv_sem, own_block)
+    exchange_inputs(
+        spec_ref, lag_ref, slow_ref, spec_in, lag_in, slow_in, local_sem, send_sem, recv_sem, own_block, out_ref.shape[0] // 2
+    )
 
     def align_other(shift, carry):
         source = lax.rem(me + shift, count)
@@ -250,17 +271,20 @@
         high = high + ((u + v) * (u + v) + (x - w) * (x - w))
     power_ref[:, :half_z] = low
     power_ref[:, half_z:] = high
-
-
-def beam_power(spec_send, lag_row, slow_rows):
+    share_kernel(power_ref, out_ref, pieces, send_rs, recv_rs, send_ag, recv_ag, share_sem)
+
+
+def beam_power(spec_send, lag_row, slow_rows, reach):
     count = spec_send.shape[0]
+    slots = 2 * reach + 1
+    cells = CX * CY
     bins, block = spec_send.shape[2], spec_send.shape[3]
     width = CHUNK
     stations = count * block
     vmem = pl.BlockSpec(memory_space=pltpu.VMEM)
     return pl.pallas_call(
         beam_kernel,
-        out_shape=jax.ShapeDtypeStruct((CX * CY, CZ), jnp.float32),
+        out_shape=jax.ShapeDtypeStruct((slots, cells, CZ), jnp.float32),
         in_specs=[vmem, vmem, vmem],
         out_specs=vmem,
         scratch_shapes=[
@@ -276,6 +300,13 @@
             pltpu.VMEM((bins, 2 * CX * CY, CZ), jnp.float32),
             pltpu.VMEM((2 * CX * CY, width), jnp.bfloat16),
             pltpu.VMEM((CZ, width), jnp.bfloat16),
+            pltpu.VMEM((cells, CZ), jnp.float32),
+            pltpu.VMEM((count, cells // count, CZ), jnp.float32),
+            pltpu.SemaphoreType.DMA((count,)),
+            pltpu.SemaphoreType.DMA((count,)),
+            pltpu.SemaphoreType.DMA((slots, count)),
+            pltpu.SemaphoreType.DMA((slots, count)),
+            pltpu.SemaphoreType.DMA((1,)),
         ],
         compiler_params=pltpu.CompilerParams(collective_id=1, has_side_effects=True),
     )(spec_send, lag_row, slow_rows)
@@ -290,21 +321,6 @@
     tile = lax.axis_index("grid")
     tiles = lax.axis_size("grid")
     mesh_ids = pl.DeviceIdType.MESH
-    barrier = pltpu.get_barrier_semaphore()
-    for shift in range(1, count):
-        pl.semaphore_signal(barrier, inc=1, device_id=(tile, lax.rem(me + shift, count)), device_id_type=mesh_ids)
-    neighbours = jnp.int32(0)
-    for k in range(-reach, reach + 1):
-        if k == 0:
-            continue
-        there = (tile + k >= 0) & (tile + k < tiles)
-        neighbours = neighbours + there.astype(jnp.int32)
-
-        @pl.when(there)
-        def _():
-            pl.semaphore_signal(barrier, inc=1, device_id=(tile + k, me), device_id_type=mesh_ids)
-
-    pl.semaphore_wait(barrier, count - 1 + neighbours)
     own = pltpu.make_async_copy(part_ref.at[pl.ds(pl.multiple_of(me * rows, 8), rows)], pieces.at[me], local_sem.at[0])
     own.start()
     sends = []
@@ -569,9 +585,8 @@
     first_bin = lax.axis_index("sta") * own_count
     block = spectra.shape[2]
     spec_send = spectra.reshape(groups, own_count, 2, block).transpose(0, 2, 1, 3)
-    local_power = beam_power(spec_send, lag_samples, slowness[0])
     halo_tiles = -(-(ITERS * 2 * HALF) // CX)
-    summed = share_power(local_power, halo_tiles)
+    summed = beam_power(spec_send, lag_samples, slowness[0], halo_tiles)
     observed = summed / (FREQS * STATIONS) + BACKGROUND
     slots = observed.shape[0]
     observed = observed.reshape(slots, CY, CX, CZ)

time: 110 us -> 106 us (0.964)
  Pallas kernels: 102 us -> 98.6 us
    pallas_call x2 -> x1, Pallas kernels: 88.7 us -> 85.4 us  [beam_power(): pl.pallas_call(beam_kernel, out_shape=jax.ShapeDtypeStruct((slots, cells,...]
where the time goes in v12:
time: 106 us
  Pallas kernels  98.6 us (93%)
  local copies, waits for them, and re-layouts  4.23 us (4%)
  other arithmetic  2.51 us (2%)
    pallas_call x1, Pallas kernels, beam_power(): pl.pallas_call(beam_kernel, out_shape=jax.ShapeDtypeStruct((slots, cells,...  85.4 us
    pallas_call x1, Pallas kernels, deblur_tile(): pl.pallas_call(deblur_kernel, out_shape=jax.ShapeDtypeStruct((planes, CX,...  13.3 us

profile of v12, /device:TPU:1, one launch (start us, length us, event | category | flops | bytes accessed | tf_op | source)
XLA Modules:
  0.0 106.1 jit_solution(7570873823824290516)
XLA Ops:
  0.6 1.6 %copy.17 = bf16[8,8,2,768]{3,1,2,0:T(8,128)(2,1)} copy(bf16[8,8,2,768]{3,2,1,0:T(2,128)(2,1)} %bitcast.16) | data formatting | bytes 393216 | tf_op jit(solution)/shard_map/reshape | solution.py:587
  2.3 85.4 %shard_map.59 = f32[5,256,128]{2,1,0:T(8,128)} custom-call(bf16[8,2,8,768]{3,2,1,0:T(8,128)(2,1)} %bitcast.14, s32[1,768]{1,0:T(1,128)} %lag_ref.1, bf16[3,768]{1,0:T(4,128)(2,1)} %bitcast.17), custom_call_target="tpu_custom_call" | custom-call | tf_op jit(solution)/shard_map/pallas_call | solution.py:285
  87.6 1.2 %multiply_add_fusion = f32[5,256,128]{2,1,0:T(8,128)S(1)} fusion(f32[5,256,128]{2,1,0:T(8,128)} %shard_map.59), kind=kLoop, calls=%fused_computation.4 | loop fusion | flops 327680 | bytes 1310720 | tf_op jit(solution)/shard_map/add | solution.py:590
  88.8 0.1 fusion.2
  88.9 0.1 fusion
  89.0 0.9 copy.11
  89.9 13.3 %shard_map.60 = f32[8,32,128]{2,1,0:T(8,128)} custom-call(f32[3,17]{1,0:T(4,128)} %taps_ref.1, f32[8,160,128]{2,1,0:T(8,128)} %bitcast.13), custom_call_target="tpu_custom_call" | custom-call | tf_op jit(solution)/shard_map/pallas_call | solution.py:570
  103.2 1.1 %slice_maximum_fusion = (f32[2,8,32,64]{3,2,1,0:T(8,128)S(1)}, f32[2,8,32,64]{3,2,1,0:T(8,128)S(1)}) fusion(f32[1,8,32,128]{3,2,1,0:T(8,128)} %bitcast.15, f32[1,8,32,128]{3,2,1,0:T(8,128)S(1)} %fusion.1), kind=kLoop, calls=%fused_computation.6 | loop fusion | flops 65536 | bytes 524288 | tf_op jit(solution)/shard_map/stack | solution.py:596
  104.3 0.1 rev.7
  104.4 0.1 maximum_bitcast_fusion
  104.6 0.7 copy.13
  105.3 0.7 copy.12
  (3 shorter events, 0.1 us)

commit v13 on v12

--- a/solution.py
+++ b/solution.py
@@ -533,35 +533,39 @@
         cell = (me - halo_tiles) * CX + low + lax.broadcasted_iota(jnp.int32, (size, depth), 0)
         return (cell >= 0) & (cell < tiles * CX)
 
+    lanes = planes * depth
+
     def blur(volume):
-        size_in = volume[0].shape[0]
+        size_in = volume.shape[0]
         size_out = size_in - 2 * HALF
         band = kx_ref[0:size_out, 0:size_in]
-        along_x = [jnp.dot(band, plane, precision=highest, preferred_element_type=jnp.float32) for plane in volume]
+        along_x = jnp.dot(band, volume, precision=highest, preferred_element_type=jnp.float32)
         along_y = []
         for y in range(planes):
             total = None
             for q in range(planes):
-                term = taps_ref[1, q - y + HALF] * along_x[q]
+                term = taps_ref[1, q - y + HALF] * along_x[:, q * depth : (q + 1) * depth]
                 total = term if total is None else total + term
             along_y.append(total)
         joined = jnp.concatenate(along_y, axis=0)
         along_z = jnp.dot(joined, kz_ref[...], precision=highest, preferred_element_type=jnp.float32)
-        return [along_z[y * size_out : (y + 1) * size_out] for y in range(planes)]
-
-    observed = [obs_ref[y] for y in range(planes)]
-    mask = inside(0, width)
-    estimate = [jnp.where(mask, plane, 0.0) for plane in observed]
+        return jnp.concatenate([along_z[y * size_out : (y + 1) * size_out] for y in range(planes)], axis=1)
+
+    def inside_wide(low, size):
+        cell = (me - halo_tiles) * CX + low + lax.broadcasted_iota(jnp.int32, (size, lanes), 0)
+        return (cell >= 0) & (cell < tiles * CX)
+
+    observed = jnp.concatenate([obs_ref[y] for y in range(planes)], axis=1)
+    estimate = jnp.where(inside_wide(0, width), observed, 0.0)
     for sweep in range(ITERS):
         low = 2 * HALF * sweep + HALF
         blurred = blur(estimate)
-        size = blurred[0].shape[0]
-        mask = inside(low, size)
-        ratio = [jnp.where(mask, observed[y][low : low + size] / blurred[y], 0.0) for y in range(planes)]
+        size = blurred.shape[0]
+        ratio = jnp.where(inside_wide(low, size), observed[low : low + size] / blurred, 0.0)
         spread = blur(ratio)
-        estimate = [estimate[y][2 * HALF : 2 * HALF + spread[y].shape[0]] * spread[y] for y in range(planes)]
+        estimate = estimate[2 * HALF : 2 * HALF + spread.shape[0]] * spread
     for y in range(planes):
-        out_ref[y] = estimate[y]
+        out_ref[y] = estimate[:, y * depth : (y + 1) * depth]
 
 
 def deblur_tile(observed, spread_taps):

time: 106 us -> 105 us (level)
  Pallas kernels: 98.6 us -> 97.5 us
    pallas_call x1, Pallas kernels: 13.3 us -> 12.1 us  [deblur_tile(): pl.pallas_call(deblur_kernel, out_shape=jax.ShapeDtypeStruct((planes, CX,...]
where the time goes in v13:
time: 105 us
  Pallas kernels  97.5 us (93%)
  local copies, waits for them, and re-layouts  4.23 us (4%)
  other arithmetic  2.51 us (2%)
    pallas_call x1, Pallas kernels, beam_power(): pl.pallas_call(beam_kernel, out_shape=jax.ShapeDtypeStruct((slots, cells,...  85.4 us
    pallas_call x1, Pallas kernels, deblur_tile(): pl.pallas_call(deblur_kernel, out_shape=jax.ShapeDtypeStruct((planes, CX,...  12.1 us

profile of v13, /device:TPU:1, one launch (start us, length us, event | category | flops | bytes accessed | tf_op | source)
XLA Modules:
  0.0 104.9 jit_solution(196010785147015160)
XLA Ops:
  0.6 1.6 %copy.17 = bf16[8,8,2,768]{3,1,2,0:T(8,128)(2,1)} copy(bf16[8,8,2,768]{3,2,1,0:T(2,128)(2,1)} %bitcast.16) | data formatting | bytes 393216 | tf_op jit(solution)/shard_map/reshape | solution.py:591
  2.3 85.4 %shard_map.59 = f32[5,256,128]{2,1,0:T(8,128)} custom-call(bf16[8,2,8,768]{3,2,1,0:T(8,128)(2,1)} %bitcast.14, s32[1,768]{1,0:T(1,128)} %lag_ref.1, bf16[3,768]{1,0:T(4,128)(2,1)} %bitcast.17), custom_call_target="tpu_custom_call" | custom-call | tf_op jit(solution)/shard_map/pallas_call | solution.py:285
  87.6 1.2 %multiply_add_fusion = f32[5,256,128]{2,1,0:T(8,128)S(1)} fusion(f32[5,256,128]{2,1,0:T(8,128)} %shard_map.59), kind=kLoop, calls=%fused_computation.4 | loop fusion | flops 327680 | bytes 1310720 | tf_op jit(solution)/shard_map/add | solution.py:594
  88.8 0.1 fusion.2
  88.9 0.1 fusion
  89.0 0.9 copy.11
  89.9 12.1 %shard_map.60 = f32[8,32,128]{2,1,0:T(8,128)} custom-call(f32[3,17]{1,0:T(4,128)} %taps_ref.1, f32[8,160,128]{2,1,0:T(8,128)} %bitcast.13), custom_call_target="tpu_custom_call" | custom-call | tf_op jit(solution)/shard_map/pallas_call | solution.py:574
  102.0 1.1 %slice_maximum_fusion = (f32[2,8,32,64]{3,2,1,0:T(8,128)S(1)}, f32[2,8,32,64]{3,2,1,0:T(8,128)S(1)}) fusion(f32[1,8,32,128]{3,2,1,0:T(8,128)} %bitcast.15, f32[1,8,32,128]{3,2,1,0:T(8,128)S(1)} %fusion.1), kind=kLoop, calls=%fused_computation.6 | loop fusion | flops 65536 | bytes 524288 | tf_op jit(solution)/shard_map/stack | solution.py:600
  103.1 0.1 rev.7
  103.3 0.1 maximum_bitcast_fusion
  103.5 0.7 copy.13
  104.2 0.7 copy.12
  (3 shorter events, 0.1 us)

commit v14 on v13

--- a/solution.py
+++ b/solution.py
@@ -74,7 +74,7 @@
     return jnp.dot(left_side, right_side, preferred_element_type=jnp.float32)
 
 
-CHUNK = 256
+CHUNK = 384
 
 
 def exp_neg(angle):

time: 105 us -> 98.1 us (0.934)
  Pallas kernels: 97.5 us -> 90.4 us
    pallas_call x1, Pallas kernels: 85.4 us -> 78.2 us  [beam_power(): pl.pallas_call(beam_kernel, out_shape=jax.ShapeDtypeStruct((slots, cells,...]
where the time goes in v14:
time: 98.1 us; the launch traced here: 97.8 us
  Pallas kernels  90.4 us (92%)
  local copies, waits for them, and re-layouts  4.23 us (4%)
  other arithmetic  2.51 us (3%)
    pallas_call x1, Pallas kernels, beam_power(): pl.pallas_call(beam_kernel, out_shape=jax.ShapeDtypeStruct((slots, cells,...  78.2 us
    pallas_call x1, Pallas kernels, deblur_tile(): pl.pallas_call(deblur_kernel, out_shape=jax.ShapeDtypeStruct((planes, CX,...  12.1 us

profile of v14, /device:TPU:1, one launch (start us, length us, event | category | flops | bytes accessed | tf_op | source)
XLA Modules:
  0.0 97.8 jit_solution(9969876599789126272)
XLA Ops:
  0.6 1.6 %copy.17 = bf16[8,8,2,768]{3,1,2,0:T(8,128)(2,1)} copy(bf16[8,8,2,768]{3,2,1,0:T(2,128)(2,1)} %bitcast.16) | data formatting | bytes 393216 | tf_op jit(solution)/shard_map/reshape | solution.py:591
  2.3 78.2 %shard_map.59 = f32[5,256,128]{2,1,0:T(8,128)} custom-call(bf16[8,2,8,768]{3,2,1,0:T(8,128)(2,1)} %bitcast.14, s32[1,768]{1,0:T(1,128)} %lag_ref.1, bf16[3,768]{1,0:T(4,128)(2,1)} %bitcast.17), custom_call_target="tpu_custom_call" | custom-call | tf_op jit(solution)/shard_map/pallas_call | solution.py:285
  80.5 1.2 %multiply_add_fusion = f32[5,256,128]{2,1,0:T(8,128)S(1)} fusion(f32[5,256,128]{2,1,0:T(8,128)} %shard_map.59), kind=kLoop, calls=%fused_computation.4 | loop fusion | flops 327680 | bytes 1310720 | tf_op jit(solution)/shard_map/add | solution.py:594
  81.7 0.1 fusion.2
  81.8 0.1 fusion
  81.9 0.9 copy.11
  82.8 12.1 %shard_map.60 = f32[8,32,128]{2,1,0:T(8,128)} custom-call(f32[3,17]{1,0:T(4,128)} %taps_ref.1, f32[8,160,128]{2,1,0:T(8,128)} %bitcast.13), custom_call_target="tpu_custom_call" | custom-call | tf_op jit(solution)/shard_map/pallas_call | solution.py:574
  94.9 1.1 %slice_maximum_fusion = (f32[2,8,32,64]{3,2,1,0:T(8,128)S(1)}, f32[2,8,32,64]{3,2,1,0:T(8,128)S(1)}) fusion(f32[1,8,32,128]{3,2,1,0:T(8,128)} %bitcast.15, f32[1,8,32,128]{3,2,1,0:T(8,128)S(1)} %fusion.1), kind=kLoop, calls=%fused_computation.6 | loop fusion | flops 65536 | bytes 524288 | tf_op jit(solution)/shard_map/stack | solution.py:600
  96.0 0.1 rev.7
  96.2 0.1 maximum_bitcast_fusion
  96.3 0.7 copy.13
  97.1 0.7 copy.12
  (3 shorter events, 0.1 us)

commit v15 on v14

--- a/solution.py
+++ b/solution.py
@@ -74,7 +74,7 @@
     return jnp.dot(left_side, right_side, preferred_element_type=jnp.float32)
 
 
-CHUNK = 384
+CHUNK = 768
 
 
 def exp_neg(angle):

time: 98.1 us -> 88.2 us (0.90)
  Pallas kernels: 90.4 us -> 80.5 us
    pallas_call x1, Pallas kernels: 78.2 us -> 68.4 us  [beam_power(): pl.pallas_call(beam_kernel, out_shape=jax.ShapeDtypeStruct((slots, cells,...]
where the time goes in v15:
time: 88.2 us; the launch traced here: 88 us
  Pallas kernels  80.5 us (91%)
  local copies, waits for them, and re-layouts  4.23 us (5%)
  other arithmetic  2.51 us (3%)
    pallas_call x1, Pallas kernels, beam_power(): pl.pallas_call(beam_kernel, out_shape=jax.ShapeDtypeStruct((slots, cells,...  68.4 us
    pallas_call x1, Pallas kernels, deblur_tile(): pl.pallas_call(deblur_kernel, out_shape=jax.ShapeDtypeStruct((planes, CX,...  12.1 us

profile of v15, /device:TPU:1, one launch (start us, length us, event | category | flops | bytes accessed | tf_op | source)
XLA Modules:
  0.0 88.0 jit_solution(1238521316173716370)
XLA Ops:
  0.6 1.6 %copy.17 = bf16[8,8,2,768]{3,1,2,0:T(8,128)(2,1)} copy(bf16[8,8,2,768]{3,2,1,0:T(2,128)(2,1)} %bitcast.16) | data formatting | bytes 393216 | tf_op jit(solution)/shard_map/reshape | solution.py:591
  2.3 68.4 %shard_map.59 = f32[5,256,128]{2,1,0:T(8,128)} custom-call(bf16[8,2,8,768]{3,2,1,0:T(8,128)(2,1)} %bitcast.14, s32[1,768]{1,0:T(1,128)} %lag_ref.1, bf16[3,768]{1,0:T(4,128)(2,1)} %bitcast.17), custom_call_target="tpu_custom_call" | custom-call | tf_op jit(solution)/shard_map/pallas_call | solution.py:285
  70.7 1.2 %multiply_add_fusion = f32[5,256,128]{2,1,0:T(8,128)S(1)} fusion(f32[5,256,128]{2,1,0:T(8,128)} %shard_map.59), kind=kLoop, calls=%fused_computation.4 | loop fusion | flops 327680 | bytes 1310720 | tf_op jit(solution)/shard_map/add | solution.py:594
  71.8 0.1 fusion.2
  72.0 0.1 fusion
  72.1 0.9 %copy.11 = f32[8,5,32,128]{3,2,1,0:T(8,128)} copy(f32[8,5,32,128]{3,2,0,1:T(8,128)S(1)} %fusion) | data formatting | bytes 1310720 | tf_op jit(solution)/shard_map/transpose | solution.py:598
  72.9 12.1 %shard_map.60 = f32[8,32,128]{2,1,0:T(8,128)} custom-call(f32[3,17]{1,0:T(4,128)} %taps_ref.1, f32[8,160,128]{2,1,0:T(8,128)} %bitcast.13), custom_call_target="tpu_custom_call" | custom-call | tf_op jit(solution)/shard_map/pallas_call | solution.py:574
  85.1 1.1 %slice_maximum_fusion = (f32[2,8,32,64]{3,2,1,0:T(8,128)S(1)}, f32[2,8,32,64]{3,2,1,0:T(8,128)S(1)}) fusion(f32[1,8,32,128]{3,2,1,0:T(8,128)} %bitcast.15, f32[1,8,32,128]{3,2,1,0:T(8,128)S(1)} %fusion.1), kind=kLoop, calls=%fused_computation.6 | loop fusion | flops 65536 | bytes 524288 | tf_op jit(solution)/shard_map/stack | solution.py:600
  86.2 0.1 rev.7
  86.3 0.1 maximum_bitcast_fusion
  86.5 0.7 copy.13
  87.2 0.7 copy.12
  (3 shorter events, 0.1 us)

commit v16 on v15

--- a/solution.py
+++ b/solution.py
@@ -242,7 +242,7 @@
             )
             return tuple(complex_times(now, turn) for now, turn in zip(state, ratio))
 
-        lax.fori_loop(0, bins, per_bin, start)
+        lax.fori_loop(0, bins, per_bin, start, unroll=2)
         return carry
 
     def own_block():

time: 88.2 us -> 84.5 us (0.958)
  Pallas kernels: 80.5 us -> 76.8 us
    pallas_call x1, Pallas kernels: 68.4 us -> 64.6 us  [beam_power(): pl.pallas_call(beam_kernel, out_shape=jax.ShapeDtypeStruct((slots, cells,...]
where the time goes in v16:
time: 84.5 us; the launch traced here: 84.2 us
  Pallas kernels  76.8 us (91%)
  local copies, waits for them, and re-layouts  4.23 us (5%)
  other arithmetic  2.51 us (3%)
    pallas_call x1, Pallas kernels, beam_power(): pl.pallas_call(beam_kernel, out_shape=jax.ShapeDtypeStruct((slots, cells,...  64.6 us
    pallas_call x1, Pallas kernels, deblur_tile(): pl.pallas_call(deblur_kernel, out_shape=jax.ShapeDtypeStruct((planes, CX,...  12.1 us

profile of v16, /device:TPU:1, one launch (start us, length us, event | category | flops | bytes accessed | tf_op | source)
XLA Modules:
  0.0 84.2 jit_solution(13946038726098704137)
XLA Ops:
  0.6 1.6 %copy.17 = bf16[8,8,2,768]{3,1,2,0:T(8,128)(2,1)} copy(bf16[8,8,2,768]{3,2,1,0:T(2,128)(2,1)} %bitcast.16) | data formatting | bytes 393216 | tf_op jit(solution)/shard_map/reshape | solution.py:591
  2.3 64.6 %shard_map.59 = f32[5,256,128]{2,1,0:T(8,128)} custom-call(bf16[8,2,8,768]{3,2,1,0:T(8,128)(2,1)} %bitcast.14, s32[1,768]{1,0:T(1,128)} %lag_ref.1, bf16[3,768]{1,0:T(4,128)(2,1)} %bitcast.17), custom_call_target="tpu_custom_call" | custom-call | tf_op jit(solution)/shard_map/pallas_call | solution.py:285
  66.9 1.2 %multiply_add_fusion = f32[5,256,128]{2,1,0:T(8,128)S(1)} fusion(f32[5,256,128]{2,1,0:T(8,128)} %shard_map.59), kind=kLoop, calls=%fused_computation.4 | loop fusion | flops 327680 | bytes 1310720 | tf_op jit(solution)/shard_map/add | solution.py:594
  68.1 0.1 fusion.2
  68.2 0.1 fusion
  68.3 0.9 %copy.11 = f32[8,5,32,128]{3,2,1,0:T(8,128)} copy(f32[8,5,32,128]{3,2,0,1:T(8,128)S(1)} %fusion) | data formatting | bytes 1310720 | tf_op jit(solution)/shard_map/transpose | solution.py:598
  69.2 12.1 %shard_map.60 = f32[8,32,128]{2,1,0:T(8,128)} custom-call(f32[3,17]{1,0:T(4,128)} %taps_ref.1, f32[8,160,128]{2,1,0:T(8,128)} %bitcast.13), custom_call_target="tpu_custom_call" | custom-call | tf_op jit(solution)/shard_map/pallas_call | solution.py:574
  81.3 1.1 %slice_maximum_fusion = (f32[2,8,32,64]{3,2,1,0:T(8,128)S(1)}, f32[2,8,32,64]{3,2,1,0:T(8,128)S(1)}) fusion(f32[1,8,32,128]{3,2,1,0:T(8,128)} %bitcast.15, f32[1,8,32,128]{3,2,1,0:T(8,128)S(1)} %fusion.1), kind=kLoop, calls=%fused_computation.6 | loop fusion | flops 65536 | bytes 524288 | tf_op jit(solution)/shard_map/stack | solution.py:600
  82.4 0.1 rev.7
  82.6 0.1 maximum_bitcast_fusion
  82.8 0.7 copy.13
  83.5 0.7 copy.12
  (3 shorter events, 0.1 us)

commit v17 on v16

--- a/solution.py
+++ b/solution.py
@@ -242,7 +242,7 @@
             )
             return tuple(complex_times(now, turn) for now, turn in zip(state, ratio))
 
-        lax.fori_loop(0, bins, per_bin, start, unroll=2)
+        lax.fori_loop(0, bins, per_bin, start, unroll=4)
         return carry
 
     def own_block():

time: 84.5 us -> 83.7 us (level)
  no operation moved by 1% of the time
where the time goes in v17:
time: 83.7 us; the launch traced here: 83.5 us
  Pallas kernels  76.1 us (91%)
  local copies, waits for them, and re-layouts  4.23 us (5%)
  other arithmetic  2.51 us (3%)
    pallas_call x1, Pallas kernels, beam_power(): pl.pallas_call(beam_kernel, out_shape=jax.ShapeDtypeStruct((slots, cells,...  63.9 us
    pallas_call x1, Pallas kernels, deblur_tile(): pl.pallas_call(deblur_kernel, out_shape=jax.ShapeDtypeStruct((planes, CX,...  12.1 us

profile of v17, /device:TPU:1, one launch (start us, length us, event | category | flops | bytes accessed | tf_op | source)
XLA Modules:
  0.0 83.5 jit_solution(13714255699197041945)
XLA Ops:
  0.6 1.6 %copy.17 = bf16[8,8,2,768]{3,1,2,0:T(8,128)(2,1)} copy(bf16[8,8,2,768]{3,2,1,0:T(2,128)(2,1)} %bitcast.16) | data formatting | bytes 393216 | tf_op jit(solution)/shard_map/reshape | solution.py:591
  2.3 63.9 %shard_map.59 = f32[5,256,128]{2,1,0:T(8,128)} custom-call(bf16[8,2,8,768]{3,2,1,0:T(8,128)(2,1)} %bitcast.14, s32[1,768]{1,0:T(1,128)} %lag_ref.1, bf16[3,768]{1,0:T(4,128)(2,1)} %bitcast.17), custom_call_target="tpu_custom_call" | custom-call | tf_op jit(solution)/shard_map/pallas_call | solution.py:285
  66.2 1.2 %multiply_add_fusion = f32[5,256,128]{2,1,0:T(8,128)S(1)} fusion(f32[5,256,128]{2,1,0:T(8,128)} %shard_map.59), kind=kLoop, calls=%fused_computation.4 | loop fusion | flops 327680 | bytes 1310720 | tf_op jit(solution)/shard_map/add | solution.py:594
  67.4 0.1 fusion.2
  67.5 0.1 fusion
  67.6 0.9 %copy.11 = f32[8,5,32,128]{3,2,1,0:T(8,128)} copy(f32[8,5,32,128]{3,2,0,1:T(8,128)S(1)} %fusion) | data formatting | bytes 1310720 | tf_op jit(solution)/shard_map/transpose | solution.py:598
  68.5 12.1 %shard_map.60 = f32[8,32,128]{2,1,0:T(8,128)} custom-call(f32[3,17]{1,0:T(4,128)} %taps_ref.1, f32[8,160,128]{2,1,0:T(8,128)} %bitcast.13), custom_call_target="tpu_custom_call" | custom-call | tf_op jit(solution)/shard_map/pallas_call | solution.py:574
  80.6 1.1 %slice_maximum_fusion = (f32[2,8,32,64]{3,2,1,0:T(8,128)S(1)}, f32[2,8,32,64]{3,2,1,0:T(8,128)S(1)}) fusion(f32[1,8,32,128]{3,2,1,0:T(8,128)} %bitcast.15, f32[1,8,32,128]{3,2,1,0:T(8,128)S(1)} %fusion.1), kind=kLoop, calls=%fused_computation.6 | loop fusion | flops 65536 | bytes 524288 | tf_op jit(solution)/shard_map/stack | solution.py:600
  81.7 0.1 rev.7
  81.8 0.1 maximum_bitcast_fusion
  82.0 0.7 copy.13
  82.8 0.7 copy.12
  (3 shorter events, 0.1 us)

commit v18 on v17

--- a/solution.py
+++ b/solution.py
@@ -258,7 +258,7 @@
         align_block(spec_in[source], lag_in[source], slow_in[source], source, real_ref, imag_ref, turn_ref)
         return carry
 
-    lax.fori_loop(1, count, align_other, 0)
+    lax.fori_loop(1, count, align_other, 0, unroll=True)
     lax.fori_loop(per_block, count * per_block, per_chunk, 0)
     cells = CX * CY
     low = jnp.zeros((cells, half_z), jnp.float32)

time: 83.7 us -> 83.6 us (level)
  no operation moved by 1% of the time
where the time goes in v18:
time: 83.6 us; the launch traced here: 83.4 us
  Pallas kernels  75.9 us (91%)
  local copies, waits for them, and re-layouts  4.23 us (5%)
  other arithmetic  2.51 us (3%)
    pallas_call x1, Pallas kernels, beam_power(): pl.pallas_call(beam_kernel, out_shape=jax.ShapeDtypeStruct((slots, cells,...  63.8 us
    pallas_call x1, Pallas kernels, deblur_tile(): pl.pallas_call(deblur_kernel, out_shape=jax.ShapeDtypeStruct((planes, CX,...  12.1 us

profile of v18, /device:TPU:1, one launch (start us, length us, event | category | flops | bytes accessed | tf_op | source)
XLA Modules:
  0.0 83.4 jit_solution(18042703806963471923)
XLA Ops:
  0.6 1.6 %copy.17 = bf16[8,8,2,768]{3,1,2,0:T(8,128)(2,1)} copy(bf16[8,8,2,768]{3,2,1,0:T(2,128)(2,1)} %bitcast.16) | data formatting | bytes 393216 | tf_op jit(solution)/shard_map/reshape | solution.py:591
  2.3 63.8 %shard_map.59 = f32[5,256,128]{2,1,0:T(8,128)} custom-call(bf16[8,2,8,768]{3,2,1,0:T(8,128)(2,1)} %bitcast.14, s32[1,768]{1,0:T(1,128)} %lag_ref.1, bf16[3,768]{1,0:T(4,128)(2,1)} %bitcast.17), custom_call_target="tpu_custom_call" | custom-call | tf_op jit(solution)/shard_map/pallas_call | solution.py:285
  66.1 1.2 %multiply_add_fusion = f32[5,256,128]{2,1,0:T(8,128)S(1)} fusion(f32[5,256,128]{2,1,0:T(8,128)} %shard_map.59), kind=kLoop, calls=%fused_computation.4 | loop fusion | flops 327680 | bytes 1310720 | tf_op jit(solution)/shard_map/add | solution.py:594
  67.2 0.1 fusion.2
  67.4 0.1 fusion
  67.5 0.9 %copy.11 = f32[8,5,32,128]{3,2,1,0:T(8,128)} copy(f32[8,5,32,128]{3,2,0,1:T(8,128)S(1)} %fusion) | data formatting | bytes 1310720 | tf_op jit(solution)/shard_map/transpose | solution.py:598
  68.4 12.1 %shard_map.60 = f32[8,32,128]{2,1,0:T(8,128)} custom-call(f32[3,17]{1,0:T(4,128)} %taps_ref.1, f32[8,160,128]{2,1,0:T(8,128)} %bitcast.13), custom_call_target="tpu_custom_call" | custom-call | tf_op jit(solution)/shard_map/pallas_call | solution.py:574
  80.5 1.1 %slice_maximum_fusion = (f32[2,8,32,64]{3,2,1,0:T(8,128)S(1)}, f32[2,8,32,64]{3,2,1,0:T(8,128)S(1)}) fusion(f32[1,8,32,128]{3,2,1,0:T(8,128)} %bitcast.15, f32[1,8,32,128]{3,2,1,0:T(8,128)S(1)} %fusion.1), kind=kLoop, calls=%fused_computation.6 | loop fusion | flops 65536 | bytes 524288 | tf_op jit(solution)/shard_map/stack | solution.py:600
  81.6 0.1 rev.7
  81.7 0.1 maximum_bitcast_fusion
  81.9 0.7 copy.13
  82.6 0.7 copy.12
  (3 shorter events, 0.1 us)

commit v19 on v17

--- a/solution.py
+++ b/solution.py
@@ -527,7 +527,7 @@
         mirror(lax.broadcasted_iota(jnp.int32, shape_z, 0), depth),
     )
     halo_tiles = (width - CX) // (2 * CX)
-    highest = lax.Precision.HIGHEST
+    highest = lax.Precision.HIGH
 
     def inside(low, size):
         cell = (me - halo_tiles) * CX + low + lax.broadcasted_iota(jnp.int32, (size, depth), 0)

time: 83.7 us -> 79.4 us (0.949)
  Pallas kernels: 76.1 us -> 71.8 us
    pallas_call x1, Pallas kernels: 12.1 us -> 7.85 us  [deblur_tile(): pl.pallas_call(deblur_kernel, out_shape=jax.ShapeDtypeStruct((planes, CX,...]
where the time goes in v19:
time: 79.4 us; the launch traced here: 79.2 us
  Pallas kernels  71.8 us (90%)
  local copies, waits for them, and re-layouts  4.23 us (5%)
  other arithmetic  2.51 us (3%)
    pallas_call x1, Pallas kernels, beam_power(): pl.pallas_call(beam_kernel, out_shape=jax.ShapeDtypeStruct((slots, cells,...  63.9 us
    pallas_call x1, Pallas kernels, deblur_tile(): pl.pallas_call(deblur_kernel, out_shape=jax.ShapeDtypeStruct((planes, CX,...  7.85 us
    reshape x1, local copies, waits for them, and re-layouts, per_device(): spectra.reshape(groups, own_count, 2, block).transpose(0, 2, 1, 3)  1.62 us

profile of v19, /device:TPU:1, one launch (start us, length us, event | category | flops | bytes accessed | tf_op | source)
XLA Modules:
  0.0 79.2 jit_solution(3540244397903194982)
XLA Ops:
  0.6 1.6 %copy.17 = bf16[8,8,2,768]{3,1,2,0:T(8,128)(2,1)} copy(bf16[8,8,2,768]{3,2,1,0:T(2,128)(2,1)} %bitcast.16) | data formatting | bytes 393216 | tf_op jit(solution)/shard_map/reshape | solution.py:591
  2.3 63.9 %shard_map.59 = f32[5,256,128]{2,1,0:T(8,128)} custom-call(bf16[8,2,8,768]{3,2,1,0:T(8,128)(2,1)} %bitcast.14, s32[1,768]{1,0:T(1,128)} %lag_ref.1, bf16[3,768]{1,0:T(4,128)(2,1)} %bitcast.17), custom_call_target="tpu_custom_call" | custom-call | tf_op jit(solution)/shard_map/pallas_call | solution.py:285
  66.2 1.2 %multiply_add_fusion = f32[5,256,128]{2,1,0:T(8,128)S(1)} fusion(f32[5,256,128]{2,1,0:T(8,128)} %shard_map.59), kind=kLoop, calls=%fused_computation.4 | loop fusion | flops 327680 | bytes 1310720 | tf_op jit(solution)/shard_map/add | solution.py:594
  67.4 0.1 fusion.2
  67.5 0.1 fusion
  67.6 0.9 %copy.11 = f32[8,5,32,128]{3,2,1,0:T(8,128)} copy(f32[8,5,32,128]{3,2,0,1:T(8,128)S(1)} %fusion) | data formatting | bytes 1310720 | tf_op jit(solution)/shard_map/transpose | solution.py:598
  68.5 7.8 %shard_map.60 = f32[8,32,128]{2,1,0:T(8,128)} custom-call(f32[3,17]{1,0:T(4,128)} %taps_ref.1, f32[8,160,128]{2,1,0:T(8,128)} %bitcast.13), custom_call_target="tpu_custom_call" | custom-call | tf_op jit(solution)/shard_map/pallas_call | solution.py:574
  76.3 1.1 %slice_maximum_fusion = (f32[2,8,32,64]{3,2,1,0:T(8,128)S(1)}, f32[2,8,32,64]{3,2,1,0:T(8,128)S(1)}) fusion(f32[1,8,32,128]{3,2,1,0:T(8,128)} %bitcast.15, f32[1,8,32,128]{3,2,1,0:T(8,128)S(1)} %fusion.1), kind=kLoop, calls=%fused_computation.6 | loop fusion | flops 65536 | bytes 524288 | tf_op jit(solution)/shard_map/stack | solution.py:600
  77.4 0.1 rev.7
  77.6 0.1 maximum_bitcast_fusion
  77.7 0.7 copy.13
  78.5 0.7 copy.12
  (3 shorter events, 0.1 us)

commit v20 on v19

--- a/solution.py
+++ b/solution.py
@@ -151,7 +151,7 @@
 
 
 def align_block(spec, lag, slow, source, real_ref, imag_ref, turn_ref):
-    bins, block = spec.shape[1], spec.shape[2]
+    bins, block = spec.shape[0], spec.shape[2]
     first_bin = lax.axis_index("sta") * bins
     bin_rows = (F0 + first_bin + lax.broadcasted_iota(jnp.int32, (bins, block), 0)).astype(jnp.float32)
     cols = pl.ds(pl.multiple_of(source * block, 128), block)
@@ -163,8 +163,8 @@
     turned = left * (TWO_PI / NT)
     cosine = jnp.cos(turned)
     sine = jnp.sin(turned)
-    real_in = spec[0].astype(jnp.float32)
-    imag_in = spec[1].astype(jnp.float32)
+    real_in = spec[:, 0, :].astype(jnp.float32)
+    imag_in = spec[:, 1, :].astype(jnp.float32)
     real_ref[:, cols] = (real_in * cosine + imag_in * sine).astype(jnp.bfloat16).astype(jnp.float32)
     imag_ref[:, cols] = (imag_in * cosine - real_in * sine).astype(jnp.bfloat16).astype(jnp.float32)
     turn_ref[:, cols] = slow.astype(jnp.float32)
@@ -187,7 +187,7 @@
 def beam_kernel(spec_ref, lag_ref, slow_ref, out_ref, spec_in, lag_in, slow_in, local_sem, send_sem, recv_sem,
                 real_ref, imag_ref, turn_ref, acc_ref, left_ref, right_ref, power_ref, pieces, send_rs, recv_rs,
                 send_ag, recv_ag, share_sem):
-    count, bins, block = spec_in.shape[0], spec_in.shape[2], spec_in.shape[3]
+    count, bins, block = spec_in.shape[0], spec_in.shape[1], spec_in.shape[3]
     me = lax.axis_index("sta")
     first_bin = me * bins
     width = CHUNK
@@ -246,7 +246,7 @@
         return carry
 
     def own_block():
-        align_block(spec_ref[me], lag_ref[...], slow_ref[...], me, real_ref, imag_ref, turn_ref)
+        align_block(spec_ref.at[me], lag_ref[...], slow_ref[...], me, real_ref, imag_ref, turn_ref)
         lax.fori_loop(0, per_block, per_chunk, 0)
 
     exchange_inputs(
@@ -255,7 +255,7 @@
 
     def align_other(shift, carry):
         source = lax.rem(me + shift, count)
-        align_block(spec_in[source], lag_in[source], slow_in[source], source, real_ref, imag_ref, turn_ref)
+        align_block(spec_in.at[source], lag_in[source], slow_in[source], source, real_ref, imag_ref, turn_ref)
         return carry
 
     lax.fori_loop(1, count, align_other, 0)
@@ -278,7 +278,7 @@
     count = spec_send.shape[0]
     slots = 2 * reach + 1
     cells = CX * CY
-    bins, block = spec_send.shape[2], spec_send.shape[3]
+    bins, block = spec_send.shape[1], spec_send.shape[3]
     width = CHUNK
     stations = count * block
     vmem = pl.BlockSpec(memory_space=pltpu.VMEM)
@@ -588,7 +588,7 @@
     own_count = FREQS // groups
     first_bin = lax.axis_index("sta") * own_count
     block = spectra.shape[2]
-    spec_send = spectra.reshape(groups, own_count, 2, block).transpose(0, 2, 1, 3)
+    spec_send = spectra.reshape(groups, own_count, 2, block)
     halo_tiles = -(-(ITERS * 2 * HALF) // CX)
     summed = beam_power(spec_send, lag_samples, slowness[0], halo_tiles)
     observed = summed / (FREQS * STATIONS) + BACKGROUND

time: 79.4 us -> 77.5 us (0.976)
  local copies, waits for them, and re-layouts: 4.23 us -> 2.6 us
    reshape x1 -> x0, local copies, waits for them, and re-layouts: 1.62 us -> none  [per_device(): spectra.reshape(groups, own_count, 2, block).transpose(0, 2, 1, 3)]
where the time goes in v20:
time: 77.5 us; the launch traced here: 77.3 us
  Pallas kernels  71.5 us (92%)
  local copies, waits for them, and re-layouts  2.6 us (3%)
  other arithmetic  2.51 us (3%)
    pallas_call x1, Pallas kernels, beam_power(): pl.pallas_call(beam_kernel, out_shape=jax.ShapeDtypeStruct((slots, cells,...  63.6 us
    pallas_call x1, Pallas kernels, deblur_tile(): pl.pallas_call(deblur_kernel, out_shape=jax.ShapeDtypeStruct((planes, CX,...  7.85 us

profile of v20, /device:TPU:1, one launch (start us, length us, event | category | flops | bytes accessed | tf_op | source)
XLA Modules:
  0.0 77.3 jit_solution(18062117910802037068)
XLA Ops:
  0.6 63.6 %shard_map.59 = f32[5,256,128]{2,1,0:T(8,128)} custom-call(bf16[8,8,2,768]{3,2,1,0:T(2,128)(2,1)} %bitcast.12, s32[1,768]{1,0:T(1,128)} %lag_ref.1, bf16[3,768]{1,0:T(4,128)(2,1)} %bitcast.13), custom_call_target="tpu_custom_call" | custom-call | tf_op jit(solution)/shard_map/pallas_call | solution.py:285
  64.3 1.2 %multiply_add_fusion = f32[5,256,128]{2,1,0:T(8,128)S(1)} fusion(f32[5,256,128]{2,1,0:T(8,128)} %shard_map.59), kind=kLoop, calls=%fused_computation.4 | loop fusion | flops 327680 | bytes 1310720 | tf_op jit(solution)/shard_map/add | solution.py:594
  65.5 0.1 fusion.2
  65.6 0.1 fusion
  65.7 0.9 %copy.6 = f32[8,5,32,128]{3,2,1,0:T(8,128)} copy(f32[8,5,32,128]{3,2,0,1:T(8,128)S(1)} %fusion) | data formatting | bytes 1310720 | tf_op jit(solution)/shard_map/transpose | solution.py:598
  66.6 7.8 %shard_map.60 = f32[8,32,128]{2,1,0:T(8,128)} custom-call(f32[3,17]{1,0:T(4,128)} %taps_ref.1, f32[8,160,128]{2,1,0:T(8,128)} %bitcast.10), custom_call_target="tpu_custom_call" | custom-call | tf_op jit(solution)/shard_map/pallas_call | solution.py:574
  74.4 1.1 %slice_maximum_fusion = (f32[2,8,32,64]{3,2,1,0:T(8,128)S(1)}, f32[2,8,32,64]{3,2,1,0:T(8,128)S(1)}) fusion(f32[1,8,32,128]{3,2,1,0:T(8,128)} %bitcast.11, f32[1,8,32,128]{3,2,1,0:T(8,128)S(1)} %fusion.1), kind=kLoop, calls=%fused_computation.6 | loop fusion | flops 65536 | bytes 524288 | tf_op jit(solution)/shard_map/stack | solution.py:600
  75.5 0.1 rev.7
  75.7 0.1 maximum_bitcast_fusion
  75.8 0.7 copy.8
  76.6 0.7 copy.7
  (3 shorter events, 0.1 us)

commit v21 on v20

--- a/solution.py
+++ b/solution.py
@@ -511,7 +511,7 @@
     return jnp.where(index < length // 2, index, 3 * (length // 2) - 1 - index)
 
 
-def deblur_kernel(taps_ref, obs_ref, out_ref, kx_ref, kz_ref):
+def deblur_kernel(taps_ref, obs_ref, out_ref, seen_ref, kx_ref, kz_ref):
     tiles = lax.axis_size("grid")
     me = lax.axis_index("grid")
     planes, width, depth = obs_ref.shape
@@ -565,7 +565,8 @@
         spread = blur(ratio)
         estimate = estimate[2 * HALF : 2 * HALF + spread.shape[0]] * spread
     for y in range(planes):
-        out_ref[y] = estimate[:, y * depth : (y + 1) * depth]
+        out_ref[:, y, :] = estimate[:, y * depth : (y + 1) * depth]
+        seen_ref[:, y, :] = obs_ref[y, halo_tiles * CX : halo_tiles * CX + CX, :]
 
 
 def deblur_tile(observed, spread_taps):
@@ -573,9 +574,9 @@
     vmem = pl.BlockSpec(memory_space=pltpu.VMEM)
     return pl.pallas_call(
         deblur_kernel,
-        out_shape=jax.ShapeDtypeStruct((planes, CX, depth), jnp.float32),
+        out_shape=[jax.ShapeDtypeStruct((CX, planes, depth), jnp.float32)] * 2,
         in_specs=[pl.BlockSpec(memory_space=pltpu.SMEM), vmem],
-        out_specs=vmem,
+        out_specs=[vmem, vmem],
         scratch_shapes=[
             pltpu.VMEM((width - 2 * HALF, width), jnp.float32),
             pltpu.VMEM((depth, depth), jnp.float32),
@@ -596,10 +597,9 @@
     observed = observed.reshape(slots, CY, CX, CZ)
     observed = jnp.concatenate([observed[:, :, : CX // 2], observed[:, :, CX // 2 :][:, :, ::-1]], axis=2)
     planes = observed.transpose(1, 0, 2, 3).reshape(CY, slots * CX, CZ)
-    estimate = deblur_tile(planes, spread_taps)
-    both = jnp.stack([observed[halo_tiles], estimate])
-    both = jnp.concatenate([both[..., : CZ // 2], both[..., CZ // 2 :][..., ::-1]], axis=-1).transpose(0, 2, 1, 3)
-    stacked, estimate = both[0], both[1]
+    estimate, stacked = deblur_tile(planes, spread_taps)
+    estimate = jnp.concatenate([estimate[..., : CZ // 2], estimate[..., CZ // 2 :][..., ::-1]], axis=-1)
+    stacked = jnp.concatenate([stacked[..., : CZ // 2], stacked[..., CZ // 2 :][..., ::-1]], axis=-1)
     return (stacked[None], estimate[None])
 
 

time: 77.5 us -> 77.7 us (level)
  other arithmetic: 2.51 us -> 3.64 us
  local copies, waits for them, and re-layouts: 2.6 us -> 1.52 us
    broadcast_in_dim x0 -> x2, other arithmetic: none -> 1.53 us  [per_device(): return (stacked[None], estimate[None])]
    unnamed x2 -> x1, local copies, waits for them, and re-layouts: 1.47 us -> 0.02 us
    slice x1, local copies, waits for them, and re-layouts: 0.02 us -> 1.22 us  [per_device(): estimate[..., :CZ // 2]]
    another operation x1 -> x0, other arithmetic: 1.1 us -> none  [per_device(): both = jnp.stack([observed[halo_tiles], estimate])]
    concatenate x1, other arithmetic: 0.01 us -> 0.93 us  [per_device(): jnp.concatenate([observed[:, :, :CX // 2], observed[:, :, CX // 2:][:, :,...]
    transpose x1 -> x0, local copies, waits for them, and re-layouts: 0.89 us -> none  [per_device(): planes = observed.transpose(1, 0, 2, 3).reshape(CY, slots * CX, CZ)]
where the time goes in v21:
time: 77.7 us; the launch traced here: 77.4 us
  Pallas kernels  71.6 us (92%)
  other arithmetic  3.64 us (5%)
  local copies, waits for them, and re-layouts  1.52 us (2%)
    pallas_call x1, Pallas kernels, beam_power(): pl.pallas_call(beam_kernel, out_shape=jax.ShapeDtypeStruct((slots, cells,...  63.6 us
    pallas_call x1, Pallas kernels, deblur_tile(): pl.pallas_call(deblur_kernel, out_shape=[jax.ShapeDtypeStruct((CX, planes...  7.96 us

profile of v21, /device:TPU:1, one launch (start us, length us, event | category | flops | bytes accessed | tf_op | source)
XLA Modules:
  0.0 77.4 jit_solution(14078702460946086161)
XLA Ops:
  0.6 63.6 %shard_map.59 = f32[5,256,128]{2,1,0:T(8,128)} custom-call(bf16[8,8,2,768]{3,2,1,0:T(2,128)(2,1)} %bitcast.12, s32[1,768]{1,0:T(1,128)} %lag_ref.1, bf16[3,768]{1,0:T(4,128)(2,1)} %bitcast.13), custom_call_target="tpu_custom_call" | custom-call | tf_op jit(solution)/shard_map/pallas_call | solution.py:285
  64.3 1.2 %multiply_add_fusion = f32[5,256,128]{2,1,0:T(8,128)S(1)} fusion(f32[5,256,128]{2,1,0:T(8,128)} %shard_map.59), kind=kLoop, calls=%fused_computation.1 | loop fusion | flops 327680 | bytes 1310720 | tf_op jit(solution)/shard_map/add | solution.py:595
  65.6 0.9 %pad_maximum_fusion = f32[5,8,32,128]{3,2,0,1:T(8,128)} fusion(f32[5,8,16,128]{3,2,0,1:T(8,128)S(1)} %rev.9, f32[5,8,16,128]{3,2,1,0:T(8,128)S(1)} %get-tuple-element.6), kind=kLoop, calls=%fused_computation | loop fusion | flops 163840 | bytes 1310720 | tf_op jit(solution)/shard_map/concatenate | solution.py:598
  66.5 8.0 %shard_map.60 = (f32[32,8,128]{2,1,0:T(8,128)}, f32[32,8,128]{2,1,0:T(8,128)}) custom-call(f32[3,17]{1,0:T(4,128)} %taps_ref.1, f32[8,160,128]{2,1,0:T(8,128)} %bitcast.10), custom_call_target="tpu_custom_call" | custom-call | tf_op jit(solution)/shard_map/pallas_call | solution.py:575
  74.5 1.2 %fusion.1 = (f32[32,8,64]{2,1,0:T(8,128)S(1)}, f32[32,8,64]{2,1,0:T(8,128)S(1)}, f32[32,8,64]{2,1,0:T(8,128)S(1)}, f32[32,8,64]{2,1,0:T(8,128)S(1)}) fusion(f32[32,8,128]{2,1,0:T(8,128)} %get-tuple-element.5, f32[32,8,128]{2,1,0:T(8,128)} %get-tuple-element.4), kind=kLoop, calls=%fused_computation.5 | loop fusion | bytes 524288 | tf_op jit(solution)/shard_map/slice | solution.py:601
  75.7 0.1 rev.11
  75.8 0.8 maximum_bitcast_fusion.1
  76.6 0.1 rev.10
  76.7 0.8 maximum_bitcast_fusion
  (3 shorter events, 0.1 us)

commit v22 on v21

--- a/solution.py
+++ b/solution.py
@@ -555,7 +555,7 @@
         cell = (me - halo_tiles) * CX + low + lax.broadcasted_iota(jnp.int32, (size, lanes), 0)
         return (cell >= 0) & (cell < tiles * CX)
 
-    observed = jnp.concatenate([obs_ref[y] for y in range(planes)], axis=1)
+    observed = jnp.concatenate([obs_ref[y] for y in range(planes)], axis=1) / (FREQS * STATIONS) + BACKGROUND
     estimate = jnp.where(inside_wide(0, width), observed, 0.0)
     for sweep in range(ITERS):
         low = 2 * HALF * sweep + HALF
@@ -566,7 +566,7 @@
         estimate = estimate[2 * HALF : 2 * HALF + spread.shape[0]] * spread
     for y in range(planes):
         out_ref[:, y, :] = estimate[:, y * depth : (y + 1) * depth]
-        seen_ref[:, y, :] = obs_ref[y, halo_tiles * CX : halo_tiles * CX + CX, :]
+        seen_ref[:, y, :] = observed[halo_tiles * CX : halo_tiles * CX + CX, y * depth : (y + 1) * depth]
 
 
 def deblur_tile(observed, spread_taps):
@@ -592,7 +592,7 @@
     spec_send = spectra.reshape(groups, own_count, 2, block)
     halo_tiles = -(-(ITERS * 2 * HALF) // CX)
     summed = beam_power(spec_send, lag_samples, slowness[0], halo_tiles)
-    observed = summed / (FREQS * STATIONS) + BACKGROUND
+    observed = summed
     slots = observed.shape[0]
     observed = observed.reshape(slots, CY, CX, CZ)
     observed = jnp.concatenate([observed[:, :, : CX // 2], observed[:, :, CX // 2 :][:, :, ::-1]], axis=2)

time: 77.7 us -> 77.6 us (level)
  other arithmetic: 3.64 us -> 2.46 us
  local copies, waits for them, and re-layouts: 1.52 us -> 2.6 us
    add x1 -> x0, other arithmetic: 1.17 us -> none  [per_device(): observed = summed / (FREQS * STATIONS) + BACKGROUND]
    slice x1, local copies, waits for them, and re-layouts: 0.04 us -> 1.13 us  [per_device(): observed[:, :, :CX // 2]]
where the time goes in v22:
time: 77.6 us; the launch traced here: 77.4 us
  Pallas kernels  71.7 us (92%)
  local copies, waits for them, and re-layouts  2.6 us (3%)
  other arithmetic  2.46 us (3%)
    pallas_call x1, Pallas kernels, beam_power(): pl.pallas_call(beam_kernel, out_shape=jax.ShapeDtypeStruct((slots, cells,...  63.6 us
    pallas_call x1, Pallas kernels, deblur_tile(): pl.pallas_call(deblur_kernel, out_shape=[jax.ShapeDtypeStruct((CX, planes...  8.02 us

profile of v22, /device:TPU:1, one launch (start us, length us, event | category | flops | bytes accessed | tf_op | source)
XLA Modules:
  0.0 77.4 jit_solution(11355582490824594066)
XLA Ops:
  0.6 63.6 %shard_map.59 = f32[5,256,128]{2,1,0:T(8,128)} custom-call(bf16[8,8,2,768]{3,2,1,0:T(2,128)(2,1)} %bitcast.12, s32[1,768]{1,0:T(1,128)} %lag_ref.1, bf16[3,768]{1,0:T(4,128)(2,1)} %bitcast.13), custom_call_target="tpu_custom_call" | custom-call | tf_op jit(solution)/shard_map/pallas_call | solution.py:285
  64.3 1.1 %fusion = (f32[5,8,16,128]{3,2,1,0:T(8,128)S(1)}, f32[5,8,16,128]{3,2,1,0:T(8,128)S(1)}) fusion(f32[5,8,32,128]{3,2,1,0:T(8,128)} %bitcast.11), kind=kLoop, calls=%fused_computation.3 | loop fusion | bytes 1310720 | tf_op jit(solution)/shard_map/slice | solution.py:598
  65.5 0.9 %pad_maximum_fusion = f32[5,8,32,128]{3,2,0,1:T(8,128)} fusion(f32[5,8,16,128]{3,2,0,1:T(8,128)S(1)} %rev.9, f32[5,8,16,128]{3,2,1,0:T(8,128)S(1)} %get-tuple-element.6), kind=kLoop, calls=%fused_computation | loop fusion | flops 163840 | bytes 1310720 | tf_op jit(solution)/shard_map/concatenate | solution.py:598
  66.4 8.0 %shard_map.60 = (f32[32,8,128]{2,1,0:T(8,128)}, f32[32,8,128]{2,1,0:T(8,128)}) custom-call(f32[3,17]{1,0:T(4,128)} %taps_ref.1, f32[8,160,128]{2,1,0:T(8,128)} %bitcast.10), custom_call_target="tpu_custom_call" | custom-call | tf_op jit(solution)/shard_map/pallas_call | solution.py:575
  74.4 1.2 %fusion.1 = (f32[32,8,64]{2,1,0:T(8,128)S(1)}, f32[32,8,64]{2,1,0:T(8,128)S(1)}, f32[32,8,64]{2,1,0:T(8,128)S(1)}, f32[32,8,64]{2,1,0:T(8,128)S(1)}) fusion(f32[32,8,128]{2,1,0:T(8,128)} %get-tuple-element.5, f32[32,8,128]{2,1,0:T(8,128)} %get-tuple-element.4), kind=kLoop, calls=%fused_computation.4 | loop fusion | bytes 524288 | tf_op jit(solution)/shard_map/slice | solution.py:601
  75.7 0.1 rev.11
  75.8 0.8 maximum_bitcast_fusion.1
  76.5 0.1 rev.10
  76.6 0.8 maximum_bitcast_fusion
  (2 shorter events, 0.1 us)

commit v23 on v20

--- a/solution.py
+++ b/solution.py
@@ -197,9 +197,8 @@
     rows16 = lax.broadcasted_iota(jnp.int32, (16, width), 0).astype(jnp.float32)
     omega0 = (F0 + first_bin).astype(jnp.float32) * (TWO_PI / NT)
     step = TWO_PI / NT
-    acc_ref[...] = jnp.zeros_like(acc_ref)
-
-    def per_chunk(k, carry):
+
+    def per_chunk(k, carry, first=False):
         source = lax.rem(me + k // per_block, count)
         cols = pl.ds(pl.multiple_of(source * block + lax.rem(k, per_block) * width, 128), width)
         slow_x = turn_ref[0:1, cols]
@@ -237,9 +236,13 @@
                 row = 16 * m
                 right_ref[row : row + 16, :] = z_r.astype(jnp.bfloat16)
                 right_ref[half_z + row : half_z + row + 16, :] = z_i.astype(jnp.bfloat16)
-            acc_ref[f] += lax.dot_general(
+            product = lax.dot_general(
                 left_ref[...], right_ref[...], (((1,), (1,)), ((), ())), preferred_element_type=jnp.float32
             )
+            if first:
+                acc_ref[f] = product
+            else:
+                acc_ref[f] += product
             return tuple(complex_times(now, turn) for now, turn in zip(state, ratio))
 
         lax.fori_loop(0, bins, per_bin, start, unroll=4)
@@ -247,7 +250,8 @@
 
     def own_block():
         align_block(spec_ref.at[me], lag_ref[...], slow_ref[...], me, real_ref, imag_ref, turn_ref)
-        lax.fori_loop(0, per_block, per_chunk, 0)
+        per_chunk(0, 0, first=True)
+        lax.fori_loop(1, per_block, per_chunk, 0)
 
     exchange_inputs(
         spec_ref, lag_ref, slow_ref, spec_in, lag_in, slow_in, local_sem, send_sem, recv_sem, own_block, out_ref.shape[0] // 2

time: 77.5 us -> 77.8 us (level)
  no operation moved by 1% of the time
where the time goes in v23:
time: 77.8 us; the launch traced here: 77.6 us
  Pallas kernels  71.7 us (92%)
  local copies, waits for them, and re-layouts  2.6 us (3%)
  other arithmetic  2.51 us (3%)
    pallas_call x1, Pallas kernels, beam_power(): pl.pallas_call(beam_kernel, out_shape=jax.ShapeDtypeStruct((slots, cells,...  63.9 us
    pallas_call x1, Pallas kernels, deblur_tile(): pl.pallas_call(deblur_kernel, out_shape=jax.ShapeDtypeStruct((planes, CX,...  7.85 us

profile of v23, /device:TPU:1, one launch (start us, length us, event | category | flops | bytes accessed | tf_op | source)
XLA Modules:
  0.0 77.6 jit_solution(15861464143146981557)
XLA Ops:
  0.6 63.9 %shard_map.59 = f32[5,256,128]{2,1,0:T(8,128)} custom-call(bf16[8,8,2,768]{3,2,1,0:T(2,128)(2,1)} %bitcast.12, s32[1,768]{1,0:T(1,128)} %lag_ref.1, bf16[3,768]{1,0:T(4,128)(2,1)} %bitcast.13), custom_call_target="tpu_custom_call" | custom-call | tf_op jit(solution)/shard_map/pallas_call | solution.py:289
  64.5 1.2 %multiply_add_fusion = f32[5,256,128]{2,1,0:T(8,128)S(1)} fusion(f32[5,256,128]{2,1,0:T(8,128)} %shard_map.59), kind=kLoop, calls=%fused_computation.4 | loop fusion | flops 327680 | bytes 1310720 | tf_op jit(solution)/shard_map/add | solution.py:598
  65.7 0.1 fusion.2
  65.8 0.1 fusion
  65.9 0.9 %copy.6 = f32[8,5,32,128]{3,2,1,0:T(8,128)} copy(f32[8,5,32,128]{3,2,0,1:T(8,128)S(1)} %fusion) | data formatting | bytes 1310720 | tf_op jit(solution)/shard_map/transpose | solution.py:602
  66.8 7.8 %shard_map.60 = f32[8,32,128]{2,1,0:T(8,128)} custom-call(f32[3,17]{1,0:T(4,128)} %taps_ref.1, f32[8,160,128]{2,1,0:T(8,128)} %bitcast.10), custom_call_target="tpu_custom_call" | custom-call | tf_op jit(solution)/shard_map/pallas_call | solution.py:578
  74.7 1.1 %slice_maximum_fusion = (f32[2,8,32,64]{3,2,1,0:T(8,128)S(1)}, f32[2,8,32,64]{3,2,1,0:T(8,128)S(1)}) fusion(f32[1,8,32,128]{3,2,1,0:T(8,128)} %bitcast.11, f32[1,8,32,128]{3,2,1,0:T(8,128)S(1)} %fusion.1), kind=kLoop, calls=%fused_computation.6 | loop fusion | flops 65536 | bytes 524288 | tf_op jit(solution)/shard_map/stack | solution.py:604
  75.8 0.1 rev.7
  75.9 0.1 maximum_bitcast_fusion
  76.1 0.7 copy.8
  76.8 0.7 copy.7
  (3 shorter events, 0.1 us)

commit v24 on v20

--- a/solution.py
+++ b/solution.py
@@ -259,7 +259,7 @@
         return carry
 
     lax.fori_loop(1, count, align_other, 0)
-    lax.fori_loop(per_block, count * per_block, per_chunk, 0)
+    lax.fori_loop(per_block, count * per_block, per_chunk, 0, unroll=2)
     cells = CX * CY
     low = jnp.zeros((cells, half_z), jnp.float32)
     high = jnp.zeros((cells, half_z), jnp.float32)

time: 77.5 us -> 77.5 us (level)
  no operation moved by 1% of the time
where the time goes in v24:
time: 77.5 us; the launch traced here: 77.3 us
  Pallas kernels  71.5 us (92%)
  local copies, waits for them, and re-layouts  2.6 us (3%)
  other arithmetic  2.51 us (3%)
    pallas_call x1, Pallas kernels, beam_power(): pl.pallas_call(beam_kernel, out_shape=jax.ShapeDtypeStruct((slots, cells,...  63.6 us
    pallas_call x1, Pallas kernels, deblur_tile(): pl.pallas_call(deblur_kernel, out_shape=jax.ShapeDtypeStruct((planes, CX,...  7.85 us

profile of v24, /device:TPU:1, one launch (start us, length us, event | category | flops | bytes accessed | tf_op | source)
XLA Modules:
  0.0 77.3 jit_solution(16019402893328159046)
XLA Ops:
  0.6 63.6 %shard_map.59 = f32[5,256,128]{2,1,0:T(8,128)} custom-call(bf16[8,8,2,768]{3,2,1,0:T(2,128)(2,1)} %bitcast.12, s32[1,768]{1,0:T(1,128)} %lag_ref.1, bf16[3,768]{1,0:T(4,128)(2,1)} %bitcast.13), custom_call_target="tpu_custom_call" | custom-call | tf_op jit(solution)/shard_map/pallas_call | solution.py:285
  64.3 1.2 %multiply_add_fusion = f32[5,256,128]{2,1,0:T(8,128)S(1)} fusion(f32[5,256,128]{2,1,0:T(8,128)} %shard_map.59), kind=kLoop, calls=%fused_computation.4 | loop fusion | flops 327680 | bytes 1310720 | tf_op jit(solution)/shard_map/add | solution.py:594
  65.4 0.1 fusion.2
  65.6 0.1 fusion
  65.7 0.9 %copy.6 = f32[8,5,32,128]{3,2,1,0:T(8,128)} copy(f32[8,5,32,128]{3,2,0,1:T(8,128)S(1)} %fusion) | data formatting | bytes 1310720 | tf_op jit(solution)/shard_map/transpose | solution.py:598
  66.6 7.8 %shard_map.60 = f32[8,32,128]{2,1,0:T(8,128)} custom-call(f32[3,17]{1,0:T(4,128)} %taps_ref.1, f32[8,160,128]{2,1,0:T(8,128)} %bitcast.10), custom_call_target="tpu_custom_call" | custom-call | tf_op jit(solution)/shard_map/pallas_call | solution.py:574
  74.4 1.1 %slice_maximum_fusion = (f32[2,8,32,64]{3,2,1,0:T(8,128)S(1)}, f32[2,8,32,64]{3,2,1,0:T(8,128)S(1)}) fusion(f32[1,8,32,128]{3,2,1,0:T(8,128)} %bitcast.11, f32[1,8,32,128]{3,2,1,0:T(8,128)S(1)} %fusion.1), kind=kLoop, calls=%fused_computation.6 | loop fusion | flops 65536 | bytes 524288 | tf_op jit(solution)/shard_map/stack | solution.py:600
  75.5 0.1 rev.7
  75.6 0.1 maximum_bitcast_fusion
  75.8 0.7 copy.8
  76.6 0.7 copy.7
  (3 shorter events, 0.1 us)

commit v25 on v20

--- a/solution.py
+++ b/solution.py
@@ -242,7 +242,7 @@
             )
             return tuple(complex_times(now, turn) for now, turn in zip(state, ratio))
 
-        lax.fori_loop(0, bins, per_bin, start, unroll=4)
+        lax.fori_loop(0, bins, per_bin, start, unroll=8)
         return carry
 
     def own_block():

time: 77.5 us -> 74.8 us (0.965)
  Pallas kernels: 71.5 us -> 68.8 us
    pallas_call x1, Pallas kernels: 63.6 us -> 60.9 us  [beam_power(): pl.pallas_call(beam_kernel, out_shape=jax.ShapeDtypeStruct((slots, cells,...]
where the time goes in v25:
time: 74.8 us; the launch traced here: 74.6 us
  Pallas kernels  68.8 us (92%)
  local copies, waits for them, and re-layouts  2.6 us (3%)
  other arithmetic  2.51 us (3%)
    pallas_call x1, Pallas kernels, beam_power(): pl.pallas_call(beam_kernel, out_shape=jax.ShapeDtypeStruct((slots, cells,...  60.9 us
    pallas_call x1, Pallas kernels, deblur_tile(): pl.pallas_call(deblur_kernel, out_shape=jax.ShapeDtypeStruct((planes, CX,...  7.85 us

profile of v25, /device:TPU:1, one launch (start us, length us, event | category | flops | bytes accessed | tf_op | source)
XLA Modules:
  0.0 74.6 jit_solution(17297689235810639138)
XLA Ops:
  0.6 60.9 %shard_map.59 = f32[5,256,128]{2,1,0:T(8,128)} custom-call(bf16[8,8,2,768]{3,2,1,0:T(2,128)(2,1)} %bitcast.12, s32[1,768]{1,0:T(1,128)} %lag_ref.1, bf16[3,768]{1,0:T(4,128)(2,1)} %bitcast.13), custom_call_target="tpu_custom_call" | custom-call | tf_op jit(solution)/shard_map/pallas_call | solution.py:285
  61.6 1.2 %multiply_add_fusion = f32[5,256,128]{2,1,0:T(8,128)S(1)} fusion(f32[5,256,128]{2,1,0:T(8,128)} %shard_map.59), kind=kLoop, calls=%fused_computation.4 | loop fusion | flops 327680 | bytes 1310720 | tf_op jit(solution)/shard_map/add | solution.py:594
  62.7 0.1 fusion.2
  62.9 0.1 fusion
  63.0 0.9 %copy.6 = f32[8,5,32,128]{3,2,1,0:T(8,128)} copy(f32[8,5,32,128]{3,2,0,1:T(8,128)S(1)} %fusion) | data formatting | bytes 1310720 | tf_op jit(solution)/shard_map/transpose | solution.py:598
  63.8 7.8 %shard_map.60 = f32[8,32,128]{2,1,0:T(8,128)} custom-call(f32[3,17]{1,0:T(4,128)} %taps_ref.1, f32[8,160,128]{2,1,0:T(8,128)} %bitcast.10), custom_call_target="tpu_custom_call" | custom-call | tf_op jit(solution)/shard_map/pallas_call | solution.py:574
  71.7 1.1 %slice_maximum_fusion = (f32[2,8,32,64]{3,2,1,0:T(8,128)S(1)}, f32[2,8,32,64]{3,2,1,0:T(8,128)S(1)}) fusion(f32[1,8,32,128]{3,2,1,0:T(8,128)} %bitcast.11, f32[1,8,32,128]{3,2,1,0:T(8,128)S(1)} %fusion.1), kind=kLoop, calls=%fused_computation.6 | loop fusion | flops 65536 | bytes 524288 | tf_op jit(solution)/shard_map/stack | solution.py:600
  72.8 0.1 rev.7
  72.9 0.1 maximum_bitcast_fusion
  73.1 0.7 copy.8
  73.8 0.7 copy.7
  (3 shorter events, 0.1 us)

commit v26 on v23

--- a/solution.py
+++ b/solution.py
@@ -245,7 +245,7 @@
                 acc_ref[f] += product
             return tuple(complex_times(now, turn) for now, turn in zip(state, ratio))
 
-        lax.fori_loop(0, bins, per_bin, start, unroll=4)
+        lax.fori_loop(0, bins, per_bin, start, unroll=8)
         return carry
 
     def own_block():

time: 77.8 us -> 74.6 us (0.959)
  Pallas kernels: 71.7 us -> 68.6 us
    pallas_call x1, Pallas kernels: 63.9 us -> 60.7 us  [beam_power(): pl.pallas_call(beam_kernel, out_shape=jax.ShapeDtypeStruct((slots, cells,...]
where the time goes in v26:
time: 74.6 us; the launch traced here: 74.4 us
  Pallas kernels  68.6 us (92%)
  local copies, waits for them, and re-layouts  2.6 us (3%)
  other arithmetic  2.51 us (3%)
    pallas_call x1, Pallas kernels, beam_power(): pl.pallas_call(beam_kernel, out_shape=jax.ShapeDtypeStruct((slots, cells,...  60.7 us
    pallas_call x1, Pallas kernels, deblur_tile(): pl.pallas_call(deblur_kernel, out_shape=jax.ShapeDtypeStruct((planes, CX,...  7.85 us

profile of v26, /device:TPU:1, one launch (start us, length us, event | category | flops | bytes accessed | tf_op | source)
XLA Modules:
  0.0 74.4 jit_solution(11797438262740547423)
XLA Ops:
  0.6 60.7 %shard_map.59 = f32[5,256,128]{2,1,0:T(8,128)} custom-call(bf16[8,8,2,768]{3,2,1,0:T(2,128)(2,1)} %bitcast.12, s32[1,768]{1,0:T(1,128)} %lag_ref.1, bf16[3,768]{1,0:T(4,128)(2,1)} %bitcast.13), custom_call_target="tpu_custom_call" | custom-call | tf_op jit(solution)/shard_map/pallas_call | solution.py:289
  61.4 1.2 %multiply_add_fusion = f32[5,256,128]{2,1,0:T(8,128)S(1)} fusion(f32[5,256,128]{2,1,0:T(8,128)} %shard_map.59), kind=kLoop, calls=%fused_computation.4 | loop fusion | flops 327680 | bytes 1310720 | tf_op jit(solution)/shard_map/add | solution.py:598
  62.6 0.1 fusion.2
  62.7 0.1 fusion
  62.8 0.9 %copy.6 = f32[8,5,32,128]{3,2,1,0:T(8,128)} copy(f32[8,5,32,128]{3,2,0,1:T(8,128)S(1)} %fusion) | data formatting | bytes 1310720 | tf_op jit(solution)/shard_map/transpose | solution.py:602
  63.7 7.8 %shard_map.60 = f32[8,32,128]{2,1,0:T(8,128)} custom-call(f32[3,17]{1,0:T(4,128)} %taps_ref.1, f32[8,160,128]{2,1,0:T(8,128)} %bitcast.10), custom_call_target="tpu_custom_call" | custom-call | tf_op jit(solution)/shard_map/pallas_call | solution.py:578
  71.5 1.1 %slice_maximum_fusion = (f32[2,8,32,64]{3,2,1,0:T(8,128)S(1)}, f32[2,8,32,64]{3,2,1,0:T(8,128)S(1)}) fusion(f32[1,8,32,128]{3,2,1,0:T(8,128)} %bitcast.11, f32[1,8,32,128]{3,2,1,0:T(8,128)S(1)} %fusion.1), kind=kLoop, calls=%fused_computation.6 | loop fusion | flops 65536 | bytes 524288 | tf_op jit(solution)/shard_map/stack | solution.py:604
  72.6 0.1 rev.7
  72.8 0.1 maximum_bitcast_fusion
  72.9 0.7 copy.8
  73.7 0.7 copy.7
  (3 shorter events, 0.1 us)
